TPU v7x, 256 devices: a whole 4x4x8 slice. The times are simulated.
256 devices in a mesh: lat: 16 (over x, y), lon: 8 (over z), ens: 2 (over core).
Axes of the slice: x: 4, y: 4, z: 8, core: 2. Of those that a mesh axis runs over, the one named last changes fastest.
Arguments:
- parameters: float32 [2, 128, 128, 1024], P(None, 'ens', 'lat', 'lon'), may hold values from -1.2 to 1.2, as said below
- initial_height: float32 [128, 1024], P('lat', 'lon'), may hold values from -6 to 6
- initial_speed: float32 [2, 128, 1024], P(None, 'lat', 'lon'), may hold values from -4 to 4
- obs_slots: int32 [2, 128, 128, 8], P(None, ('lat', 'lon')), may hold values from -1 to 1023, as said below
- obs_values: float32 [2, 128, 128, 8], P(None, ('lat', 'lon')), may hold values from -6 to 6
- obs_precision: float32 [2, 128, 128, 8], P(None, ('lat', 'lon')), may hold values from 0 to 2, as said below
Outputs:
- calibrated: float32 [2, 128, 128, 1024], P(None, 'ens', 'lat', 'lon')
Inputs may be any that keep to these rules, and one draw needn't show every extreme that they name: `obs_slots`: for each iteration and owner, the live slots towards one receiver come first and name distinct cells of the owner's block (local index row * 128 + column); no cell is named twice by one owner in one iteration; in each iteration some receiving block has all 8 slots live from every owner. `obs_precision`: zero exactly where the matching slot of obs_slots (with receiver and owner swapped) is empty, 0.5 or more elsewhere. `parameters`: friction rates lie in 0.02 to 0.2, forcing in -1.2 to 1.2.
All inputs are finite; a program needn't handle non-finite values.
Results may differ from a plain program's by a relative error of at most 0.0003.
Values sent between devices are 32-bit elements; how exact they have to be, the bound alone decides.
No kernel may reach another device: no remote copies, remote signals or barrier semaphores. Data moves between devices by JAX's collectives and lax.ppermute only.
A program may use at most 64 MiB of HBM per device.

v0:
```python
import functools

import jax
import jax.numpy as jnp
from jax import lax
from jax.experimental import pallas as pl
from jax.experimental.pallas import tpu as pltpu
from jax.sharding import Mesh
from jax.sharding import PartitionSpec as P

STEPS = 6
LAT = ("lat_0", "lat_1")
LAT_LON = ("lat_0", "lat_1", "lon")
LON_ENS = ("lon", "ens")

DEPTH = 0.7
GRAVITY = 0.7
CORIOLIS = 0.1

MEMBERS = 128
HALF = 64
ROWS = 8
COLS = 128
EXT = 28
WIDE = 112
LEFT = 24
RIGHT = LEFT + HALF
INIT = 24
GLOBAL_ROWS = 128
OWN = 2 * ROWS * HALF
PIVOTS = 16

F32 = jnp.float32
HIGHEST = lax.Precision.HIGHEST
VMEM = pl.BlockSpec(memory_space=pltpu.VMEM)
SMEM = pl.BlockSpec(memory_space=pltpu.SMEM)


def params():
    return pltpu.CompilerParams(vmem_limit_bytes=24 * 1024 * 1024)


def shape(*dims):
    return jax.ShapeDtypeStruct(dims, F32)


def iota(dims, axis):
    return lax.broadcasted_iota(jnp.int32, dims, axis)


def collect(own_hbm, height_hbm, speed_hbm, values_hbm, precision_hbm,
            out, up2, dn2, obs, values, precision, sems):
    pairs = (
        (values_hbm, values), (precision_hbm, precision), (own_hbm, out.at[:OWN]),
        (height_hbm, out.at[OWN : OWN + ROWS]), (speed_hbm, out.at[OWN + ROWS :]),
    )
    copies = [pltpu.make_async_copy(src, dst, sems.at[k]) for k, (src, dst) in enumerate(pairs)]
    for copy in copies:
        copy.start()
    for copy in copies[:2]:
        copy.wait()
    lines = [values[...], precision[...], jnp.zeros((96, MEMBERS), F32)]
    obs[...] = jnp.concatenate(lines, axis=0).T[:, :32]
    for copy in copies[2:]:
        copy.wait()
    for k, (f, up_row, down_row) in enumerate(((1, 6, 0), (1, 7, 1), (0, 7, 0))):
        start = f * HALF * ROWS
        up2[k * HALF : (k + 1) * HALF] = out[pl.ds(start + up_row, HALF, stride=ROWS), :]
        dn2[k * HALF : (k + 1) * HALF] = out[pl.ds(start + down_row, HALF, stride=ROWS), :]
    up2[3 * HALF :] = out[OWN:]
    dn2[3 * HALF :] = out[OWN:]


def edge_rows():
    rows = []
    for field, first in ((1, 0), (0, 1)):
        for r in range(first, EXT - first):
            away = max(10 - r, r - 17, 0)
            need = 9 + field - away
            rows.append((field, r, 16 if need > 8 else 8))
    return rows


EDGE_ROWS = edge_rows()
EDGE = sum(n for _, _, n in EDGE_ROWS)


def both_cores(first, mine, others, start, stride):
    lines = pl.ds(start, HALF, stride=stride)
    mine, others = mine[lines, :], others[lines, :]
    return jnp.concatenate([jnp.where(first, mine, others), jnp.where(first, others, mine)], axis=0)


def turn_rows(pos, own, m1, p1, m2, p2, own_o, m1_o, p1_o, m2_o, p2_o, FR, FO, tiles, right, left):
    def row_source(field, r):
        if 2 <= r < 26:
            which = (r - 2) // ROWS
            return (m1, own, p1)[which], (m1_o, own_o, p1_o)[which], field * HALF * ROWS + (r - 2) % ROWS, ROWS
        k = 2 if field == 0 else (r if r < 2 else r - 26)
        refs = (m2, m2_o) if r < 2 else (p2, p2_o)
        return *refs, k * HALF, 1

    first = pos[1] == 0
    at = 0
    for field, r, n in EDGE_ROWS:
        mine, others, start, stride = row_source(field, r)
        turned = both_cores(first, mine, others, start, stride).T
        turned = jnp.where(first, turned[:HALF], turned[HALF:])
        if field == 1 and not 10 <= r < 18:
            turned = jnp.where(inside(pos[0], r), turned, 0.0)
        (FO if field else FR)[r, LEFT:RIGHT] = turned
        right[at : at + n] = turned[HALF - n :]
        left[at : at + n] = turned[:n]
        at += n

    fields = ((m2, 3 * HALF), (m1, OWN), (own, OWN), (p1, OWN), (p2, 3 * HALF))
    for k, (ref, start) in enumerate(fields):
        tile = ref[start : start + INIT]
        for out, at in ((tiles, 0), (right, EDGE), (left, EDGE)):
            out[at + k * INIT : at + (k + 1) * INIT] = tile


def scatter_obs(pos, slots, received, weights, observed):
    received = jnp.concatenate([received[...], jnp.zeros((MEMBERS, 96), F32)], axis=1).T
    values, precision = received[:16], received[16:32]
    lines = ROWS * HALF
    k = iota((lines, MEMBERS), 0)
    cell = (k // HALF) * COLS + pos[1] * HALF + k % HALF
    for t in range(2):
        found_w = jnp.zeros((lines, MEMBERS), F32)
        found_y = jnp.zeros((lines, MEMBERS), F32)
        for s in range(8):
            at = t * 8 + s
            hit = cell == slots[at : at + 1, :]
            found_w = found_w + jnp.where(hit, precision[at : at + 1, :], 0.0)
            found_y = found_y + jnp.where(hit, values[at : at + 1, :], 0.0)
        weights[t] = jnp.broadcast_to(jnp.sum(found_w, axis=1, keepdims=True), (lines, MEMBERS))
        observed[t] = jnp.broadcast_to(jnp.sum(found_y, axis=1, keepdims=True), (lines, MEMBERS))


def inside(lat, r):
    row = lat * ROWS + r - 10
    return jnp.logical_and(row >= 0, row < GLOBAL_ROWS)


def initial_table(pos, tiles, lz, rz):
    lane = iota((ROWS, COLS), 1)
    row = iota((ROWS, COLS), 0)
    e = pos[1]
    fields = [[], [], []]
    for k in range(5):
        for f in range(3):
            at = k * INIT + f * ROWS
            own = tiles[at : at + ROWS]
            at += EDGE
            before = lz[at : at + ROWS]
            after = rz[at : at + ROWS]
            low = pltpu.roll(jnp.where(lane >= 112, before, own), 16, 1)
            high = pltpu.roll(jnp.where(lane < 16, after, own), 80, 1)
            window = jnp.where(e == 0, low, high)
            place = pos[0] * ROWS + (k - 2) * ROWS + row
            ok = jnp.logical_and(place >= 0, place < GLOBAL_ROWS)
            fields[f].append(jnp.where(ok, window, 0.0))
    h, u, v = (jnp.concatenate(f, axis=0) for f in fields)
    east = pltpu.roll(u, COLS - 1, 1) - pltpu.roll(u, 1, 1)
    north = jnp.concatenate([v[1:], v[:1]], axis=0) - jnp.concatenate([v[-1:], v[:-1]], axis=0)
    place = pos[0] * ROWS - 16 + iota((40, COLS), 0)
    ok = jnp.logical_and(place >= 0, place < GLOBAL_ROWS)
    base = jnp.where(ok, h - DEPTH * (east + north), 0.0)
    return jnp.concatenate([base, u, v, jnp.zeros((8, COLS), F32)], axis=0).T


def forward(lat, table, FR, FO, H, U, V):
    first = table[0:96]

    def start(f, r):
        lane = f * 40 + r + 6
        return jnp.broadcast_to(first[:, lane : lane + 1], (96, MEMBERS))

    def gains(r):
        ok = inside(lat, r)
        return jnp.where(ok, F32(GRAVITY), F32(0.0)), jnp.where(ok, F32(CORIOLIS), F32(0.0))

    for r in range(EXT):
        H[r, 8:104] = start(0, r) + FO[r, 8:104]
    for r in range(1, EXT - 1):
        g, c = gains(r)
        u, v = start(1, r), start(2, r)
        keep = 1.0 - FR[r, 8:104]
        U[r, 8:104] = keep * u - g * (H[r, 9:105] - H[r, 7:103]) + c * v
        V[r, 8:104] = keep * v - g * (H[r + 1, 8:104] - H[r - 1, 8:104]) - c * u

    def height_row(a, b, r):
        g, _ = gains(r)
        n = b - a
        east = U[r, pl.ds(a + 1, n)] - U[r, pl.ds(a - 1, n)]
        north = V[r + 1, pl.ds(a, n)] - V[r - 1, pl.ds(a, n)]
        H[r, pl.ds(a, n)] = H[r, pl.ds(a, n)] - g * (east + north) + FO[r, pl.ds(a, n)]

    def speed_row(a, b, r):
        g, c = gains(r)
        n = b - a
        u, v = U[r, pl.ds(a, n)], V[r, pl.ds(a, n)]
        keep = 1.0 - FR[r, pl.ds(a, n)]
        east = H[r, pl.ds(a + 1, n)] - H[r, pl.ds(a - 1, n)]
        north = H[r + 1, pl.ds(a, n)] - H[r - 1, pl.ds(a, n)]
        U[r, pl.ds(a, n)] = keep * u - g * east + c * v
        V[r, pl.ds(a, n)] = keep * v - g * north - c * u

    def sweep(row, reach, a, b):
        def body(i, carry):
            row(a, b, 10 - reach + 2 * i)
            row(a, b, 11 - reach + 2 * i)
            return carry

        lax.fori_loop(0, (ROWS + 2 * reach) // 2, body, 0)

    for step in range(1, STEPS):
        reach = 2 * (STEPS - 1 - step)
        a, b = (16, 96) if reach else (LEFT, RIGHT)
        sweep(height_row, reach, a, b)
        if reach:
            sweep(speed_row, reach - 1, a, b)


def gram(pos, H, weights, observed, keep, send):
    lines = ROWS * HALF
    h = H[10:18, LEFT:RIGHT].reshape(lines, MEMBERS)
    centre = jnp.mean(h, axis=1, keepdims=True)
    spread = h - centre
    weighted = spread * weights
    g = lax.dot_general(spread, weighted, (((0,), (0,)), ((), ())), precision=HIGHEST, preferred_element_type=F32)
    d = jnp.sum(weighted * (observed - centre), axis=0, keepdims=True)
    row, lane = iota((HALF, MEMBERS), 0), iota((HALF, MEMBERS), 1)
    top, bottom = g[:HALF], g[HALF:]
    packed = jnp.where(jnp.logical_and(lane < HALF, lane > row), pltpu.roll(bottom, HALF, 1), top)
    diagonal = jnp.sum(jnp.where(lane == row + HALF, bottom, 0.0), axis=0, keepdims=True)
    line = iota((8, MEMBERS), 0)
    rest = jnp.where(line == 0, d, jnp.where(line == 1, diagonal, 0.0))
    one = jnp.concatenate([packed[:32], rest], axis=0)
    two = jnp.concatenate([packed[32:], jnp.zeros((8, MEMBERS), F32)], axis=0)
    keep[...] = jnp.where(pos[1] == 0, one, two)
    send[...] = jnp.where(pos[1] == 0, two, one)


def first_run(pos, fr, fo, tiles, lz, rz, weights, observed, FR, FO, table, keep, send, H, U, V):
    del fr, fo
    at = 0
    for field, r, n in EDGE_ROWS:
        out = FO if field else FR
        out[r, LEFT - n : LEFT] = lz[at : at + n]
        out[r, RIGHT : RIGHT + n] = rz[at : at + n]
        at += n
    table[...] = initial_table(pos, tiles, lz, rz)
    forward(pos[0], table[...], FR, FO, H, U, V)
    gram(pos, H, weights[0], observed[0], keep, send)


def inverse(x):
    n = PIVOTS
    panels = [x[k : k + n] for k in range(0, MEMBERS, n)]
    row, lane = iota((n, MEMBERS), 0), iota((n, MEMBERS), 1)
    lower, scaled = [], []

    def spread(panel, column):
        return jnp.broadcast_to(panel[:, column : column + 1], (n, MEMBERS))

    for k in range(len(panels)):
        first = k * n
        block = jnp.logical_and(lane >= first, lane < first + n)
        columns = [spread(panels[k], first + j) for j in range(n)]
        top = jnp.where(block, jnp.where(lane - first == row, 1.0, 0.0), panels[k])
        lower.append(jnp.where(lane < first + n, top, 0.0))
        for j in range(n):
            over = 1.0 / columns[j][j : j + 1]

            def eliminate(m, j=j, over=over):
                pivot = m[j : j + 1] * over
                return jnp.where(row == j, pivot, m - columns[j] * pivot)

            top = eliminate(top)
            columns[j + 1 :] = [eliminate(m) for m in columns[j + 1 :]]
        scaled.append(jnp.where(lane < first + n, top, 0.0))
        for i in range(k + 1, len(panels)):
            terms = [spread(panels[i], first + j) * top[j : j + 1] for j in range(n)]
            while len(terms) > 1:
                terms = [a + b for a, b in zip(terms[::2], terms[1::2])]
            panels[i] = jnp.where(block, 0.0, panels[i]) - terms[0]
    lower, scaled = jnp.concatenate(lower, axis=0), jnp.concatenate(scaled, axis=0)
    return lax.dot_general(lower, scaled, (((0,), (0,)), ((), ())), precision=HIGHEST, preferred_element_type=F32)


def weights_of(pos, mine, other):
    one = jnp.where(pos[1] == 0, mine, other)
    two = jnp.where(pos[1] == 0, other, mine)
    packed = jnp.concatenate([one[:32], two[:32]], axis=0)
    d, diagonal = one[32:33], one[33:34]
    turned = jnp.concatenate([packed, jnp.zeros((HALF, MEMBERS), F32)], axis=0).T
    row, lane = iota((HALF, MEMBERS), 0), iota((HALF, MEMBERS), 1)
    a = jnp.where(lane <= row, packed, turned[:HALF])
    c = pltpu.roll(jnp.where(lane > row, packed, turned[:HALF]), HALF, 1)
    c = jnp.where(lane == row + HALF, diagonal, c)
    top = jnp.where(lane < HALF, a, packed)
    bottom = jnp.where(lane < HALF, turned[HALF:], c)
    g = jnp.concatenate([top, bottom], axis=0)
    row, lane = iota((MEMBERS, MEMBERS), 0), iota((MEMBERS, MEMBERS), 1)
    x = g * (1.0 / MEMBERS) + jnp.where(row == lane, 1.0, 0.0)
    x = inverse(x)
    shift = jnp.sum(x * d, axis=1, keepdims=True) * (1.0 / MEMBERS)
    z = x + shift
    return z - jnp.mean(z, axis=0, keepdims=True) + 1.0 / MEMBERS


def second_run(pos, mine, other, fr, fo, table, weights, observed, k1, keep, send, FR, FO, H, U, V):
    k = weights_of(pos, mine[...], other[...])
    k1[...] = k
    for src, out in ((fr, FR), (fo, FO)):
        new = jnp.dot(src[...].reshape(EXT * WIDE, MEMBERS), k, precision=HIGHEST, preferred_element_type=F32)
        out[...] = new.reshape(EXT, WIDE, MEMBERS)
    forward(pos[0], table[...], FR, FO, H, U, V)
    gram(pos, H, weights[1], observed[1], keep, send)


def last_update(pos, mine, other, k1, own_p, other_p, out):
    k = jnp.dot(k1[...], weights_of(pos, mine[...], other[...]), precision=HIGHEST, preferred_element_type=F32)

    first = pos[1] == 0
    kt = k.T
    kt = jnp.where(first, kt[:HALF], kt[HALF:])
    for start in [f * HALF * ROWS + r for f in range(2) for r in range(ROWS)]:
        block = both_cores(first, own_p, other_p, start, ROWS)
        out[pl.ds(start, HALF, stride=ROWS), :] = jnp.dot(kt, block, precision=HIGHEST, preferred_element_type=F32)


def swap(value):
    return lax.ppermute(value, "ens", [(0, 1), (1, 0)])


def moved(value, axes, by):
    n = lax.axis_size(axes)
    return lax.ppermute(value, axes, [(i, (i + by) % n) for i in range(n)])


def copied_sum(*refs):
    *parts, out = refs
    terms = [ref[k] for ref in parts for k in range(ref.shape[0])]
    total = terms[0]
    for term in terms[1:]:
        total = total + term
    for k in range(out.shape[0]):
        out[k] = total


def summed(copies, *parts):
    return pl.pallas_call(
        copied_sum,
        out_shape=shape(copies, *parts[0].shape[1:]),
        in_specs=[VMEM] * len(parts),
        out_specs=VMEM,
        compiler_params=pltpu.CompilerParams(vmem_limit_bytes=4 * 1024 * 1024),
    )(*parts)


def reduced(keep, send):
    parts = keep[None], swap(send)[None]
    for axes in (LAT, "lon"):
        parts = [lax.all_to_all(summed(lax.axis_size(axes), *parts), axes, 0, 0, tiled=True)]
    value = summed(1, *parts)[0]
    return value, swap(value)


def call(kernel, out_shape, scalars, *args, scratch=(), aliases=None):
    return pl.pallas_call(
        kernel,
        out_shape=out_shape,
        in_specs=[SMEM] + [VMEM] * len(args),
        out_specs=jax.tree.map(lambda _: VMEM, out_shape),
        scratch_shapes=list(scratch),
        input_output_aliases=aliases or {},
        compiler_params=params(),
    )(scalars, *args)


def per_device(parameters, initial_height, initial_speed, obs_slots, obs_values, obs_precision):
    pos = jnp.stack([lax.axis_index(LAT), lax.axis_index("ens")]).astype(jnp.int32)
    own_p = parameters.reshape(2 * HALF * ROWS, COLS)
    slots, values, precision = (
        x[:, 0].transpose(0, 2, 1).reshape(16, 128) for x in (obs_slots, obs_values, obs_precision)
    )
    two_far = shape(3 * HALF + INIT, COLS)
    own, up2, dn2, obs = pl.pallas_call(
        collect,
        out_shape=[shape(OWN + INIT, COLS), two_far, two_far, shape(128, 32)],
        in_specs=[pl.BlockSpec(memory_space=pl.ANY)] * 5,
        out_specs=[VMEM] * 4,
        scratch_shapes=[pltpu.VMEM((16, COLS), F32)] * 2 + [pltpu.SemaphoreType.DMA((5,))],
    )(own_p, initial_height, initial_speed.reshape(16, COLS), values, precision)
    near = [moved(own, LAT, 1), moved(own, LAT, -1)]
    far = [moved(up2, LAT, 2), moved(dn2, LAT, -2)]
    own_other = swap(own)
    obs = lax.all_to_all(obs, LAT_LON, 0, 0, tiled=True)
    *halo, obs = lax.optimization_barrier((*near, *far, obs))
    blocks = [own, *halo]
    others = [own_other] + [swap(x) for x in halo]
    weights, observed = call(scatter_obs, [shape(2, 512, 128), shape(2, 512, 128)], pos, slots, obs)

    field = shape(EXT, WIDE, MEMBERS)
    half = shape(40, MEMBERS)
    square = shape(MEMBERS, MEMBERS)
    edge = shape(EDGE + 5 * INIT, MEMBERS)
    ext_fr, ext_fo, tiles, right, left = call(
        turn_rows, [field, field, shape(5 * INIT, COLS), edge, edge], pos, *blocks, *others
    )
    lz, rz = moved(right, LON_ENS, 1), moved(left, LON_ENS, -1)
    state = [pltpu.VMEM((EXT, WIDE, MEMBERS), F32)]
    ext_fr, ext_fo, table, keep, send = call(
        first_run, [field, field, square, half, half],
        pos, ext_fr, ext_fo, tiles, lz, rz, weights, observed,
        scratch=state * 3, aliases={1: 0, 2: 1},
    )
    mine, other = reduced(keep, send)
    k1, keep, send = call(
        second_run, [square, half, half],
        pos, mine, other, ext_fr, ext_fo, table, weights, observed,
        scratch=state * 5,
    )
    mine, other = reduced(keep, send)
    out = call(last_update, shape(2 * HALF * ROWS, COLS), pos, mine, other, k1, own_p, others[0])
    return out.reshape(parameters.shape)


def solution(mesh):
    torus = Mesh(
        mesh.devices.reshape(4, 4, mesh.shape["lon"], mesh.shape["ens"]),
        ("lat_0", "lat_1", "lon", "ens"),
    )
    in_specs = (
        P(None, "ens", LAT, "lon"),
        P(LAT, "lon"),
        P(None, LAT, "lon"),
        P(None, LAT_LON, None, None),
        P(None, LAT_LON, None, None),
        P(None, LAT_LON, None, None),
    )
    out_specs = P(None, "ens", LAT, "lon")
    return jax.shard_map(
        per_device, mesh=torus, in_specs=in_specs, out_specs=out_specs, check_vma=False
    )
```

profile of v0, /device:TPU:1, one launch (start us, length us, event | category | flops | bytes accessed | tf_op | source)
XLA Modules:
  0.0 131.8 jit_solution(6553294952773526353)
XLA Ops:
  0.0 2.0 %shard_map.64 = (f32[1048,128]{1,0:T(8,128)}, f32[216,128]{1,0:T(8,128)}, f32[216,128]{1,0:T(8,128)}, f32[128,32]{1,0:T(8,128)}) custom-call(f32[1024,128]{1,0:T(8,128)} %bitcast.30, f32[8,128]{1,0:T(8,128)} %height_hbm.1, f32[16,128]{1,0:T(8,128)} %bitcast.43, f32[16,128]{1,0:T(8,128)} %bitcast.44, f32[16,128]{1,0:T(8,128)} %bitcast.45), custom_call_target="tpu_custom_call" | custom-call | tf_op jit(solution)/shard_map/pallas_call | solution.py:391
  2.0 5.8 %collective-permute-start.1 = (f32[1048,128]{1,0:T(8,128)}, f32[1048,128]{1,0:T(8,128)S(1)}, u32[]{:S(2)}, u32[]{:S(2)}) collective-permute-start(f32[1048,128]{1,0:T(8,128)} %get-tuple-element.29.own), channel_id=1, source_target_pairs={{0,240},{16,0},{32,16},{48,32},{64,48},{80,64},{96,80},{112,96},{1... | collective-permute-start | bytes 1609736 | tf_op jit(solution)/shard_map/ppermute | solution.py:341
  7.9 5.1 %collective-permute-start.3 = (f32[216,128]{1,0:T(8,128)}, f32[216,128]{1,0:T(8,128)S(1)}, u32[]{:S(2)}, u32[]{:S(2)}) collective-permute-start(f32[216,128]{1,0:T(8,128)} %get-tuple-element.31), channel_id=1, source_target_pairs={{0,224},{16,240},{32,0},{48,16},{64,32},{80,48},{96,64},{112,80},{... | collective-permute-start | bytes 331784 | tf_op jit(solution)/shard_map/ppermute | solution.py:341
  12.9 12.8 %all-to-all-start = ((f32[128,1,32]{2,1,0:T(1,128)}), f32[128,1,32]{2,1,0:T(1,128)S(1)}, u32[]{:S(2)}, u32[]{:S(2)}) async-start(f32[128,1,32]{2,1,0:T(1,128)} %bitcast.42), calls=%async_computation | async-start | bytes 131072 | tf_op jit(solution)/shard_map/all_to_all | solution.py:401
  25.8 2.2 %collective-permute-start.4 = (f32[1048,128]{1,0:T(8,128)}, f32[1048,128]{1,0:T(8,128)S(1)}, u32[]{:S(2)}, u32[]{:S(2)}) collective-permute-start(f32[1048,128]{1,0:T(8,128)} %get-tuple-element.29.own), channel_id=1, source_target_pairs={{0,1},{1,0},{2,3},{3,2},{4,5},{5,4},{6,7},{7,6},{8,9},{9,8},{10,11... | collective-permute-start | bytes 1609736 | tf_op jit(solution)/shard_map/ppermute | solution.py:336
  27.9 8.4 %all-to-all-done = f32[128,1,32]{2,1,0:T(1,128)S(1)} async-done(((f32[128,1,32]{2,1,0:T(1,128)}), f32[128,1,32]{2,1,0:T(1,128)S(1)}, u32[]{:S(2)}, u32[]{:S(2)}) %all-to-all-start) | async-done | bytes 16416 | tf_op jit(solution)/shard_map/all_to_all | solution.py:401
  36.3 3.3 %collective-permute-start.5 = (f32[1048,128]{1,0:T(8,128)S(1)}, f32[1048,128]{1,0:T(8,128)S(1)}, u32[]{:S(2)}, u32[]{:S(2)}) collective-permute-start(f32[1048,128]{1,0:T(8,128)S(1)} %collective-permute-done.m1), channel_id=1, source_target_pairs={{0,1},{1,0},{2,3},{3,2},{4,5},{5,4},{6,7},{7,6},{8,9},{9,8},{10,11... | collective-permute-start | bytes 1609736 | tf_op jit(solution)/shard_map/ppermute | solution.py:336
  40.3 1.8 %collective-permute-done.7.m2_o = f32[216,128]{1,0:T(8,128)S(1)} collective-permute-done((f32[216,128]{1,0:T(8,128)S(1)}, f32[216,128]{1,0:T(8,128)S(1)}, u32[]{:S(2)}, u32[]{:S(2)}) %collective-permute-start.7) | collective-permute-done | bytes 110624 | tf_op jit(solution)/shard_map/ppermute | solution.py:336
  42.3 1.0 copy-done.1
  43.3 1.5 %shard_map.65 = (f32[28,112,128]{2,1,0:T(8,128)S(1)}, f32[28,112,128]{2,1,0:T(8,128)S(1)}, f32[120,128]{1,0:T(8,128)S(1)}, f32[696,128]{1,0:T(8,128)S(1)}, f32[696,128]{1,0:T(8,128)S(1)}) custom-call(s32[2]{0:T(128)S(1)} %pad_add_fusion.pos, f32[1048,128]{1,0:T(8,128)S(1)} %copy-done.1, f32[1048,128]{1,0:T(8,128)S(1)} %collective-permute-done.m1, ...), custom_call_target="tpu_custom_call" | custom-call | tf_op jit(solution)/shard_map/pallas_call | solution.py:373
  45.4 1.5 %shard_map.66 = (f32[2,512,128]{2,1,0:T(8,128)S(1)}, f32[2,512,128]{2,1,0:T(8,128)S(1)}) custom-call(s32[2]{0:T(128)S(1)} %pad_add_fusion.pos, s32[16,128]{1,0:T(8,128)S(1)} %bitcast.41, f32[128,32]{1,0:T(8,128)S(1)} %bitcast.32), custom_call_target="tpu_custom_call" | custom-call | tf_op jit(solution)/shard_map/pallas_call | solution.py:373
  46.8 2.9 %collective-permute-done.9.lz = f32[696,128]{1,0:T(8,128)S(1)} collective-permute-done((f32[696,128]{1,0:T(8,128)S(1)}, f32[696,128]{1,0:T(8,128)S(1)}, u32[]{:S(2)}, u32[]{:S(2)}) %collective-permute-start.9) | collective-permute-done | bytes 356384 | tf_op jit(solution)/shard_map/ppermute | solution.py:341
  49.7 2.8 %collective-permute-done.10.rz = f32[696,128]{1,0:T(8,128)S(1)} collective-permute-done((f32[696,128]{1,0:T(8,128)S(1)}, f32[696,128]{1,0:T(8,128)S(1)}, u32[]{:S(2)}, u32[]{:S(2)}) %collective-permute-start.10) | collective-permute-done | bytes 356384 | tf_op jit(solution)/shard_map/ppermute | solution.py:341
  52.5 5.2 %shard_map.67 = (f32[28,112,128]{2,1,0:T(8,128)S(1)}, f32[28,112,128]{2,1,0:T(8,128)S(1)}, f32[128,128]{1,0:T(8,128)S(1)}, f32[40,128]{1,0:T(8,128)S(1)}, f32[40,128]{1,0:T(8,128)S(1)}) custom-call(s32[2]{0:T(128)S(1)} %pad_add_fusion.pos, f32[28,112,128]{2,1,0:T(8,128)S(1)} %get-tuple-element.37.fr, ...), custom_call_target="tpu_custom_call", output_to_operand_aliasing={{0}: (1, {}), {1}: (2, {})} | custom-call | tf_op jit(solution)/shard_map/pallas_call | solution.py:373
  57.7 1.1 collective-permute-start.11
  59.6 10.6 %all_to_all.32.refs_0_ = f32[16,40,128]{2,1,0:T(8,128)S(1)} all-to-all(f32[16,40,128]{2,1,0:T(8,128)S(1)} %shard_map.68), channel_id=1, replica_groups=mesh['lat_0'=4,'lat_1'=4,'lon'=8,'ens'=2] {'lat_0','lat_1'}, dimensions={0} | all-to-all | bytes 655360 | tf_op jit(solution)/shard_map/all_to_all | solution.py:367
  70.2 12.6 %all_to_all.33.refs_0_ = f32[8,40,128]{2,1,0:T(8,128)S(1)} all-to-all(f32[8,40,128]{2,1,0:T(8,128)S(1)} %shard_map.69), channel_id=1, replica_groups=mesh['lat_0'=4,'lat_1'=4,'lon'=8,'ens'=2] {'lon'}, dimensions={0} | all-to-all | bytes 327680 | tf_op jit(solution)/shard_map/all_to_all | solution.py:367
  82.8 3.4 %collective-permute-start.12 = (f32[40,128]{1,0:T(8,128)S(1)}, f32[40,128]{1,0:T(8,128)S(1)}, u32[]{:S(2)}, u32[]{:S(2)}) collective-permute-start(f32[40,128]{1,0:T(8,128)S(1)} %bitcast.33), channel_id=1, source_target_pairs={{0,1},{1,0},{2,3},{3,2},{4,5},{5,4},{6,7},{7,6},{8,9},{9,8},{10,11... | collective-permute-start | bytes 61448 | tf_op jit(solution)/shard_map/ppermute | solution.py:336
  86.2 0.8 collective-permute-done.12.other
  87.0 10.8 %shard_map.71 = (f32[128,128]{1,0:T(8,128)S(1)}, f32[40,128]{1,0:T(8,128)S(1)}, f32[40,128]{1,0:T(8,128)S(1)}) custom-call(s32[2]{0:T(128)S(1)} %pad_add_fusion.pos, f32[40,128]{1,0:T(8,128)S(1)} %bitcast.34, f32[40,128]{1,0:T(8,128)S(1)} %collective-permute-done.12.other, f32[28,112,128]{2,1,0:T(8,128)S(1)} %get-tuple-element.47.fr, ...), custom_call_target="tpu_custom_call" | custom-call | tf_op jit(solution)/shard_map/pallas_call | solution.py:373
  99.2 11.2 %all_to_all.34.refs_0_ = f32[16,40,128]{2,1,0:T(8,128)S(1)} all-to-all(f32[16,40,128]{2,1,0:T(8,128)S(1)} %shard_map.72), channel_id=1, replica_groups=mesh['lat_0'=4,'lat_1'=4,'lon'=8,'ens'=2] {'lat_0','lat_1'}, dimensions={0} | all-to-all | bytes 655360 | tf_op jit(solution)/shard_map/all_to_all | solution.py:367
  110.4 10.8 %all_to_all.35.refs_0_ = f32[8,40,128]{2,1,0:T(8,128)S(1)} all-to-all(f32[8,40,128]{2,1,0:T(8,128)S(1)} %shard_map.73), channel_id=1, replica_groups=mesh['lat_0'=4,'lat_1'=4,'lon'=8,'ens'=2] {'lon'}, dimensions={0} | all-to-all | bytes 327680 | tf_op jit(solution)/shard_map/all_to_all | solution.py:367
  121.1 3.5 %collective-permute-start.14 = (f32[40,128]{1,0:T(8,128)S(1)}, f32[40,128]{1,0:T(8,128)S(1)}, u32[]{:S(2)}, u32[]{:S(2)}) collective-permute-start(f32[40,128]{1,0:T(8,128)S(1)} %bitcast.35), channel_id=1, source_target_pairs={{0,1},{1,0},{2,3},{3,2},{4,5},{5,4},{6,7},{7,6},{8,9},{9,8},{10,11... | collective-permute-start | bytes 61448 | tf_op jit(solution)/shard_map/ppermute | solution.py:336
  125.5 6.2 %shard_map.75 = f32[1024,128]{1,0:T(8,128)} custom-call(s32[2]{0:T(128)S(1)} %pad_add_fusion.pos, f32[40,128]{1,0:T(8,128)S(1)} %bitcast.36, f32[40,128]{1,0:T(8,128)S(1)} %collective-permute-done.14.other, f32[128,128]{1,0:T(8,128)S(1)} %get-tuple-element.52.k1, f32[1024,128]{1,0:T(8,128)S(1)} %bitcast.31, f32[1048,128]{1,0:T(8,128)S(1)} %collective-permute-done.4.own_o.other_p), custom_call_target="tpu_custom_call" | custom-call | tf_op jit(solution)/shard_map/pallas_call | solution.py:373
  (31 shorter events, 4.5 us)
Async XLA Ops:
  2.0 34.3 %collective-permute-start.1 = (f32[1048,128]{1,0:T(8,128)}, f32[1048,128]{1,0:T(8,128)S(1)}, u32[]{:S(2)}, u32[]{:S(2)}) collective-permute-start(f32[1048,128]{1,0:T(8,128)} %get-tuple-element.29.own), channel_id=1, source_target_pairs={{0,240},{16,0},{32,16},{48,32},{64,48},{80,64},{96,80},{112,96},{1... | collective-permute-start | bytes 1609736 | tf_op jit(solution)/shard_map/ppermute | solution.py:341
  7.9 28.5 %collective-permute-start = (f32[1048,128]{1,0:T(8,128)}, f32[1048,128]{1,0:T(8,128)S(1)}, u32[]{:S(2)}, u32[]{:S(2)}) collective-permute-start(f32[1048,128]{1,0:T(8,128)} %get-tuple-element.29.own), channel_id=1, source_target_pairs={{0,16},{16,32},{32,48},{48,64},{64,80},{80,96},{96,112},{112,128},... | collective-permute-start | bytes 1609736 | tf_op jit(solution)/shard_map/ppermute | solution.py:341
  7.9 28.4 %collective-permute-start.2 = (f32[216,128]{1,0:T(8,128)}, f32[216,128]{1,0:T(8,128)S(1)}, u32[]{:S(2)}, u32[]{:S(2)}) collective-permute-start(f32[216,128]{1,0:T(8,128)} %get-tuple-element.30), channel_id=1, source_target_pairs={{0,32},{16,48},{32,64},{48,80},{64,96},{80,112},{96,128},{112,144}... | collective-permute-start | bytes 331784 | tf_op jit(solution)/shard_map/ppermute | solution.py:341
  7.9 28.4 %collective-permute-start.3 = (f32[216,128]{1,0:T(8,128)}, f32[216,128]{1,0:T(8,128)S(1)}, u32[]{:S(2)}, u32[]{:S(2)}) collective-permute-start(f32[216,128]{1,0:T(8,128)} %get-tuple-element.31), channel_id=1, source_target_pairs={{0,224},{16,240},{32,0},{48,16},{64,32},{80,48},{96,64},{112,80},{... | collective-permute-start | bytes 331784 | tf_op jit(solution)/shard_map/ppermute | solution.py:341
  12.9 23.4 %all-to-all-start = ((f32[128,1,32]{2,1,0:T(1,128)}), f32[128,1,32]{2,1,0:T(1,128)S(1)}, u32[]{:S(2)}, u32[]{:S(2)}) async-start(f32[128,1,32]{2,1,0:T(1,128)} %bitcast.42), calls=%async_computation | async-start | bytes 131072 | tf_op jit(solution)/shard_map/all_to_all | solution.py:401
  25.8 14.6 %collective-permute-start.4 = (f32[1048,128]{1,0:T(8,128)}, f32[1048,128]{1,0:T(8,128)S(1)}, u32[]{:S(2)}, u32[]{:S(2)}) collective-permute-start(f32[1048,128]{1,0:T(8,128)} %get-tuple-element.29.own), channel_id=1, source_target_pairs={{0,1},{1,0},{2,3},{3,2},{4,5},{5,4},{6,7},{7,6},{8,9},{9,8},{10,11... | collective-permute-start | bytes 1609736 | tf_op jit(solution)/shard_map/ppermute | solution.py:336
  36.3 6.0 %collective-permute-start.5 = (f32[1048,128]{1,0:T(8,128)S(1)}, f32[1048,128]{1,0:T(8,128)S(1)}, u32[]{:S(2)}, u32[]{:S(2)}) collective-permute-start(f32[1048,128]{1,0:T(8,128)S(1)} %collective-permute-done.m1), channel_id=1, source_target_pairs={{0,1},{1,0},{2,3},{3,2},{4,5},{5,4},{6,7},{7,6},{8,9},{9,8},{10,11... | collective-permute-start | bytes 1609736 | tf_op jit(solution)/shard_map/ppermute | solution.py:336
  39.6 2.6 %collective-permute-start.6 = (f32[1048,128]{1,0:T(8,128)S(1)}, f32[1048,128]{1,0:T(8,128)S(1)}, u32[]{:S(2)}, u32[]{:S(2)}) collective-permute-start(f32[1048,128]{1,0:T(8,128)S(1)} %collective-permute-done.1.p1), channel_id=1, source_target_pairs={{0,1},{1,0},{2,3},{3,2},{4,5},{5,4},{6,7},{7,6},{8,9},{9,8},{10,11... | collective-permute-start | bytes 1609736 | tf_op jit(solution)/shard_map/ppermute | solution.py:336
  39.7 2.4 %collective-permute-start.7 = (f32[216,128]{1,0:T(8,128)S(1)}, f32[216,128]{1,0:T(8,128)S(1)}, u32[]{:S(2)}, u32[]{:S(2)}) collective-permute-start(f32[216,128]{1,0:T(8,128)S(1)} %collective-permute-done.2.m2), channel_id=1, source_target_pairs={{0,1},{1,0},{2,3},{3,2},{4,5},{5,4},{6,7},{7,6},{8,9},{9,8},{10,11... | collective-permute-start | bytes 331784 | tf_op jit(solution)/shard_map/ppermute | solution.py:336
  40.2 2.1 %collective-permute-start.8 = (f32[216,128]{1,0:T(8,128)S(1)}, f32[216,128]{1,0:T(8,128)S(1)}, u32[]{:S(2)}, u32[]{:S(2)}) collective-permute-start(f32[216,128]{1,0:T(8,128)S(1)} %collective-permute-done.3.p2), channel_id=1, source_target_pairs={{0,1},{1,0},{2,3},{3,2},{4,5},{5,4},{6,7},{7,6},{8,9},{9,8},{10,11... | collective-permute-start | bytes 331784 | tf_op jit(solution)/shard_map/ppermute | solution.py:336
  42.3 1.0 copy-start.1
  43.3 2.1 %copy-start.2 = (s32[2,1,128,8]{2,3,1,0:T(8,128)S(1)}, s32[2,1,128,8]{2,3,1,0:T(8,128)}, u32[]{:S(2)}) copy-start(s32[2,1,128,8]{2,3,1,0:T(8,128)} %param.9) | copy-start | bytes 24580
  44.9 4.8 %collective-permute-start.9 = (f32[696,128]{1,0:T(8,128)S(1)}, f32[696,128]{1,0:T(8,128)S(1)}, u32[]{:S(2)}, u32[]{:S(2)}) collective-permute-start(f32[696,128]{1,0:T(8,128)S(1)} %get-tuple-element.40), channel_id=1, source_target_pairs={{0,1},{1,2},{2,3},{3,4},{4,5},{5,6},{6,7},{7,8},{8,9},{9,10},{10,1... | collective-permute-start | bytes 1069064 | tf_op jit(solution)/shard_map/ppermute | solution.py:341
  45.4 7.1 %collective-permute-start.10 = (f32[696,128]{1,0:T(8,128)S(1)}, f32[696,128]{1,0:T(8,128)S(1)}, u32[]{:S(2)}, u32[]{:S(2)}) collective-permute-start(f32[696,128]{1,0:T(8,128)S(1)} %get-tuple-element.41), channel_id=1, source_target_pairs={{0,15},{1,0},{2,1},{3,2},{4,3},{5,4},{6,5},{7,6},{8,7},{9,8},{10,9... | collective-permute-start | bytes 1069064 | tf_op jit(solution)/shard_map/ppermute | solution.py:341
  57.7 1.9 %collective-permute-start.11 = (f32[40,128]{1,0:T(8,128)S(1)}, f32[40,128]{1,0:T(8,128)S(1)}, u32[]{:S(2)}, u32[]{:S(2)}) collective-permute-start(f32[40,128]{1,0:T(8,128)S(1)} %get-tuple-element.46), channel_id=1, source_target_pairs={{0,1},{1,0},{2,3},{3,2},{4,5},{5,4},{6,7},{7,6},{8,9},{9,8},{10,11... | collective-permute-start | bytes 61448 | tf_op jit(solution)/shard_map/ppermute | solution.py:336
  82.8 4.2 %collective-permute-start.12 = (f32[40,128]{1,0:T(8,128)S(1)}, f32[40,128]{1,0:T(8,128)S(1)}, u32[]{:S(2)}, u32[]{:S(2)}) collective-permute-start(f32[40,128]{1,0:T(8,128)S(1)} %bitcast.33), channel_id=1, source_target_pairs={{0,1},{1,0},{2,3},{3,2},{4,5},{5,4},{6,7},{7,6},{8,9},{9,8},{10,11... | collective-permute-start | bytes 61448 | tf_op jit(solution)/shard_map/ppermute | solution.py:336
  97.8 27.7 %copy-start = (f32[2,64,8,128]{3,2,1,0:T(8,128)S(1)}, f32[2,64,8,128]{3,2,1,0:T(8,128)}, u32[]{:S(2)}) copy-start(f32[2,64,8,128]{3,2,1,0:T(8,128)} %param.6) | copy-start | bytes 1572868
  97.9 1.3 collective-permute-start.13
  121.1 4.4 %collective-permute-start.14 = (f32[40,128]{1,0:T(8,128)S(1)}, f32[40,128]{1,0:T(8,128)S(1)}, u32[]{:S(2)}, u32[]{:S(2)}) collective-permute-start(f32[40,128]{1,0:T(8,128)S(1)} %bitcast.35), channel_id=1, source_target_pairs={{0,1},{1,0},{2,3},{3,2},{4,5},{5,4},{6,7},{7,6},{8,9},{9,8},{10,11... | collective-permute-start | bytes 61448 | tf_op jit(solution)/shard_map/ppermute | solution.py:336
where the time goes:
time: 132 us
  blocking collectives  45.1 us (34%)
  starting transfers between devices  38.7 us (29%)
  Pallas kernels  27.4 us (21%)
  waiting for transfers between devices  19.4 us (15%)
    all_to_all x4, blocking collectives, reduced(): lax.all_to_all(summed(lax.axis_size(axes), *parts), axes, 0, 0, tiled=True)  45.1 us
    pallas_call x5, Pallas kernels, call(): pl.pallas_call(kernel, out_shape=out_shape, in_specs=[SMEM] + [VMEM] * le...  25.2 us
    ppermute x9, starting transfers between devices, swap(): return lax.ppermute(value, 'ens', [(0, 1), (1, 0)])  14.5 us
    all_to_all x1, starting transfers between devices, per_device(): obs = lax.all_to_all(obs, LAT_LON, 0, 0, tiled=True)  12.8 us
    ppermute x6, starting transfers between devices, moved(): return lax.ppermute(value, axes, [(i, (i + by) % n) for i in range(n)])  11.4 us
    all_to_all x1, waiting for transfers between devices, per_device(): obs = lax.all_to_all(obs, LAT_LON, 0, 0, tiled=True)  8.37 us
    ppermute x6, waiting for transfers between devices, moved(): return lax.ppermute(value, axes, [(i, (i + by) % n) for i in range(n)])  5.65 us
    ppermute x9, waiting for transfers between devices, swap(): return lax.ppermute(value, 'ens', [(0, 1), (1, 0)])  5.33 us
  transfers between devices with their start and end apart: 16, of which 9 were waited for; matrix products, arithmetic and copies ran while one was open for 0% of the time, Pallas kernels for 1%

commit v1 on v0

--- a/solution.py
+++ b/solution.py
@@ -60,7 +60,13 @@
     for copy in copies[:2]:
         copy.wait()
     lines = [values[...], precision[...], jnp.zeros((96, MEMBERS), F32)]
-    obs[...] = jnp.concatenate(lines, axis=0).T[:, :32]
+    by_owner = jnp.concatenate(lines, axis=0).T
+    for x in range(4):
+        line = jnp.zeros((ROWS, MEMBERS), F32)
+        for y in range(4):
+            at = (4 * x + y) * 8
+            line = line + pltpu.roll(by_owner[at : at + 8], 32 * y, 1)
+        obs[pl.ds(x, 8, stride=4), :] = line
     for copy in copies[2:]:
         copy.wait()
     for k, (f, up_row, down_row) in enumerate(((1, 6, 0), (1, 7, 1), (0, 7, 0))):
@@ -120,8 +126,16 @@
             out[at + k * INIT : at + (k + 1) * INIT] = tile
 
 
+def by_xy(received, out):
+    for x in range(4):
+        line = received[pl.ds(x, 8, stride=4), :]
+        for y in range(4):
+            at = (4 * x + y) * 8
+            out[at : at + 8] = pltpu.roll(line, (4 - y) % 4 * 32, 1)
+
+
 def scatter_obs(pos, slots, received, weights, observed):
-    received = jnp.concatenate([received[...], jnp.zeros((MEMBERS, 96), F32)], axis=1).T
+    received = received[...].T
     values, precision = received[:16], received[16:32]
     lines = ROWS * HALF
     k = iota((lines, MEMBERS), 0)
@@ -390,7 +404,7 @@
     two_far = shape(3 * HALF + INIT, COLS)
     own, up2, dn2, obs = pl.pallas_call(
         collect,
-        out_shape=[shape(OWN + INIT, COLS), two_far, two_far, shape(128, 32)],
+        out_shape=[shape(OWN + INIT, COLS), two_far, two_far, shape(32, 128)],
         in_specs=[pl.BlockSpec(memory_space=pl.ANY)] * 5,
         out_specs=[VMEM] * 4,
         scratch_shapes=[pltpu.VMEM((16, COLS), F32)] * 2 + [pltpu.SemaphoreType.DMA((5,))],
@@ -398,12 +412,10 @@
     near = [moved(own, LAT, 1), moved(own, LAT, -1)]
     far = [moved(up2, LAT, 2), moved(dn2, LAT, -2)]
     own_other = swap(own)
-    obs = lax.all_to_all(obs, LAT_LON, 0, 0, tiled=True)
+    obs = lax.all_to_all(obs, "lon", 0, 0, tiled=True)
     *halo, obs = lax.optimization_barrier((*near, *far, obs))
     blocks = [own, *halo]
     others = [own_other] + [swap(x) for x in halo]
-    weights, observed = call(scatter_obs, [shape(2, 512, 128), shape(2, 512, 128)], pos, slots, obs)
-
     field = shape(EXT, WIDE, MEMBERS)
     half = shape(40, MEMBERS)
     square = shape(MEMBERS, MEMBERS)
@@ -411,7 +423,13 @@
     ext_fr, ext_fo, tiles, right, left = call(
         turn_rows, [field, field, shape(5 * INIT, COLS), edge, edge], pos, *blocks, *others
     )
+    right, left, obs = lax.optimization_barrier((right, left, obs))
     lz, rz = moved(right, LON_ENS, 1), moved(left, LON_ENS, -1)
+    obs = pl.pallas_call(
+        by_xy, out_shape=shape(128, 128), in_specs=[VMEM], out_specs=VMEM, compiler_params=params()
+    )(obs)
+    obs = lax.all_to_all(obs, LAT, 0, 0, tiled=True)
+    weights, observed = call(scatter_obs, [shape(2, 512, 128), shape(2, 512, 128)], pos, slots, obs)
     state = [pltpu.VMEM((EXT, WIDE, MEMBERS), F32)]
     ext_fr, ext_fo, table, keep, send = call(
         first_run, [field, field, square, half, half],

time: 132 us -> 136 us (1.030)
  blocking collectives: 45.1 us -> 56.1 us
  waiting for transfers between devices: 19.4 us -> 11.1 us
    all_to_all x0 -> x1, blocking collectives: none -> 9.55 us  [per_device(): obs = lax.all_to_all(obs, LAT, 0, 0, tiled=True)]
    ppermute x6, waiting for transfers between devices: 5.65 us -> 0.82 us  [moved(): return lax.ppermute(value, axes, [(i, (i + by) % n) for i in range(n)])]
    all_to_all x1, starting transfers between devices: 12.8 us -> 8.19 us  [per_device(): obs = lax.all_to_all(obs, 'lon', 0, 0, tiled=True)]
    ppermute x9, starting transfers between devices: 14.5 us -> 18.4 us  [swap(): return lax.ppermute(value, 'ens', [(0, 1), (1, 0)])]
    all_to_all x1, waiting for transfers between devices: 8.37 us -> 4.83 us  [per_device(): obs = lax.all_to_all(obs, 'lon', 0, 0, tiled=True)]
    all_to_all x4, blocking collectives: 45.1 us -> 46.5 us  [reduced(): lax.all_to_all(summed(lax.axis_size(axes), *parts), axes, 0, 0, tiled=True)]
    ppermute x6, starting transfers between devices: 11.4 us -> 12.8 us  [moved(): return lax.ppermute(value, axes, [(i, (i + by) % n) for i in range(n)])]
  transfers between devices with their start and end apart: 16 -> 16, of which waited for: 9 -> 8; matrix products, arithmetic and copies ran while one was open for 0% -> 0% of each run, Pallas kernels for 1% -> 1%
where the time goes in v1:
time: 136 us; the launch traced here: 135 us
  blocking collectives  56.1 us (41%)
  starting transfers between devices  39.4 us (29%)
  Pallas kernels  27.4 us (20%)
  waiting for transfers between devices  11.1 us (8%)
    all_to_all x4, blocking collectives, reduced(): lax.all_to_all(summed(lax.axis_size(axes), *parts), axes, 0, 0, tiled=True)  46.5 us
    pallas_call x5, Pallas kernels, call(): pl.pallas_call(kernel, out_shape=out_shape, in_specs=[SMEM] + [VMEM] * le...  25.3 us
    ppermute x9, starting transfers between devices, swap(): return lax.ppermute(value, 'ens', [(0, 1), (1, 0)])  18.4 us
    ppermute x6, starting transfers between devices, moved(): return lax.ppermute(value, axes, [(i, (i + by) % n) for i in range(n)])  12.8 us
    all_to_all x1, blocking collectives, per_device(): obs = lax.all_to_all(obs, LAT, 0, 0, tiled=True)  9.55 us
    all_to_all x1, starting transfers between devices, per_device(): obs = lax.all_to_all(obs, 'lon', 0, 0, tiled=True)  8.19 us
    ppermute x9, waiting for transfers between devices, swap(): return lax.ppermute(value, 'ens', [(0, 1), (1, 0)])  5.43 us
    all_to_all x1, waiting for transfers between devices, per_device(): obs = lax.all_to_all(obs, 'lon', 0, 0, tiled=True)  4.83 us
  transfers between devices with their start and end apart: 16, of which 8 were waited for; matrix products, arithmetic and copies ran while one was open for 0% of the time, Pallas kernels for 1%

profile of v1, /device:TPU:1, one launch (start us, length us, event | category | flops | bytes accessed | tf_op | source)
XLA Modules:
  0.0 135.2 jit_solution(1365550486997215707)
XLA Ops:
  0.0 2.0 %shard_map.64 = (f32[1048,128]{1,0:T(8,128)}, f32[216,128]{1,0:T(8,128)}, f32[216,128]{1,0:T(8,128)}, f32[32,128]{1,0:T(8,128)}) custom-call(f32[1024,128]{1,0:T(8,128)} %bitcast.30, f32[8,128]{1,0:T(8,128)} %height_hbm.1, f32[16,128]{1,0:T(8,128)} %bitcast.45, f32[16,128]{1,0:T(8,128)} %bitcast.46, f32[16,128]{1,0:T(8,128)} %bitcast.47), custom_call_target="tpu_custom_call" | custom-call | tf_op jit(solution)/shard_map/pallas_call | solution.py:405
  2.0 5.8 %collective-permute-start.1 = (f32[1048,128]{1,0:T(8,128)}, f32[1048,128]{1,0:T(8,128)S(1)}, u32[]{:S(2)}, u32[]{:S(2)}) collective-permute-start(f32[1048,128]{1,0:T(8,128)} %get-tuple-element.32.own), channel_id=1, source_target_pairs={{0,240},{16,0},{32,16},{48,32},{64,48},{80,64},{96,80},{112,96},{1... | collective-permute-start | bytes 1609736 | tf_op jit(solution)/shard_map/ppermute | solution.py:355
  7.8 5.1 %collective-permute-start.3 = (f32[216,128]{1,0:T(8,128)}, f32[216,128]{1,0:T(8,128)S(1)}, u32[]{:S(2)}, u32[]{:S(2)}) collective-permute-start(f32[216,128]{1,0:T(8,128)} %get-tuple-element.34), channel_id=1, source_target_pairs={{0,224},{16,240},{32,0},{48,16},{64,32},{80,48},{96,64},{112,80},{... | collective-permute-start | bytes 331784 | tf_op jit(solution)/shard_map/ppermute | solution.py:355
  12.9 8.2 %all-to-all-start = ((f32[8,4,128]{2,1,0:T(4,128)}), f32[8,4,128]{2,1,0:T(4,128)S(1)}, u32[]{:S(2)}, u32[]{:S(2)}) async-start(f32[8,4,128]{2,1,0:T(4,128)} %bitcast.44), calls=%async_computation | async-start | bytes 32768 | tf_op jit(solution)/shard_map/all_to_all | solution.py:415
  21.1 1.8 %collective-permute-start.4 = (f32[1048,128]{1,0:T(8,128)}, f32[1048,128]{1,0:T(8,128)S(1)}, u32[]{:S(2)}, u32[]{:S(2)}) collective-permute-start(f32[1048,128]{1,0:T(8,128)} %get-tuple-element.32.own), channel_id=1, source_target_pairs={{0,1},{1,0},{2,3},{3,2},{4,5},{5,4},{6,7},{7,6},{8,9},{9,8},{10,11... | collective-permute-start | bytes 1609736 | tf_op jit(solution)/shard_map/ppermute | solution.py:350
  22.9 4.8 %all-to-all-done = f32[8,4,128]{2,1,0:T(4,128)S(1)} async-done(((f32[8,4,128]{2,1,0:T(4,128)}), f32[8,4,128]{2,1,0:T(4,128)S(1)}, u32[]{:S(2)}, u32[]{:S(2)}) %all-to-all-start) | async-done | bytes 16416 | tf_op jit(solution)/shard_map/all_to_all | solution.py:415
  28.6 2.7 %collective-permute-start.5 = (f32[1048,128]{1,0:T(8,128)S(1)}, f32[1048,128]{1,0:T(8,128)S(1)}, u32[]{:S(2)}, u32[]{:S(2)}) collective-permute-start(f32[1048,128]{1,0:T(8,128)S(1)} %collective-permute-done.m1), channel_id=1, source_target_pairs={{0,1},{1,0},{2,3},{3,2},{4,5},{5,4},{6,7},{7,6},{8,9},{9,8},{10,11... | collective-permute-start | bytes 1609736 | tf_op jit(solution)/shard_map/ppermute | solution.py:350
  31.9 1.9 %collective-permute-done.7.m2_o = f32[216,128]{1,0:T(8,128)S(1)} collective-permute-done((f32[216,128]{1,0:T(8,128)S(1)}, f32[216,128]{1,0:T(8,128)S(1)}, u32[]{:S(2)}, u32[]{:S(2)}) %collective-permute-start.7) | collective-permute-done | bytes 110624 | tf_op jit(solution)/shard_map/ppermute | solution.py:350
  33.9 1.0 copy-done.1
  35.0 1.5 %shard_map.65 = (f32[28,112,128]{2,1,0:T(8,128)S(1)}, f32[28,112,128]{2,1,0:T(8,128)S(1)}, f32[120,128]{1,0:T(8,128)S(1)}, f32[696,128]{1,0:T(8,128)S(1)}, f32[696,128]{1,0:T(8,128)S(1)}) custom-call(s32[2]{0:T(128)S(1)} %pad_add_fusion.pos, f32[1048,128]{1,0:T(8,128)S(1)} %copy-done.1, f32[1048,128]{1,0:T(8,128)S(1)} %collective-permute-done.m1, ...), custom_call_target="tpu_custom_call" | custom-call | tf_op jit(solution)/shard_map/pallas_call | solution.py:387
  36.5 1.9 %collective-permute-start.9 = (f32[696,128]{1,0:T(8,128)S(1)}, f32[696,128]{1,0:T(8,128)S(1)}, u32[]{:S(2)}, u32[]{:S(2)}) collective-permute-start(f32[696,128]{1,0:T(8,128)S(1)} %get-tuple-element.46), channel_id=1, source_target_pairs={{0,1},{1,2},{2,3},{3,4},{4,5},{5,6},{6,7},{7,8},{8,9},{9,10},{10,1... | collective-permute-start | bytes 1069064 | tf_op jit(solution)/shard_map/ppermute | solution.py:355
  38.5 9.6 %all_to_all.43 = f32[16,8,128]{2,1,0:T(8,128)S(1)} all-to-all(f32[16,8,128]{2,1,0:T(8,128)S(1)} %bitcast.32), channel_id=1, replica_groups=mesh['lat_0'=4,'lat_1'=4,'lon'=8,'ens'=2] {'lat_0','lat_1'}, dimensions={0} | all-to-all | bytes 131072 | tf_op jit(solution)/shard_map/all_to_all | solution.py:431
  48.1 1.5 %shard_map.67 = (f32[2,512,128]{2,1,0:T(8,128)S(1)}, f32[2,512,128]{2,1,0:T(8,128)S(1)}) custom-call(s32[2]{0:T(128)S(1)} %pad_add_fusion.pos, s32[16,128]{1,0:T(8,128)S(1)} %bitcast.43, f32[128,128]{1,0:T(8,128)S(1)} %bitcast.33), custom_call_target="tpu_custom_call" | custom-call | tf_op jit(solution)/shard_map/pallas_call | solution.py:387
  49.5 5.2 %shard_map.68 = (f32[28,112,128]{2,1,0:T(8,128)S(1)}, f32[28,112,128]{2,1,0:T(8,128)S(1)}, f32[128,128]{1,0:T(8,128)S(1)}, f32[40,128]{1,0:T(8,128)S(1)}, f32[40,128]{1,0:T(8,128)S(1)}) custom-call(s32[2]{0:T(128)S(1)} %pad_add_fusion.pos, f32[28,112,128]{2,1,0:T(8,128)S(1)} %get-tuple-element.40.fr, ...), custom_call_target="tpu_custom_call", output_to_operand_aliasing={{0}: (1, {}), {1}: (2, {})} | custom-call | tf_op jit(solution)/shard_map/pallas_call | solution.py:387
  54.7 5.6 %collective-permute-start.11 = (f32[40,128]{1,0:T(8,128)S(1)}, f32[40,128]{1,0:T(8,128)S(1)}, u32[]{:S(2)}, u32[]{:S(2)}) collective-permute-start(f32[40,128]{1,0:T(8,128)S(1)} %get-tuple-element.52), channel_id=1, source_target_pairs={{0,1},{1,0},{2,3},{3,2},{4,5},{5,4},{6,7},{7,6},{8,9},{9,8},{10,11... | collective-permute-start | bytes 61448 | tf_op jit(solution)/shard_map/ppermute | solution.py:350
  60.4 0.8 collective-permute-done.11
  61.2 10.9 %all_to_all.44.refs_0_ = f32[16,40,128]{2,1,0:T(8,128)S(1)} all-to-all(f32[16,40,128]{2,1,0:T(8,128)S(1)} %shard_map.69), channel_id=1, replica_groups=mesh['lat_0'=4,'lat_1'=4,'lon'=8,'ens'=2] {'lat_0','lat_1'}, dimensions={0} | all-to-all | bytes 655360 | tf_op jit(solution)/shard_map/all_to_all | solution.py:381
  72.2 13.7 %all_to_all.45.refs_0_ = f32[8,40,128]{2,1,0:T(8,128)S(1)} all-to-all(f32[8,40,128]{2,1,0:T(8,128)S(1)} %shard_map.70), channel_id=1, replica_groups=mesh['lat_0'=4,'lat_1'=4,'lon'=8,'ens'=2] {'lon'}, dimensions={0} | all-to-all | bytes 327680 | tf_op jit(solution)/shard_map/all_to_all | solution.py:381
  85.9 3.7 %collective-permute-start.12 = (f32[40,128]{1,0:T(8,128)S(1)}, f32[40,128]{1,0:T(8,128)S(1)}, u32[]{:S(2)}, u32[]{:S(2)}) collective-permute-start(f32[40,128]{1,0:T(8,128)S(1)} %bitcast.34), channel_id=1, source_target_pairs={{0,1},{1,0},{2,3},{3,2},{4,5},{5,4},{6,7},{7,6},{8,9},{9,8},{10,11... | collective-permute-start | bytes 61448 | tf_op jit(solution)/shard_map/ppermute | solution.py:350
  90.5 10.8 %shard_map.72 = (f32[128,128]{1,0:T(8,128)S(1)}, f32[40,128]{1,0:T(8,128)S(1)}, f32[40,128]{1,0:T(8,128)S(1)}) custom-call(s32[2]{0:T(128)S(1)} %pad_add_fusion.pos, f32[40,128]{1,0:T(8,128)S(1)} %bitcast.35, f32[40,128]{1,0:T(8,128)S(1)} %collective-permute-done.12.other, f32[28,112,128]{2,1,0:T(8,128)S(1)} %get-tuple-element.53.fr, ...), custom_call_target="tpu_custom_call" | custom-call | tf_op jit(solution)/shard_map/pallas_call | solution.py:387
  102.6 11.2 %all_to_all.46.refs_0_ = f32[16,40,128]{2,1,0:T(8,128)S(1)} all-to-all(f32[16,40,128]{2,1,0:T(8,128)S(1)} %shard_map.73), channel_id=1, replica_groups=mesh['lat_0'=4,'lat_1'=4,'lon'=8,'ens'=2] {'lat_0','lat_1'}, dimensions={0} | all-to-all | bytes 655360 | tf_op jit(solution)/shard_map/all_to_all | solution.py:381
  113.8 10.8 %all_to_all.47.refs_0_ = f32[8,40,128]{2,1,0:T(8,128)S(1)} all-to-all(f32[8,40,128]{2,1,0:T(8,128)S(1)} %shard_map.74), channel_id=1, replica_groups=mesh['lat_0'=4,'lat_1'=4,'lon'=8,'ens'=2] {'lon'}, dimensions={0} | all-to-all | bytes 327680 | tf_op jit(solution)/shard_map/all_to_all | solution.py:381
  124.6 3.5 %collective-permute-start.14 = (f32[40,128]{1,0:T(8,128)S(1)}, f32[40,128]{1,0:T(8,128)S(1)}, u32[]{:S(2)}, u32[]{:S(2)}) collective-permute-start(f32[40,128]{1,0:T(8,128)S(1)} %bitcast.36), channel_id=1, source_target_pairs={{0,1},{1,0},{2,3},{3,2},{4,5},{5,4},{6,7},{7,6},{8,9},{9,8},{10,11... | collective-permute-start | bytes 61448 | tf_op jit(solution)/shard_map/ppermute | solution.py:350
  129.0 6.2 %shard_map.76 = f32[1024,128]{1,0:T(8,128)} custom-call(s32[2]{0:T(128)S(1)} %pad_add_fusion.pos, f32[40,128]{1,0:T(8,128)S(1)} %bitcast.37, f32[40,128]{1,0:T(8,128)S(1)} %collective-permute-done.14.other, f32[128,128]{1,0:T(8,128)S(1)} %get-tuple-element.58.k1, f32[1024,128]{1,0:T(8,128)S(1)} %bitcast.31, f32[1048,128]{1,0:T(8,128)S(1)} %collective-permute-done.4.own_o.other_p), custom_call_target="tpu_custom_call" | custom-call | tf_op jit(solution)/shard_map/pallas_call | solution.py:387
  (33 shorter events, 4.8 us)
Async XLA Ops:
  2.0 25.7 %collective-permute-start.1 = (f32[1048,128]{1,0:T(8,128)}, f32[1048,128]{1,0:T(8,128)S(1)}, u32[]{:S(2)}, u32[]{:S(2)}) collective-permute-start(f32[1048,128]{1,0:T(8,128)} %get-tuple-element.32.own), channel_id=1, source_target_pairs={{0,240},{16,0},{32,16},{48,32},{64,48},{80,64},{96,80},{112,96},{1... | collective-permute-start | bytes 1609736 | tf_op jit(solution)/shard_map/ppermute | solution.py:355
  7.8 20.7 %collective-permute-start = (f32[1048,128]{1,0:T(8,128)}, f32[1048,128]{1,0:T(8,128)S(1)}, u32[]{:S(2)}, u32[]{:S(2)}) collective-permute-start(f32[1048,128]{1,0:T(8,128)} %get-tuple-element.32.own), channel_id=1, source_target_pairs={{0,16},{16,32},{32,48},{48,64},{64,80},{80,96},{96,112},{112,128},... | collective-permute-start | bytes 1609736 | tf_op jit(solution)/shard_map/ppermute | solution.py:355
  7.8 19.9 %collective-permute-start.2 = (f32[216,128]{1,0:T(8,128)}, f32[216,128]{1,0:T(8,128)S(1)}, u32[]{:S(2)}, u32[]{:S(2)}) collective-permute-start(f32[216,128]{1,0:T(8,128)} %get-tuple-element.33), channel_id=1, source_target_pairs={{0,32},{16,48},{32,64},{48,80},{64,96},{80,112},{96,128},{112,144}... | collective-permute-start | bytes 331784 | tf_op jit(solution)/shard_map/ppermute | solution.py:355
  7.8 19.9 %collective-permute-start.3 = (f32[216,128]{1,0:T(8,128)}, f32[216,128]{1,0:T(8,128)S(1)}, u32[]{:S(2)}, u32[]{:S(2)}) collective-permute-start(f32[216,128]{1,0:T(8,128)} %get-tuple-element.34), channel_id=1, source_target_pairs={{0,224},{16,240},{32,0},{48,16},{64,32},{80,48},{96,64},{112,80},{... | collective-permute-start | bytes 331784 | tf_op jit(solution)/shard_map/ppermute | solution.py:355
  12.9 14.8 %all-to-all-start = ((f32[8,4,128]{2,1,0:T(4,128)}), f32[8,4,128]{2,1,0:T(4,128)S(1)}, u32[]{:S(2)}, u32[]{:S(2)}) async-start(f32[8,4,128]{2,1,0:T(4,128)} %bitcast.44), calls=%async_computation | async-start | bytes 32768 | tf_op jit(solution)/shard_map/all_to_all | solution.py:415
  21.1 10.8 %collective-permute-start.4 = (f32[1048,128]{1,0:T(8,128)}, f32[1048,128]{1,0:T(8,128)S(1)}, u32[]{:S(2)}, u32[]{:S(2)}) collective-permute-start(f32[1048,128]{1,0:T(8,128)} %get-tuple-element.32.own), channel_id=1, source_target_pairs={{0,1},{1,0},{2,3},{3,2},{4,5},{5,4},{6,7},{7,6},{8,9},{9,8},{10,11... | collective-permute-start | bytes 1609736 | tf_op jit(solution)/shard_map/ppermute | solution.py:350
  28.6 5.4 %collective-permute-start.5 = (f32[1048,128]{1,0:T(8,128)S(1)}, f32[1048,128]{1,0:T(8,128)S(1)}, u32[]{:S(2)}, u32[]{:S(2)}) collective-permute-start(f32[1048,128]{1,0:T(8,128)S(1)} %collective-permute-done.m1), channel_id=1, source_target_pairs={{0,1},{1,0},{2,3},{3,2},{4,5},{5,4},{6,7},{7,6},{8,9},{9,8},{10,11... | collective-permute-start | bytes 1609736 | tf_op jit(solution)/shard_map/ppermute | solution.py:350
  31.3 2.6 %collective-permute-start.6 = (f32[1048,128]{1,0:T(8,128)S(1)}, f32[1048,128]{1,0:T(8,128)S(1)}, u32[]{:S(2)}, u32[]{:S(2)}) collective-permute-start(f32[1048,128]{1,0:T(8,128)S(1)} %collective-permute-done.1.p1), channel_id=1, source_target_pairs={{0,1},{1,0},{2,3},{3,2},{4,5},{5,4},{6,7},{7,6},{8,9},{9,8},{10,11... | collective-permute-start | bytes 1609736 | tf_op jit(solution)/shard_map/ppermute | solution.py:350
  31.3 2.5 %collective-permute-start.7 = (f32[216,128]{1,0:T(8,128)S(1)}, f32[216,128]{1,0:T(8,128)S(1)}, u32[]{:S(2)}, u32[]{:S(2)}) collective-permute-start(f32[216,128]{1,0:T(8,128)S(1)} %collective-permute-done.2.m2), channel_id=1, source_target_pairs={{0,1},{1,0},{2,3},{3,2},{4,5},{5,4},{6,7},{7,6},{8,9},{9,8},{10,11... | collective-permute-start | bytes 331784 | tf_op jit(solution)/shard_map/ppermute | solution.py:350
  31.8 2.1 %collective-permute-start.8 = (f32[216,128]{1,0:T(8,128)S(1)}, f32[216,128]{1,0:T(8,128)S(1)}, u32[]{:S(2)}, u32[]{:S(2)}) collective-permute-start(f32[216,128]{1,0:T(8,128)S(1)} %collective-permute-done.3.p2), channel_id=1, source_target_pairs={{0,1},{1,0},{2,3},{3,2},{4,5},{5,4},{6,7},{7,6},{8,9},{9,8},{10,11... | collective-permute-start | bytes 331784 | tf_op jit(solution)/shard_map/ppermute | solution.py:350
  33.9 1.0 copy-start.1
  35.0 13.1 %copy-start.2 = (s32[2,1,128,8]{2,3,1,0:T(8,128)S(1)}, s32[2,1,128,8]{2,3,1,0:T(8,128)}, u32[]{:S(2)}) copy-start(s32[2,1,128,8]{2,3,1,0:T(8,128)} %param.9) | copy-start | bytes 24580
  36.5 13.0 %collective-permute-start.9 = (f32[696,128]{1,0:T(8,128)S(1)}, f32[696,128]{1,0:T(8,128)S(1)}, u32[]{:S(2)}, u32[]{:S(2)}) collective-permute-start(f32[696,128]{1,0:T(8,128)S(1)} %get-tuple-element.46), channel_id=1, source_target_pairs={{0,1},{1,2},{2,3},{3,4},{4,5},{5,6},{6,7},{7,8},{8,9},{9,10},{10,1... | collective-permute-start | bytes 1069064 | tf_op jit(solution)/shard_map/ppermute | solution.py:355
  38.4 11.1 %collective-permute-start.10 = (f32[696,128]{1,0:T(8,128)S(1)}, f32[696,128]{1,0:T(8,128)S(1)}, u32[]{:S(2)}, u32[]{:S(2)}) collective-permute-start(f32[696,128]{1,0:T(8,128)S(1)} %get-tuple-element.47), channel_id=1, source_target_pairs={{0,15},{1,0},{2,1},{3,2},{4,3},{5,4},{6,5},{7,6},{8,7},{9,8},{10,9... | collective-permute-start | bytes 1069064 | tf_op jit(solution)/shard_map/ppermute | solution.py:355
  54.7 6.5 %collective-permute-start.11 = (f32[40,128]{1,0:T(8,128)S(1)}, f32[40,128]{1,0:T(8,128)S(1)}, u32[]{:S(2)}, u32[]{:S(2)}) collective-permute-start(f32[40,128]{1,0:T(8,128)S(1)} %get-tuple-element.52), channel_id=1, source_target_pairs={{0,1},{1,0},{2,3},{3,2},{4,5},{5,4},{6,7},{7,6},{8,9},{9,8},{10,11... | collective-permute-start | bytes 61448 | tf_op jit(solution)/shard_map/ppermute | solution.py:350
  85.9 4.6 %collective-permute-start.12 = (f32[40,128]{1,0:T(8,128)S(1)}, f32[40,128]{1,0:T(8,128)S(1)}, u32[]{:S(2)}, u32[]{:S(2)}) collective-permute-start(f32[40,128]{1,0:T(8,128)S(1)} %bitcast.34), channel_id=1, source_target_pairs={{0,1},{1,0},{2,3},{3,2},{4,5},{5,4},{6,7},{7,6},{8,9},{9,8},{10,11... | collective-permute-start | bytes 61448 | tf_op jit(solution)/shard_map/ppermute | solution.py:350
  101.3 27.7 %copy-start = (f32[2,64,8,128]{3,2,1,0:T(8,128)S(1)}, f32[2,64,8,128]{3,2,1,0:T(8,128)}, u32[]{:S(2)}) copy-start(f32[2,64,8,128]{3,2,1,0:T(8,128)} %param.6) | copy-start | bytes 1572868
  101.3 1.3 collective-permute-start.13
  124.6 4.4 %collective-permute-start.14 = (f32[40,128]{1,0:T(8,128)S(1)}, f32[40,128]{1,0:T(8,128)S(1)}, u32[]{:S(2)}, u32[]{:S(2)}) collective-permute-start(f32[40,128]{1,0:T(8,128)S(1)} %bitcast.36), channel_id=1, source_target_pairs={{0,1},{1,0},{2,3},{3,2},{4,5},{5,4},{6,7},{7,6},{8,9},{9,8},{10,11... | collective-permute-start | bytes 61448 | tf_op jit(solution)/shard_map/ppermute | solution.py:350

commit v2 on v0

--- a/solution.py
+++ b/solution.py
@@ -60,7 +60,7 @@
     for copy in copies[:2]:
         copy.wait()
     lines = [values[...], precision[...], jnp.zeros((96, MEMBERS), F32)]
-    obs[...] = jnp.concatenate(lines, axis=0).T[:, :32]
+    obs[...] = jnp.concatenate(lines, axis=0).T
     for copy in copies[2:]:
         copy.wait()
     for k, (f, up_row, down_row) in enumerate(((1, 6, 0), (1, 7, 1), (0, 7, 0))):
@@ -121,7 +121,7 @@
 
 
 def scatter_obs(pos, slots, received, weights, observed):
-    received = jnp.concatenate([received[...], jnp.zeros((MEMBERS, 96), F32)], axis=1).T
+    received = received[...].T
     values, precision = received[:16], received[16:32]
     lines = ROWS * HALF
     k = iota((lines, MEMBERS), 0)
@@ -290,9 +290,10 @@
     return lax.dot_general(lower, scaled, (((0,), (0,)), ((), ())), precision=HIGHEST, preferred_element_type=F32)
 
 
-def weights_of(pos, mine, other):
-    one = jnp.where(pos[1] == 0, mine, other)
-    two = jnp.where(pos[1] == 0, other, mine)
+def weights_of(parts):
+    one, two = parts[0], parts[1]
+    for k in range(2, parts.shape[0], 2):
+        one, two = one + parts[k], two + parts[k + 1]
     packed = jnp.concatenate([one[:32], two[:32]], axis=0)
     d, diagonal = one[32:33], one[33:34]
     turned = jnp.concatenate([packed, jnp.zeros((HALF, MEMBERS), F32)], axis=0).T
@@ -311,8 +312,8 @@
     return z - jnp.mean(z, axis=0, keepdims=True) + 1.0 / MEMBERS
 
 
-def second_run(pos, mine, other, fr, fo, table, weights, observed, k1, keep, send, FR, FO, H, U, V):
-    k = weights_of(pos, mine[...], other[...])
+def second_run(pos, parts, fr, fo, table, weights, observed, k1, keep, send, FR, FO, H, U, V):
+    k = weights_of(parts)
     k1[...] = k
     for src, out in ((fr, FR), (fo, FO)):
         new = jnp.dot(src[...].reshape(EXT * WIDE, MEMBERS), k, precision=HIGHEST, preferred_element_type=F32)
@@ -321,8 +322,8 @@
     gram(pos, H, weights[1], observed[1], keep, send)
 
 
-def last_update(pos, mine, other, k1, own_p, other_p, out):
-    k = jnp.dot(k1[...], weights_of(pos, mine[...], other[...]), precision=HIGHEST, preferred_element_type=F32)
+def last_update(pos, parts, k1, own_p, other_p, out):
+    k = jnp.dot(k1[...], weights_of(parts), precision=HIGHEST, preferred_element_type=F32)
 
     first = pos[1] == 0
     kt = k.T
@@ -362,11 +363,10 @@
 
 
 def reduced(keep, send):
-    parts = keep[None], swap(send)[None]
-    for axes in (LAT, "lon"):
+    parts = [keep[None], swap(send)[None]]
+    for axes in (LAT, LON_ENS):
         parts = [lax.all_to_all(summed(lax.axis_size(axes), *parts), axes, 0, 0, tiled=True)]
-    value = summed(1, *parts)[0]
-    return value, swap(value)
+    return parts[0]
 
 
 def call(kernel, out_shape, scalars, *args, scratch=(), aliases=None):
@@ -390,7 +390,7 @@
     two_far = shape(3 * HALF + INIT, COLS)
     own, up2, dn2, obs = pl.pallas_call(
         collect,
-        out_shape=[shape(OWN + INIT, COLS), two_far, two_far, shape(128, 32)],
+        out_shape=[shape(OWN + INIT, COLS), two_far, two_far, shape(128, 128)],
         in_specs=[pl.BlockSpec(memory_space=pl.ANY)] * 5,
         out_specs=[VMEM] * 4,
         scratch_shapes=[pltpu.VMEM((16, COLS), F32)] * 2 + [pltpu.SemaphoreType.DMA((5,))],
@@ -418,14 +418,14 @@
         pos, ext_fr, ext_fo, tiles, lz, rz, weights, observed,
         scratch=state * 3, aliases={1: 0, 2: 1},
     )
-    mine, other = reduced(keep, send)
+    parts = reduced(keep, send)
     k1, keep, send = call(
         second_run, [square, half, half],
-        pos, mine, other, ext_fr, ext_fo, table, weights, observed,
+        pos, parts, ext_fr, ext_fo, table, weights, observed,
         scratch=state * 5,
     )
-    mine, other = reduced(keep, send)
-    out = call(last_update, shape(2 * HALF * ROWS, COLS), pos, mine, other, k1, own_p, others[0])
+    parts = reduced(keep, send)
+    out = call(last_update, shape(2 * HALF * ROWS, COLS), pos, parts, k1, own_p, others[0])
     return out.reshape(parameters.shape)
 
 

time: 132 us -> 138 us (1.045)
  blocking collectives: 45.1 us -> 62.4 us
  starting transfers between devices: 38.7 us -> 32.3 us
  waiting for transfers between devices: 19.4 us -> 13.5 us
    all_to_all x4, blocking collectives: 45.1 us -> 62.4 us  [reduced(): lax.all_to_all(summed(lax.axis_size(axes), *parts), axes, 0, 0, tiled=True)]
    ppermute x9 -> x7, starting transfers between devices: 14.5 us -> 5.84 us  [swap(): return lax.ppermute(value, 'ens', [(0, 1), (1, 0)])]
    all_to_all x1, waiting for transfers between devices: 8.37 us -> 0.01 us  [per_device(): obs = lax.all_to_all(obs, LAT_LON, 0, 0, tiled=True)]
    ppermute x6, waiting for transfers between devices: 5.65 us -> 9.52 us  [moved(): return lax.ppermute(value, axes, [(i, (i + by) % n) for i in range(n)])]
    all_to_all x1, starting transfers between devices: 12.8 us -> 14.9 us  [per_device(): obs = lax.all_to_all(obs, LAT_LON, 0, 0, tiled=True)]
    ppermute x9 -> x7, waiting for transfers between devices: 5.33 us -> 3.98 us  [swap(): return lax.ppermute(value, 'ens', [(0, 1), (1, 0)])]
  transfers between devices with their start and end apart: 16 -> 14, of which waited for: 9 -> 8; matrix products, arithmetic and copies ran while one was open for 0% -> 0% of each run, Pallas kernels for 1% -> 1%
where the time goes in v2:
time: 138 us; the launch traced here: 137 us
  blocking collectives  62.4 us (45%)
  starting transfers between devices  32.3 us (23%)
  Pallas kernels  27.7 us (20%)
  waiting for transfers between devices  13.5 us (10%)
    all_to_all x4, blocking collectives, reduced(): lax.all_to_all(summed(lax.axis_size(axes), *parts), axes, 0, 0, tiled=True)  62.4 us
    pallas_call x5, Pallas kernels, call(): pl.pallas_call(kernel, out_shape=out_shape, in_specs=[SMEM] + [VMEM] * le...  25.6 us
    all_to_all x1, starting transfers between devices, per_device(): obs = lax.all_to_all(obs, LAT_LON, 0, 0, tiled=True)  14.9 us
    ppermute x6, starting transfers between devices, moved(): return lax.ppermute(value, axes, [(i, (i + by) % n) for i in range(n)])  11.6 us
    ppermute x6, waiting for transfers between devices, moved(): return lax.ppermute(value, axes, [(i, (i + by) % n) for i in range(n)])  9.52 us
    ppermute x7, starting transfers between devices, swap(): return lax.ppermute(value, 'ens', [(0, 1), (1, 0)])  5.84 us
    ppermute x7, waiting for transfers between devices, swap(): return lax.ppermute(value, 'ens', [(0, 1), (1, 0)])  3.98 us
  transfers between devices with their start and end apart: 14, of which 8 were waited for; matrix products, arithmetic and copies ran while one was open for 0% of the time, Pallas kernels for 1%

profile of v2, /device:TPU:1, one launch (start us, length us, event | category | flops | bytes accessed | tf_op | source)
XLA Modules:
  0.0 137.2 jit_solution(9341557978523219473)
XLA Ops:
  0.0 2.0 %shard_map.64 = (f32[1048,128]{1,0:T(8,128)}, f32[216,128]{1,0:T(8,128)}, f32[216,128]{1,0:T(8,128)}, f32[128,128]{1,0:T(8,128)}) custom-call(f32[1024,128]{1,0:T(8,128)} %bitcast.28, f32[8,128]{1,0:T(8,128)} %height_hbm.1, f32[16,128]{1,0:T(8,128)} %bitcast.37, f32[16,128]{1,0:T(8,128)} %bitcast.38, f32[16,128]{1,0:T(8,128)} %bitcast.39), custom_call_target="tpu_custom_call" | custom-call | tf_op jit(solution)/shard_map/pallas_call | solution.py:391
  2.0 5.8 %collective-permute-start.1 = (f32[1048,128]{1,0:T(8,128)}, f32[1048,128]{1,0:T(8,128)S(1)}, u32[]{:S(2)}, u32[]{:S(2)}) collective-permute-start(f32[1048,128]{1,0:T(8,128)} %get-tuple-element.29.own), channel_id=1, source_target_pairs={{0,240},{16,0},{32,16},{48,32},{64,48},{80,64},{96,80},{112,96},{1... | collective-permute-start | bytes 1609736 | tf_op jit(solution)/shard_map/ppermute | solution.py:342
  7.9 14.9 %all-to-all-start = ((f32[128,1,128]{2,1,0:T(1,128)}), f32[128,1,128]{2,1,0:T(1,128)S(1)}, u32[]{:S(2)}, u32[]{:S(2)}) async-start(f32[128,1,128]{2,1,0:T(1,128)} %bitcast.36), calls=%async_computation | async-start | bytes 131072 | tf_op jit(solution)/shard_map/all_to_all | solution.py:401
  22.8 2.2 %collective-permute-start.2 = (f32[216,128]{1,0:T(8,128)}, f32[216,128]{1,0:T(8,128)S(1)}, u32[]{:S(2)}, u32[]{:S(2)}) collective-permute-start(f32[216,128]{1,0:T(8,128)} %get-tuple-element.30), channel_id=1, source_target_pairs={{0,32},{16,48},{32,64},{48,80},{64,96},{80,112},{96,128},{112,144}... | collective-permute-start | bytes 331784 | tf_op jit(solution)/shard_map/ppermute | solution.py:342
  24.9 3.0 %collective-permute-start.3 = (f32[216,128]{1,0:T(8,128)}, f32[216,128]{1,0:T(8,128)S(1)}, u32[]{:S(2)}, u32[]{:S(2)}) collective-permute-start(f32[216,128]{1,0:T(8,128)} %get-tuple-element.31), channel_id=1, source_target_pairs={{0,224},{16,240},{32,0},{48,16},{64,32},{80,48},{96,64},{112,80},{... | collective-permute-start | bytes 331784 | tf_op jit(solution)/shard_map/ppermute | solution.py:342
  27.9 2.1 %collective-permute-start.4 = (f32[1048,128]{1,0:T(8,128)}, f32[1048,128]{1,0:T(8,128)S(1)}, u32[]{:S(2)}, u32[]{:S(2)}) collective-permute-start(f32[1048,128]{1,0:T(8,128)} %get-tuple-element.29.own), channel_id=1, source_target_pairs={{0,1},{1,0},{2,3},{3,2},{4,5},{5,4},{6,7},{7,6},{8,9},{9,8},{10,11... | collective-permute-start | bytes 1609736 | tf_op jit(solution)/shard_map/ppermute | solution.py:337
  30.7 3.2 %collective-permute-done.3.p2 = f32[216,128]{1,0:T(8,128)S(1)} collective-permute-done((f32[216,128]{1,0:T(8,128)}, f32[216,128]{1,0:T(8,128)S(1)}, u32[]{:S(2)}, u32[]{:S(2)}) %collective-permute-start.3) | collective-permute-done | bytes 110624 | tf_op jit(solution)/shard_map/ppermute | solution.py:342
  33.9 2.1 %collective-permute-start.5 = (f32[1048,128]{1,0:T(8,128)S(1)}, f32[1048,128]{1,0:T(8,128)S(1)}, u32[]{:S(2)}, u32[]{:S(2)}) collective-permute-start(f32[1048,128]{1,0:T(8,128)S(1)} %collective-permute-done.m1), channel_id=1, source_target_pairs={{0,1},{1,0},{2,3},{3,2},{4,5},{5,4},{6,7},{7,6},{8,9},{9,8},{10,11... | collective-permute-start | bytes 1609736 | tf_op jit(solution)/shard_map/ppermute | solution.py:337
  36.7 1.8 %collective-permute-done.7.m2_o = f32[216,128]{1,0:T(8,128)S(1)} collective-permute-done((f32[216,128]{1,0:T(8,128)S(1)}, f32[216,128]{1,0:T(8,128)S(1)}, u32[]{:S(2)}, u32[]{:S(2)}) %collective-permute-start.7) | collective-permute-done | bytes 110624 | tf_op jit(solution)/shard_map/ppermute | solution.py:337
  38.6 1.0 copy-done.1
  39.7 1.5 %shard_map.65 = (f32[28,112,128]{2,1,0:T(8,128)S(1)}, f32[28,112,128]{2,1,0:T(8,128)S(1)}, f32[120,128]{1,0:T(8,128)S(1)}, f32[696,128]{1,0:T(8,128)S(1)}, f32[696,128]{1,0:T(8,128)S(1)}) custom-call(s32[2]{0:T(128)S(1)} %pad_add_fusion.pos, f32[1048,128]{1,0:T(8,128)S(1)} %copy-done.1, f32[1048,128]{1,0:T(8,128)S(1)} %collective-permute-done.m1, ...), custom_call_target="tpu_custom_call" | custom-call | tf_op jit(solution)/shard_map/pallas_call | solution.py:373
  41.8 1.5 %shard_map.66 = (f32[2,512,128]{2,1,0:T(8,128)S(1)}, f32[2,512,128]{2,1,0:T(8,128)S(1)}) custom-call(s32[2]{0:T(128)S(1)} %pad_add_fusion.pos, s32[16,128]{1,0:T(8,128)S(1)} %bitcast.35, f32[128,128]{1,0:T(8,128)S(1)} %bitcast.30), custom_call_target="tpu_custom_call" | custom-call | tf_op jit(solution)/shard_map/pallas_call | solution.py:373
  43.3 2.9 %collective-permute-done.9.lz = f32[696,128]{1,0:T(8,128)S(1)} collective-permute-done((f32[696,128]{1,0:T(8,128)S(1)}, f32[696,128]{1,0:T(8,128)S(1)}, u32[]{:S(2)}, u32[]{:S(2)}) %collective-permute-start.9) | collective-permute-done | bytes 356384 | tf_op jit(solution)/shard_map/ppermute | solution.py:342
  46.1 2.8 %collective-permute-done.10.rz = f32[696,128]{1,0:T(8,128)S(1)} collective-permute-done((f32[696,128]{1,0:T(8,128)S(1)}, f32[696,128]{1,0:T(8,128)S(1)}, u32[]{:S(2)}, u32[]{:S(2)}) %collective-permute-start.10) | collective-permute-done | bytes 356384 | tf_op jit(solution)/shard_map/ppermute | solution.py:342
  48.9 5.5 %shard_map.67 = (f32[28,112,128]{2,1,0:T(8,128)S(1)}, f32[28,112,128]{2,1,0:T(8,128)S(1)}, f32[128,128]{1,0:T(8,128)S(1)}, f32[40,128]{1,0:T(8,128)S(1)}, f32[40,128]{1,0:T(8,128)S(1)}) custom-call(s32[2]{0:T(128)S(1)} %pad_add_fusion.pos, f32[28,112,128]{2,1,0:T(8,128)S(1)} %get-tuple-element.37.fr, ...), custom_call_target="tpu_custom_call", output_to_operand_aliasing={{0}: (1, {}), {1}: (2, {})} | custom-call | tf_op jit(solution)/shard_map/pallas_call | solution.py:373
  54.4 1.0 collective-permute-start.11
  55.4 0.8 collective-permute-done.11
  56.2 12.5 %all_to_all.32.refs_0_ = f32[16,40,128]{2,1,0:T(8,128)S(1)} all-to-all(f32[16,40,128]{2,1,0:T(8,128)S(1)} %shard_map.68), channel_id=1, replica_groups=mesh['lat_0'=4,'lat_1'=4,'lon'=8,'ens'=2] {'lat_0','lat_1'}, dimensions={0} | all-to-all | bytes 655360 | tf_op jit(solution)/shard_map/all_to_all | solution.py:368
  68.8 21.8 %all_to_all.33.parts = f32[16,40,128]{2,1,0:T(8,128)S(1)} all-to-all(f32[16,40,128]{2,1,0:T(8,128)S(1)} %shard_map.69), channel_id=1, replica_groups=mesh['lat_0'=4,'lat_1'=4,'lon'=8,'ens'=2] {'lon','ens'}, dimensions={0} | all-to-all | bytes 655360 | tf_op jit(solution)/shard_map/all_to_all | solution.py:368
  90.6 10.9 %shard_map.70 = (f32[128,128]{1,0:T(8,128)S(1)}, f32[40,128]{1,0:T(8,128)S(1)}, f32[40,128]{1,0:T(8,128)S(1)}) custom-call(s32[2]{0:T(128)S(1)} %pad_add_fusion.pos, f32[16,40,128]{2,1,0:T(8,128)S(1)} %all_to_all.33.parts, f32[28,112,128]{2,1,0:T(8,128)S(1)} %get-tuple-element.47.fr, f32[28,112,128]{2,1,0:T(8,128)S(1)} %get-tuple-element.48.fo, ...), custom_call_target="tpu_custom_call" | custom-call | tf_op jit(solution)/shard_map/pallas_call | solution.py:373
  101.6 1.2 collective-permute-done.12
  102.8 11.4 %all_to_all.34.refs_0_ = f32[16,40,128]{2,1,0:T(8,128)S(1)} all-to-all(f32[16,40,128]{2,1,0:T(8,128)S(1)} %shard_map.71), channel_id=1, replica_groups=mesh['lat_0'=4,'lat_1'=4,'lon'=8,'ens'=2] {'lat_0','lat_1'}, dimensions={0} | all-to-all | bytes 655360 | tf_op jit(solution)/shard_map/all_to_all | solution.py:368
  114.2 16.7 %all_to_all.35.parts = f32[16,40,128]{2,1,0:T(8,128)S(1)} all-to-all(f32[16,40,128]{2,1,0:T(8,128)S(1)} %shard_map.72), channel_id=1, replica_groups=mesh['lat_0'=4,'lat_1'=4,'lon'=8,'ens'=2] {'lon','ens'}, dimensions={0} | all-to-all | bytes 655360 | tf_op jit(solution)/shard_map/all_to_all | solution.py:368
  130.9 6.3 %shard_map.73 = f32[1024,128]{1,0:T(8,128)} custom-call(s32[2]{0:T(128)S(1)} %pad_add_fusion.pos, f32[16,40,128]{2,1,0:T(8,128)S(1)} %all_to_all.35.parts, f32[128,128]{1,0:T(8,128)S(1)} %get-tuple-element.52.k1, f32[1024,128]{1,0:T(8,128)S(1)} %bitcast.29, f32[1048,128]{1,0:T(8,128)S(1)} %collective-permute-done.4.own_o.other_p), custom_call_target="tpu_custom_call" | custom-call | tf_op jit(solution)/shard_map/pallas_call | solution.py:373
  (25 shorter events, 2.3 us)
Async XLA Ops:
  2.0 31.9 %collective-permute-start.1 = (f32[1048,128]{1,0:T(8,128)}, f32[1048,128]{1,0:T(8,128)S(1)}, u32[]{:S(2)}, u32[]{:S(2)}) collective-permute-start(f32[1048,128]{1,0:T(8,128)} %get-tuple-element.29.own), channel_id=1, source_target_pairs={{0,240},{16,0},{32,16},{48,32},{64,48},{80,64},{96,80},{112,96},{1... | collective-permute-start | bytes 1609736 | tf_op jit(solution)/shard_map/ppermute | solution.py:342
  7.9 26.1 %collective-permute-start = (f32[1048,128]{1,0:T(8,128)}, f32[1048,128]{1,0:T(8,128)S(1)}, u32[]{:S(2)}, u32[]{:S(2)}) collective-permute-start(f32[1048,128]{1,0:T(8,128)} %get-tuple-element.29.own), channel_id=1, source_target_pairs={{0,16},{16,32},{32,48},{48,64},{64,80},{80,96},{96,112},{112,128},... | collective-permute-start | bytes 1609736 | tf_op jit(solution)/shard_map/ppermute | solution.py:342
  7.9 26.0 %all-to-all-start = ((f32[128,1,128]{2,1,0:T(1,128)}), f32[128,1,128]{2,1,0:T(1,128)S(1)}, u32[]{:S(2)}, u32[]{:S(2)}) async-start(f32[128,1,128]{2,1,0:T(1,128)} %bitcast.36), calls=%async_computation | async-start | bytes 131072 | tf_op jit(solution)/shard_map/all_to_all | solution.py:401
  22.8 7.9 %collective-permute-start.2 = (f32[216,128]{1,0:T(8,128)}, f32[216,128]{1,0:T(8,128)S(1)}, u32[]{:S(2)}, u32[]{:S(2)}) collective-permute-start(f32[216,128]{1,0:T(8,128)} %get-tuple-element.30), channel_id=1, source_target_pairs={{0,32},{16,48},{32,64},{48,80},{64,96},{80,112},{96,128},{112,144}... | collective-permute-start | bytes 331784 | tf_op jit(solution)/shard_map/ppermute | solution.py:342
  24.9 9.0 %collective-permute-start.3 = (f32[216,128]{1,0:T(8,128)}, f32[216,128]{1,0:T(8,128)S(1)}, u32[]{:S(2)}, u32[]{:S(2)}) collective-permute-start(f32[216,128]{1,0:T(8,128)} %get-tuple-element.31), channel_id=1, source_target_pairs={{0,224},{16,240},{32,0},{48,16},{64,32},{80,48},{96,64},{112,80},{... | collective-permute-start | bytes 331784 | tf_op jit(solution)/shard_map/ppermute | solution.py:342
  27.9 8.7 %collective-permute-start.4 = (f32[1048,128]{1,0:T(8,128)}, f32[1048,128]{1,0:T(8,128)S(1)}, u32[]{:S(2)}, u32[]{:S(2)}) collective-permute-start(f32[1048,128]{1,0:T(8,128)} %get-tuple-element.29.own), channel_id=1, source_target_pairs={{0,1},{1,0},{2,3},{3,2},{4,5},{5,4},{6,7},{7,6},{8,9},{9,8},{10,11... | collective-permute-start | bytes 1609736 | tf_op jit(solution)/shard_map/ppermute | solution.py:337
  33.9 4.7 %collective-permute-start.5 = (f32[1048,128]{1,0:T(8,128)S(1)}, f32[1048,128]{1,0:T(8,128)S(1)}, u32[]{:S(2)}, u32[]{:S(2)}) collective-permute-start(f32[1048,128]{1,0:T(8,128)S(1)} %collective-permute-done.m1), channel_id=1, source_target_pairs={{0,1},{1,0},{2,3},{3,2},{4,5},{5,4},{6,7},{7,6},{8,9},{9,8},{10,11... | collective-permute-start | bytes 1609736 | tf_op jit(solution)/shard_map/ppermute | solution.py:337
  36.0 2.6 %collective-permute-start.6 = (f32[1048,128]{1,0:T(8,128)S(1)}, f32[1048,128]{1,0:T(8,128)S(1)}, u32[]{:S(2)}, u32[]{:S(2)}) collective-permute-start(f32[1048,128]{1,0:T(8,128)S(1)} %collective-permute-done.1.p1), channel_id=1, source_target_pairs={{0,1},{1,0},{2,3},{3,2},{4,5},{5,4},{6,7},{7,6},{8,9},{9,8},{10,11... | collective-permute-start | bytes 1609736 | tf_op jit(solution)/shard_map/ppermute | solution.py:337
  36.1 2.4 %collective-permute-start.7 = (f32[216,128]{1,0:T(8,128)S(1)}, f32[216,128]{1,0:T(8,128)S(1)}, u32[]{:S(2)}, u32[]{:S(2)}) collective-permute-start(f32[216,128]{1,0:T(8,128)S(1)} %collective-permute-done.2.m2), channel_id=1, source_target_pairs={{0,1},{1,0},{2,3},{3,2},{4,5},{5,4},{6,7},{7,6},{8,9},{9,8},{10,11... | collective-permute-start | bytes 331784 | tf_op jit(solution)/shard_map/ppermute | solution.py:337
  36.5 2.1 %collective-permute-start.8 = (f32[216,128]{1,0:T(8,128)S(1)}, f32[216,128]{1,0:T(8,128)S(1)}, u32[]{:S(2)}, u32[]{:S(2)}) collective-permute-start(f32[216,128]{1,0:T(8,128)S(1)} %collective-permute-done.3.p2), channel_id=1, source_target_pairs={{0,1},{1,0},{2,3},{3,2},{4,5},{5,4},{6,7},{7,6},{8,9},{9,8},{10,11... | collective-permute-start | bytes 331784 | tf_op jit(solution)/shard_map/ppermute | solution.py:337
  38.6 1.0 copy-start.1
  39.7 2.1 %copy-start.2 = (s32[2,1,128,8]{2,3,1,0:T(8,128)S(1)}, s32[2,1,128,8]{2,3,1,0:T(8,128)}, u32[]{:S(2)}) copy-start(s32[2,1,128,8]{2,3,1,0:T(8,128)} %param.9) | copy-start | bytes 24580
  41.2 4.9 %collective-permute-start.9 = (f32[696,128]{1,0:T(8,128)S(1)}, f32[696,128]{1,0:T(8,128)S(1)}, u32[]{:S(2)}, u32[]{:S(2)}) collective-permute-start(f32[696,128]{1,0:T(8,128)S(1)} %get-tuple-element.40), channel_id=1, source_target_pairs={{0,1},{1,2},{2,3},{3,4},{4,5},{5,6},{6,7},{7,8},{8,9},{9,10},{10,1... | collective-permute-start | bytes 1069064 | tf_op jit(solution)/shard_map/ppermute | solution.py:342
  41.8 7.1 %collective-permute-start.10 = (f32[696,128]{1,0:T(8,128)S(1)}, f32[696,128]{1,0:T(8,128)S(1)}, u32[]{:S(2)}, u32[]{:S(2)}) collective-permute-start(f32[696,128]{1,0:T(8,128)S(1)} %get-tuple-element.41), channel_id=1, source_target_pairs={{0,15},{1,0},{2,1},{3,2},{4,3},{5,4},{6,5},{7,6},{8,7},{9,8},{10,9... | collective-permute-start | bytes 1069064 | tf_op jit(solution)/shard_map/ppermute | solution.py:342
  54.4 1.8 %collective-permute-start.11 = (f32[40,128]{1,0:T(8,128)S(1)}, f32[40,128]{1,0:T(8,128)S(1)}, u32[]{:S(2)}, u32[]{:S(2)}) collective-permute-start(f32[40,128]{1,0:T(8,128)S(1)} %get-tuple-element.46), channel_id=1, source_target_pairs={{0,1},{1,0},{2,3},{3,2},{4,5},{5,4},{6,7},{7,6},{8,9},{9,8},{10,11... | collective-permute-start | bytes 61448 | tf_op jit(solution)/shard_map/ppermute | solution.py:337
  101.5 29.5 %copy-start = (f32[2,64,8,128]{3,2,1,0:T(8,128)S(1)}, f32[2,64,8,128]{3,2,1,0:T(8,128)}, u32[]{:S(2)}) copy-start(f32[2,64,8,128]{3,2,1,0:T(8,128)} %param.6) | copy-start | bytes 1572868
  101.5 1.3 collective-permute-start.12

commit v3 on v0

--- a/solution.py
+++ b/solution.py
@@ -60,7 +60,7 @@
     for copy in copies[:2]:
         copy.wait()
     lines = [values[...], precision[...], jnp.zeros((96, MEMBERS), F32)]
-    obs[...] = jnp.concatenate(lines, axis=0).T[:, :32]
+    obs[...] = jnp.concatenate(lines, axis=0).T
     for copy in copies[2:]:
         copy.wait()
     for k, (f, up_row, down_row) in enumerate(((1, 6, 0), (1, 7, 1), (0, 7, 0))):
@@ -121,7 +121,7 @@
 
 
 def scatter_obs(pos, slots, received, weights, observed):
-    received = jnp.concatenate([received[...], jnp.zeros((MEMBERS, 96), F32)], axis=1).T
+    received = received[...].T
     values, precision = received[:16], received[16:32]
     lines = ROWS * HALF
     k = iota((lines, MEMBERS), 0)
@@ -315,8 +315,9 @@
     k = weights_of(pos, mine[...], other[...])
     k1[...] = k
     for src, out in ((fr, FR), (fo, FO)):
-        new = jnp.dot(src[...].reshape(EXT * WIDE, MEMBERS), k, precision=HIGHEST, preferred_element_type=F32)
-        out[...] = new.reshape(EXT, WIDE, MEMBERS)
+        old = src[:, 8:104].reshape(EXT * 96, MEMBERS)
+        new = jnp.dot(old, k, precision=HIGHEST, preferred_element_type=F32)
+        out[:, 8:104] = new.reshape(EXT, 96, MEMBERS)
     forward(pos[0], table[...], FR, FO, H, U, V)
     gram(pos, H, weights[1], observed[1], keep, send)
 
@@ -390,7 +391,7 @@
     two_far = shape(3 * HALF + INIT, COLS)
     own, up2, dn2, obs = pl.pallas_call(
         collect,
-        out_shape=[shape(OWN + INIT, COLS), two_far, two_far, shape(128, 32)],
+        out_shape=[shape(OWN + INIT, COLS), two_far, two_far, shape(128, 128)],
         in_specs=[pl.BlockSpec(memory_space=pl.ANY)] * 5,
         out_specs=[VMEM] * 4,
         scratch_shapes=[pltpu.VMEM((16, COLS), F32)] * 2 + [pltpu.SemaphoreType.DMA((5,))],

time: 132 us -> 132 us (level)
  waiting for transfers between devices: 19.4 us -> 14.9 us
  blocking collectives: 45.1 us -> 49.3 us
    all_to_all x1, waiting for transfers between devices: 8.37 us -> 0.01 us  [per_device(): obs = lax.all_to_all(obs, LAT_LON, 0, 0, tiled=True)]
    all_to_all x4, blocking collectives: 45.1 us -> 49.3 us  [reduced(): lax.all_to_all(summed(lax.axis_size(axes), *parts), axes, 0, 0, tiled=True)]
    ppermute x6, waiting for transfers between devices: 5.65 us -> 9.54 us  [moved(): return lax.ppermute(value, axes, [(i, (i + by) % n) for i in range(n)])]
    all_to_all x1, starting transfers between devices: 12.8 us -> 14.9 us  [per_device(): obs = lax.all_to_all(obs, LAT_LON, 0, 0, tiled=True)]
    ppermute x9, starting transfers between devices: 14.5 us -> 13.1 us  [swap(): return lax.ppermute(value, 'ens', [(0, 1), (1, 0)])]
  transfers between devices with their start and end apart: 16 -> 16, of which waited for: 9 -> 10; matrix products, arithmetic and copies ran while one was open for 0% -> 0% of each run, Pallas kernels for 1% -> 1%
where the time goes in v3:
time: 132 us
  blocking collectives  49.3 us (37%)
  starting transfers between devices  39.6 us (30%)
  Pallas kernels  27 us (20%)
  waiting for transfers between devices  14.9 us (11%)
    all_to_all x4, blocking collectives, reduced(): lax.all_to_all(summed(lax.axis_size(axes), *parts), axes, 0, 0, tiled=True)  49.3 us
    pallas_call x5, Pallas kernels, call(): pl.pallas_call(kernel, out_shape=out_shape, in_specs=[SMEM] + [VMEM] * le...  24.8 us
    all_to_all x1, starting transfers between devices, per_device(): obs = lax.all_to_all(obs, LAT_LON, 0, 0, tiled=True)  14.9 us
    ppermute x9, starting transfers between devices, swap(): return lax.ppermute(value, 'ens', [(0, 1), (1, 0)])  13.1 us
    ppermute x6, starting transfers between devices, moved(): return lax.ppermute(value, axes, [(i, (i + by) % n) for i in range(n)])  11.5 us
    ppermute x6, waiting for transfers between devices, moved(): return lax.ppermute(value, axes, [(i, (i + by) % n) for i in range(n)])  9.54 us
    ppermute x9, waiting for transfers between devices, swap(): return lax.ppermute(value, 'ens', [(0, 1), (1, 0)])  5.34 us
  transfers between devices with their start and end apart: 16, of which 10 were waited for; matrix products, arithmetic and copies ran while one was open for 0% of the time, Pallas kernels for 1%

profile of v3, /device:TPU:1, one launch (start us, length us, event | category | flops | bytes accessed | tf_op | source)
XLA Modules:
  0.0 132.0 jit_solution(13083293468912380463)
XLA Ops:
  0.0 2.0 %shard_map.64 = (f32[1048,128]{1,0:T(8,128)}, f32[216,128]{1,0:T(8,128)}, f32[216,128]{1,0:T(8,128)}, f32[128,128]{1,0:T(8,128)}) custom-call(f32[1024,128]{1,0:T(8,128)} %bitcast.30, f32[8,128]{1,0:T(8,128)} %height_hbm.1, f32[16,128]{1,0:T(8,128)} %bitcast.43, f32[16,128]{1,0:T(8,128)} %bitcast.44, f32[16,128]{1,0:T(8,128)} %bitcast.45), custom_call_target="tpu_custom_call" | custom-call | tf_op jit(solution)/shard_map/pallas_call | solution.py:392
  2.0 5.8 %collective-permute-start.1 = (f32[1048,128]{1,0:T(8,128)}, f32[1048,128]{1,0:T(8,128)S(1)}, u32[]{:S(2)}, u32[]{:S(2)}) collective-permute-start(f32[1048,128]{1,0:T(8,128)} %get-tuple-element.29.own), channel_id=1, source_target_pairs={{0,240},{16,0},{32,16},{48,32},{64,48},{80,64},{96,80},{112,96},{1... | collective-permute-start | bytes 1609736 | tf_op jit(solution)/shard_map/ppermute | solution.py:342
  7.9 14.9 %all-to-all-start = ((f32[128,1,128]{2,1,0:T(1,128)}), f32[128,1,128]{2,1,0:T(1,128)S(1)}, u32[]{:S(2)}, u32[]{:S(2)}) async-start(f32[128,1,128]{2,1,0:T(1,128)} %bitcast.42), calls=%async_computation | async-start | bytes 131072 | tf_op jit(solution)/shard_map/all_to_all | solution.py:402
  22.8 2.2 %collective-permute-start.2 = (f32[216,128]{1,0:T(8,128)}, f32[216,128]{1,0:T(8,128)S(1)}, u32[]{:S(2)}, u32[]{:S(2)}) collective-permute-start(f32[216,128]{1,0:T(8,128)} %get-tuple-element.30), channel_id=1, source_target_pairs={{0,32},{16,48},{32,64},{48,80},{64,96},{80,112},{96,128},{112,144}... | collective-permute-start | bytes 331784 | tf_op jit(solution)/shard_map/ppermute | solution.py:342
  24.9 3.0 %collective-permute-start.3 = (f32[216,128]{1,0:T(8,128)}, f32[216,128]{1,0:T(8,128)S(1)}, u32[]{:S(2)}, u32[]{:S(2)}) collective-permute-start(f32[216,128]{1,0:T(8,128)} %get-tuple-element.31), channel_id=1, source_target_pairs={{0,224},{16,240},{32,0},{48,16},{64,32},{80,48},{96,64},{112,80},{... | collective-permute-start | bytes 331784 | tf_op jit(solution)/shard_map/ppermute | solution.py:342
  27.9 2.1 %collective-permute-start.4 = (f32[1048,128]{1,0:T(8,128)}, f32[1048,128]{1,0:T(8,128)S(1)}, u32[]{:S(2)}, u32[]{:S(2)}) collective-permute-start(f32[1048,128]{1,0:T(8,128)} %get-tuple-element.29.own), channel_id=1, source_target_pairs={{0,1},{1,0},{2,3},{3,2},{4,5},{5,4},{6,7},{7,6},{8,9},{9,8},{10,11... | collective-permute-start | bytes 1609736 | tf_op jit(solution)/shard_map/ppermute | solution.py:337
  30.7 3.2 %collective-permute-done.3.p2 = f32[216,128]{1,0:T(8,128)S(1)} collective-permute-done((f32[216,128]{1,0:T(8,128)}, f32[216,128]{1,0:T(8,128)S(1)}, u32[]{:S(2)}, u32[]{:S(2)}) %collective-permute-start.3) | collective-permute-done | bytes 110624 | tf_op jit(solution)/shard_map/ppermute | solution.py:342
  33.9 2.1 %collective-permute-start.5 = (f32[1048,128]{1,0:T(8,128)S(1)}, f32[1048,128]{1,0:T(8,128)S(1)}, u32[]{:S(2)}, u32[]{:S(2)}) collective-permute-start(f32[1048,128]{1,0:T(8,128)S(1)} %collective-permute-done.m1), channel_id=1, source_target_pairs={{0,1},{1,0},{2,3},{3,2},{4,5},{5,4},{6,7},{7,6},{8,9},{9,8},{10,11... | collective-permute-start | bytes 1609736 | tf_op jit(solution)/shard_map/ppermute | solution.py:337
  36.7 1.8 %collective-permute-done.7.m2_o = f32[216,128]{1,0:T(8,128)S(1)} collective-permute-done((f32[216,128]{1,0:T(8,128)S(1)}, f32[216,128]{1,0:T(8,128)S(1)}, u32[]{:S(2)}, u32[]{:S(2)}) %collective-permute-start.7) | collective-permute-done | bytes 110624 | tf_op jit(solution)/shard_map/ppermute | solution.py:337
  38.7 1.0 copy-done.1
  39.7 1.5 %shard_map.65 = (f32[28,112,128]{2,1,0:T(8,128)S(1)}, f32[28,112,128]{2,1,0:T(8,128)S(1)}, f32[120,128]{1,0:T(8,128)S(1)}, f32[696,128]{1,0:T(8,128)S(1)}, f32[696,128]{1,0:T(8,128)S(1)}) custom-call(s32[2]{0:T(128)S(1)} %pad_add_fusion.pos, f32[1048,128]{1,0:T(8,128)S(1)} %copy-done.1, f32[1048,128]{1,0:T(8,128)S(1)} %collective-permute-done.m1, ...), custom_call_target="tpu_custom_call" | custom-call | tf_op jit(solution)/shard_map/pallas_call | solution.py:374
  41.8 1.5 %shard_map.66 = (f32[2,512,128]{2,1,0:T(8,128)S(1)}, f32[2,512,128]{2,1,0:T(8,128)S(1)}) custom-call(s32[2]{0:T(128)S(1)} %pad_add_fusion.pos, s32[16,128]{1,0:T(8,128)S(1)} %bitcast.41, f32[128,128]{1,0:T(8,128)S(1)} %bitcast.32), custom_call_target="tpu_custom_call" | custom-call | tf_op jit(solution)/shard_map/pallas_call | solution.py:374
  43.2 2.9 %collective-permute-done.9.lz = f32[696,128]{1,0:T(8,128)S(1)} collective-permute-done((f32[696,128]{1,0:T(8,128)S(1)}, f32[696,128]{1,0:T(8,128)S(1)}, u32[]{:S(2)}, u32[]{:S(2)}) %collective-permute-start.9) | collective-permute-done | bytes 356384 | tf_op jit(solution)/shard_map/ppermute | solution.py:342
  46.1 2.8 %collective-permute-done.10.rz = f32[696,128]{1,0:T(8,128)S(1)} collective-permute-done((f32[696,128]{1,0:T(8,128)S(1)}, f32[696,128]{1,0:T(8,128)S(1)}, u32[]{:S(2)}, u32[]{:S(2)}) %collective-permute-start.10) | collective-permute-done | bytes 356384 | tf_op jit(solution)/shard_map/ppermute | solution.py:342
  48.9 5.2 %shard_map.67 = (f32[28,112,128]{2,1,0:T(8,128)S(1)}, f32[28,112,128]{2,1,0:T(8,128)S(1)}, f32[128,128]{1,0:T(8,128)S(1)}, f32[40,128]{1,0:T(8,128)S(1)}, f32[40,128]{1,0:T(8,128)S(1)}) custom-call(s32[2]{0:T(128)S(1)} %pad_add_fusion.pos, f32[28,112,128]{2,1,0:T(8,128)S(1)} %get-tuple-element.37.fr, ...), custom_call_target="tpu_custom_call", output_to_operand_aliasing={{0}: (1, {}), {1}: (2, {})} | custom-call | tf_op jit(solution)/shard_map/pallas_call | solution.py:374
  54.1 1.1 collective-permute-start.11
  56.0 12.5 %all_to_all.32.refs_0_ = f32[16,40,128]{2,1,0:T(8,128)S(1)} all-to-all(f32[16,40,128]{2,1,0:T(8,128)S(1)} %shard_map.68), channel_id=1, replica_groups=mesh['lat_0'=4,'lat_1'=4,'lon'=8,'ens'=2] {'lat_0','lat_1'}, dimensions={0} | all-to-all | bytes 655360 | tf_op jit(solution)/shard_map/all_to_all | solution.py:368
  68.5 14.9 %all_to_all.33.refs_0_ = f32[8,40,128]{2,1,0:T(8,128)S(1)} all-to-all(f32[8,40,128]{2,1,0:T(8,128)S(1)} %shard_map.69), channel_id=1, replica_groups=mesh['lat_0'=4,'lat_1'=4,'lon'=8,'ens'=2] {'lon'}, dimensions={0} | all-to-all | bytes 327680 | tf_op jit(solution)/shard_map/all_to_all | solution.py:368
  83.4 3.4 %collective-permute-start.12 = (f32[40,128]{1,0:T(8,128)S(1)}, f32[40,128]{1,0:T(8,128)S(1)}, u32[]{:S(2)}, u32[]{:S(2)}) collective-permute-start(f32[40,128]{1,0:T(8,128)S(1)} %bitcast.33), channel_id=1, source_target_pairs={{0,1},{1,0},{2,3},{3,2},{4,5},{5,4},{6,7},{7,6},{8,9},{9,8},{10,11... | collective-permute-start | bytes 61448 | tf_op jit(solution)/shard_map/ppermute | solution.py:337
  87.6 10.4 %shard_map.71 = (f32[128,128]{1,0:T(8,128)S(1)}, f32[40,128]{1,0:T(8,128)S(1)}, f32[40,128]{1,0:T(8,128)S(1)}) custom-call(s32[2]{0:T(128)S(1)} %pad_add_fusion.pos, f32[40,128]{1,0:T(8,128)S(1)} %bitcast.34, f32[40,128]{1,0:T(8,128)S(1)} %collective-permute-done.12.other, f32[28,112,128]{2,1,0:T(8,128)S(1)} %get-tuple-element.47.fr, ...), custom_call_target="tpu_custom_call" | custom-call | tf_op jit(solution)/shard_map/pallas_call | solution.py:374
  99.4 11.2 %all_to_all.34.refs_0_ = f32[16,40,128]{2,1,0:T(8,128)S(1)} all-to-all(f32[16,40,128]{2,1,0:T(8,128)S(1)} %shard_map.72), channel_id=1, replica_groups=mesh['lat_0'=4,'lat_1'=4,'lon'=8,'ens'=2] {'lat_0','lat_1'}, dimensions={0} | all-to-all | bytes 655360 | tf_op jit(solution)/shard_map/all_to_all | solution.py:368
  110.6 10.8 %all_to_all.35.refs_0_ = f32[8,40,128]{2,1,0:T(8,128)S(1)} all-to-all(f32[8,40,128]{2,1,0:T(8,128)S(1)} %shard_map.73), channel_id=1, replica_groups=mesh['lat_0'=4,'lat_1'=4,'lon'=8,'ens'=2] {'lon'}, dimensions={0} | all-to-all | bytes 327680 | tf_op jit(solution)/shard_map/all_to_all | solution.py:368
  121.4 3.5 %collective-permute-start.14 = (f32[40,128]{1,0:T(8,128)S(1)}, f32[40,128]{1,0:T(8,128)S(1)}, u32[]{:S(2)}, u32[]{:S(2)}) collective-permute-start(f32[40,128]{1,0:T(8,128)S(1)} %bitcast.35), channel_id=1, source_target_pairs={{0,1},{1,0},{2,3},{3,2},{4,5},{5,4},{6,7},{7,6},{8,9},{9,8},{10,11... | collective-permute-start | bytes 61448 | tf_op jit(solution)/shard_map/ppermute | solution.py:337
  125.7 6.2 %shard_map.75 = f32[1024,128]{1,0:T(8,128)} custom-call(s32[2]{0:T(128)S(1)} %pad_add_fusion.pos, f32[40,128]{1,0:T(8,128)S(1)} %bitcast.36, f32[40,128]{1,0:T(8,128)S(1)} %collective-permute-done.14.other, f32[128,128]{1,0:T(8,128)S(1)} %get-tuple-element.52.k1, f32[1024,128]{1,0:T(8,128)S(1)} %bitcast.31, f32[1048,128]{1,0:T(8,128)S(1)} %collective-permute-done.4.own_o.other_p), custom_call_target="tpu_custom_call" | custom-call | tf_op jit(solution)/shard_map/pallas_call | solution.py:374
  (31 shorter events, 6.0 us)
Async XLA Ops:
  2.0 31.9 %collective-permute-start.1 = (f32[1048,128]{1,0:T(8,128)}, f32[1048,128]{1,0:T(8,128)S(1)}, u32[]{:S(2)}, u32[]{:S(2)}) collective-permute-start(f32[1048,128]{1,0:T(8,128)} %get-tuple-element.29.own), channel_id=1, source_target_pairs={{0,240},{16,0},{32,16},{48,32},{64,48},{80,64},{96,80},{112,96},{1... | collective-permute-start | bytes 1609736 | tf_op jit(solution)/shard_map/ppermute | solution.py:342
  7.9 26.1 %collective-permute-start = (f32[1048,128]{1,0:T(8,128)}, f32[1048,128]{1,0:T(8,128)S(1)}, u32[]{:S(2)}, u32[]{:S(2)}) collective-permute-start(f32[1048,128]{1,0:T(8,128)} %get-tuple-element.29.own), channel_id=1, source_target_pairs={{0,16},{16,32},{32,48},{48,64},{64,80},{80,96},{96,112},{112,128},... | collective-permute-start | bytes 1609736 | tf_op jit(solution)/shard_map/ppermute | solution.py:342
  7.9 26.1 %all-to-all-start = ((f32[128,1,128]{2,1,0:T(1,128)}), f32[128,1,128]{2,1,0:T(1,128)S(1)}, u32[]{:S(2)}, u32[]{:S(2)}) async-start(f32[128,1,128]{2,1,0:T(1,128)} %bitcast.42), calls=%async_computation | async-start | bytes 131072 | tf_op jit(solution)/shard_map/all_to_all | solution.py:402
  22.8 7.9 %collective-permute-start.2 = (f32[216,128]{1,0:T(8,128)}, f32[216,128]{1,0:T(8,128)S(1)}, u32[]{:S(2)}, u32[]{:S(2)}) collective-permute-start(f32[216,128]{1,0:T(8,128)} %get-tuple-element.30), channel_id=1, source_target_pairs={{0,32},{16,48},{32,64},{48,80},{64,96},{80,112},{96,128},{112,144}... | collective-permute-start | bytes 331784 | tf_op jit(solution)/shard_map/ppermute | solution.py:342
  24.9 9.0 %collective-permute-start.3 = (f32[216,128]{1,0:T(8,128)}, f32[216,128]{1,0:T(8,128)S(1)}, u32[]{:S(2)}, u32[]{:S(2)}) collective-permute-start(f32[216,128]{1,0:T(8,128)} %get-tuple-element.31), channel_id=1, source_target_pairs={{0,224},{16,240},{32,0},{48,16},{64,32},{80,48},{96,64},{112,80},{... | collective-permute-start | bytes 331784 | tf_op jit(solution)/shard_map/ppermute | solution.py:342
  27.9 8.8 %collective-permute-start.4 = (f32[1048,128]{1,0:T(8,128)}, f32[1048,128]{1,0:T(8,128)S(1)}, u32[]{:S(2)}, u32[]{:S(2)}) collective-permute-start(f32[1048,128]{1,0:T(8,128)} %get-tuple-element.29.own), channel_id=1, source_target_pairs={{0,1},{1,0},{2,3},{3,2},{4,5},{5,4},{6,7},{7,6},{8,9},{9,8},{10,11... | collective-permute-start | bytes 1609736 | tf_op jit(solution)/shard_map/ppermute | solution.py:337
  33.9 4.7 %collective-permute-start.5 = (f32[1048,128]{1,0:T(8,128)S(1)}, f32[1048,128]{1,0:T(8,128)S(1)}, u32[]{:S(2)}, u32[]{:S(2)}) collective-permute-start(f32[1048,128]{1,0:T(8,128)S(1)} %collective-permute-done.m1), channel_id=1, source_target_pairs={{0,1},{1,0},{2,3},{3,2},{4,5},{5,4},{6,7},{7,6},{8,9},{9,8},{10,11... | collective-permute-start | bytes 1609736 | tf_op jit(solution)/shard_map/ppermute | solution.py:337
  36.0 2.6 %collective-permute-start.6 = (f32[1048,128]{1,0:T(8,128)S(1)}, f32[1048,128]{1,0:T(8,128)S(1)}, u32[]{:S(2)}, u32[]{:S(2)}) collective-permute-start(f32[1048,128]{1,0:T(8,128)S(1)} %collective-permute-done.1.p1), channel_id=1, source_target_pairs={{0,1},{1,0},{2,3},{3,2},{4,5},{5,4},{6,7},{7,6},{8,9},{9,8},{10,11... | collective-permute-start | bytes 1609736 | tf_op jit(solution)/shard_map/ppermute | solution.py:337
  36.1 2.4 %collective-permute-start.7 = (f32[216,128]{1,0:T(8,128)S(1)}, f32[216,128]{1,0:T(8,128)S(1)}, u32[]{:S(2)}, u32[]{:S(2)}) collective-permute-start(f32[216,128]{1,0:T(8,128)S(1)} %collective-permute-done.2.m2), channel_id=1, source_target_pairs={{0,1},{1,0},{2,3},{3,2},{4,5},{5,4},{6,7},{7,6},{8,9},{9,8},{10,11... | collective-permute-start | bytes 331784 | tf_op jit(solution)/shard_map/ppermute | solution.py:337
  36.5 2.1 %collective-permute-start.8 = (f32[216,128]{1,0:T(8,128)S(1)}, f32[216,128]{1,0:T(8,128)S(1)}, u32[]{:S(2)}, u32[]{:S(2)}) collective-permute-start(f32[216,128]{1,0:T(8,128)S(1)} %collective-permute-done.3.p2), channel_id=1, source_target_pairs={{0,1},{1,0},{2,3},{3,2},{4,5},{5,4},{6,7},{7,6},{8,9},{9,8},{10,11... | collective-permute-start | bytes 331784 | tf_op jit(solution)/shard_map/ppermute | solution.py:337
  38.7 1.0 copy-start.1
  39.7 2.1 %copy-start.2 = (s32[2,1,128,8]{2,3,1,0:T(8,128)S(1)}, s32[2,1,128,8]{2,3,1,0:T(8,128)}, u32[]{:S(2)}) copy-start(s32[2,1,128,8]{2,3,1,0:T(8,128)} %param.9) | copy-start | bytes 24580
  41.2 4.8 %collective-permute-start.9 = (f32[696,128]{1,0:T(8,128)S(1)}, f32[696,128]{1,0:T(8,128)S(1)}, u32[]{:S(2)}, u32[]{:S(2)}) collective-permute-start(f32[696,128]{1,0:T(8,128)S(1)} %get-tuple-element.40), channel_id=1, source_target_pairs={{0,1},{1,2},{2,3},{3,4},{4,5},{5,6},{6,7},{7,8},{8,9},{9,10},{10,1... | collective-permute-start | bytes 1069064 | tf_op jit(solution)/shard_map/ppermute | solution.py:342
  41.8 7.1 %collective-permute-start.10 = (f32[696,128]{1,0:T(8,128)S(1)}, f32[696,128]{1,0:T(8,128)S(1)}, u32[]{:S(2)}, u32[]{:S(2)}) collective-permute-start(f32[696,128]{1,0:T(8,128)S(1)} %get-tuple-element.41), channel_id=1, source_target_pairs={{0,15},{1,0},{2,1},{3,2},{4,3},{5,4},{6,5},{7,6},{8,7},{9,8},{10,9... | collective-permute-start | bytes 1069064 | tf_op jit(solution)/shard_map/ppermute | solution.py:342
  54.1 1.9 %collective-permute-start.11 = (f32[40,128]{1,0:T(8,128)S(1)}, f32[40,128]{1,0:T(8,128)S(1)}, u32[]{:S(2)}, u32[]{:S(2)}) collective-permute-start(f32[40,128]{1,0:T(8,128)S(1)} %get-tuple-element.46), channel_id=1, source_target_pairs={{0,1},{1,0},{2,3},{3,2},{4,5},{5,4},{6,7},{7,6},{8,9},{9,8},{10,11... | collective-permute-start | bytes 61448 | tf_op jit(solution)/shard_map/ppermute | solution.py:337
  83.4 4.2 %collective-permute-start.12 = (f32[40,128]{1,0:T(8,128)S(1)}, f32[40,128]{1,0:T(8,128)S(1)}, u32[]{:S(2)}, u32[]{:S(2)}) collective-permute-start(f32[40,128]{1,0:T(8,128)S(1)} %bitcast.33), channel_id=1, source_target_pairs={{0,1},{1,0},{2,3},{3,2},{4,5},{5,4},{6,7},{7,6},{8,9},{9,8},{10,11... | collective-permute-start | bytes 61448 | tf_op jit(solution)/shard_map/ppermute | solution.py:337
  98.1 27.6 %copy-start = (f32[2,64,8,128]{3,2,1,0:T(8,128)S(1)}, f32[2,64,8,128]{3,2,1,0:T(8,128)}, u32[]{:S(2)}) copy-start(f32[2,64,8,128]{3,2,1,0:T(8,128)} %param.6) | copy-start | bytes 1572868
  98.1 1.3 collective-permute-start.13
  121.4 4.4 %collective-permute-start.14 = (f32[40,128]{1,0:T(8,128)S(1)}, f32[40,128]{1,0:T(8,128)S(1)}, u32[]{:S(2)}, u32[]{:S(2)}) collective-permute-start(f32[40,128]{1,0:T(8,128)S(1)} %bitcast.35), channel_id=1, source_target_pairs={{0,1},{1,0},{2,3},{3,2},{4,5},{5,4},{6,7},{7,6},{8,9},{9,8},{10,11... | collective-permute-start | bytes 61448 | tf_op jit(solution)/shard_map/ppermute | solution.py:337

commit v4 on v3

--- a/solution.py
+++ b/solution.py
@@ -75,14 +75,13 @@
     rows = []
     for field, first in ((1, 0), (0, 1)):
         for r in range(first, EXT - first):
-            away = max(10 - r, r - 17, 0)
-            need = 9 + field - away
-            rows.append((field, r, 16 if need > 8 else 8))
+            rows.append((field, r, 9 + field - max(10 - r, r - 17, 0)))
     return rows
 
 
 EDGE_ROWS = edge_rows()
-EDGE = sum(n for _, _, n in EDGE_ROWS)
+EDGE = (sum(n for _, _, n in EDGE_ROWS) + 7) // 8 * 8
+NEAR = 16
 
 
 def both_cores(first, mine, others, start, stride):
@@ -109,15 +108,25 @@
         if field == 1 and not 10 <= r < 18:
             turned = jnp.where(inside(pos[0], r), turned, 0.0)
         (FO if field else FR)[r, LEFT:RIGHT] = turned
-        right[at : at + n] = turned[HALF - n :]
-        left[at : at + n] = turned[:n]
+        if n:
+            right[at : at + n] = turned[HALF - n :]
+            left[at : at + n] = turned[:n]
         at += n
 
     fields = ((m2, 3 * HALF), (m1, OWN), (own, OWN), (p1, OWN), (p2, 3 * HALF))
+    slot = iota((ROWS, COLS), 1) // NEAR
+    packed = [[jnp.zeros((ROWS, COLS), F32)] * 2, [jnp.zeros((ROWS, COLS), F32)] * 2]
     for k, (ref, start) in enumerate(fields):
-        tile = ref[start : start + INIT]
-        for out, at in ((tiles, 0), (right, EDGE), (left, EDGE)):
-            out[at + k * INIT : at + (k + 1) * INIT] = tile
+        for f in range(3):
+            j = 3 * k + f
+            tile = ref[start + f * ROWS : start + (f + 1) * ROWS]
+            tiles[j * ROWS : (j + 1) * ROWS] = tile
+            for side, first_lane in ((0, COLS - NEAR), (1, 0)):
+                there = pltpu.roll(tile, (NEAR * (j % 8) - first_lane) % COLS, 1)
+                packed[side][j // 8] = jnp.where(slot == j % 8, there, packed[side][j // 8])
+    for side, out in ((0, right), (1, left)):
+        out[EDGE : EDGE + ROWS] = packed[side][0]
+        out[EDGE + ROWS : EDGE + 2 * ROWS] = packed[side][1]
 
 
 def scatter_obs(pos, slots, received, weights, observed):
@@ -152,9 +161,10 @@
         for f in range(3):
             at = k * INIT + f * ROWS
             own = tiles[at : at + ROWS]
-            at += EDGE
-            before = lz[at : at + ROWS]
-            after = rz[at : at + ROWS]
+            j = 3 * k + f
+            at = EDGE + j // 8 * ROWS
+            before = pltpu.roll(lz[at : at + ROWS], (COLS - NEAR - NEAR * (j % 8)) % COLS, 1)
+            after = pltpu.roll(rz[at : at + ROWS], -NEAR * (j % 8) % COLS, 1)
             low = pltpu.roll(jnp.where(lane >= 112, before, own), 16, 1)
             high = pltpu.roll(jnp.where(lane < 16, after, own), 80, 1)
             window = jnp.where(e == 0, low, high)
@@ -248,8 +258,9 @@
     at = 0
     for field, r, n in EDGE_ROWS:
         out = FO if field else FR
-        out[r, LEFT - n : LEFT] = lz[at : at + n]
-        out[r, RIGHT : RIGHT + n] = rz[at : at + n]
+        if n:
+            out[r, LEFT - n : LEFT] = lz[at : at + n]
+            out[r, RIGHT : RIGHT + n] = rz[at : at + n]
         at += n
     table[...] = initial_table(pos, tiles, lz, rz)
     forward(pos[0], table[...], FR, FO, H, U, V)
@@ -408,7 +419,7 @@
     field = shape(EXT, WIDE, MEMBERS)
     half = shape(40, MEMBERS)
     square = shape(MEMBERS, MEMBERS)
-    edge = shape(EDGE + 5 * INIT, MEMBERS)
+    edge = shape(EDGE + 2 * ROWS, MEMBERS)
     ext_fr, ext_fo, tiles, right, left = call(
         turn_rows, [field, field, shape(5 * INIT, COLS), edge, edge], pos, *blocks, *others
     )

time: 132 us -> 130 us (0.985)
  waiting for transfers between devices: 14.9 us -> 12.9 us
    ppermute x6, waiting for transfers between devices: 9.54 us -> 7.57 us  [moved(): return lax.ppermute(value, axes, [(i, (i + by) % n) for i in range(n)])]
where the time goes in v4:
time: 130 us
  blocking collectives  49.3 us (38%)
  starting transfers between devices  39.6 us (30%)
  Pallas kernels  27 us (21%)
  waiting for transfers between devices  12.9 us (10%)
    all_to_all x4, blocking collectives, reduced(): lax.all_to_all(summed(lax.axis_size(axes), *parts), axes, 0, 0, tiled=True)  49.3 us
    pallas_call x5, Pallas kernels, call(): pl.pallas_call(kernel, out_shape=out_shape, in_specs=[SMEM] + [VMEM] * le...  24.9 us
    all_to_all x1, starting transfers between devices, per_device(): obs = lax.all_to_all(obs, LAT_LON, 0, 0, tiled=True)  14.9 us
    ppermute x9, starting transfers between devices, swap(): return lax.ppermute(value, 'ens', [(0, 1), (1, 0)])  13.1 us
    ppermute x6, starting transfers between devices, moved(): return lax.ppermute(value, axes, [(i, (i + by) % n) for i in range(n)])  11.5 us
    ppermute x6, waiting for transfers between devices, moved(): return lax.ppermute(value, axes, [(i, (i + by) % n) for i in range(n)])  7.57 us
    ppermute x9, waiting for transfers between devices, swap(): return lax.ppermute(value, 'ens', [(0, 1), (1, 0)])  5.34 us
  transfers between devices with their start and end apart: 16, of which 10 were waited for; matrix products, arithmetic and copies ran while one was open for 0% of the time, Pallas kernels for 1%

profile of v4, /device:TPU:1, one launch (start us, length us, event | category | flops | bytes accessed | tf_op | source)
XLA Modules:
  0.0 130.0 jit_solution(3772011012306126734)
XLA Ops:
  0.0 2.0 %shard_map.64 = (f32[1048,128]{1,0:T(8,128)}, f32[216,128]{1,0:T(8,128)}, f32[216,128]{1,0:T(8,128)}, f32[128,128]{1,0:T(8,128)}) custom-call(f32[1024,128]{1,0:T(8,128)} %bitcast.30, f32[8,128]{1,0:T(8,128)} %height_hbm.1, f32[16,128]{1,0:T(8,128)} %bitcast.43, f32[16,128]{1,0:T(8,128)} %bitcast.44, f32[16,128]{1,0:T(8,128)} %bitcast.45), custom_call_target="tpu_custom_call" | custom-call | tf_op jit(solution)/shard_map/pallas_call | solution.py:403
  2.0 5.8 %collective-permute-start.1 = (f32[1048,128]{1,0:T(8,128)}, f32[1048,128]{1,0:T(8,128)S(1)}, u32[]{:S(2)}, u32[]{:S(2)}) collective-permute-start(f32[1048,128]{1,0:T(8,128)} %get-tuple-element.29.own), channel_id=1, source_target_pairs={{0,240},{16,0},{32,16},{48,32},{64,48},{80,64},{96,80},{112,96},{1... | collective-permute-start | bytes 1609736 | tf_op jit(solution)/shard_map/ppermute | solution.py:353
  7.9 14.9 %all-to-all-start = ((f32[128,1,128]{2,1,0:T(1,128)}), f32[128,1,128]{2,1,0:T(1,128)S(1)}, u32[]{:S(2)}, u32[]{:S(2)}) async-start(f32[128,1,128]{2,1,0:T(1,128)} %bitcast.42), calls=%async_computation | async-start | bytes 131072 | tf_op jit(solution)/shard_map/all_to_all | solution.py:413
  22.8 2.2 %collective-permute-start.2 = (f32[216,128]{1,0:T(8,128)}, f32[216,128]{1,0:T(8,128)S(1)}, u32[]{:S(2)}, u32[]{:S(2)}) collective-permute-start(f32[216,128]{1,0:T(8,128)} %get-tuple-element.30), channel_id=1, source_target_pairs={{0,32},{16,48},{32,64},{48,80},{64,96},{80,112},{96,128},{112,144}... | collective-permute-start | bytes 331784 | tf_op jit(solution)/shard_map/ppermute | solution.py:353
  24.9 3.0 %collective-permute-start.3 = (f32[216,128]{1,0:T(8,128)}, f32[216,128]{1,0:T(8,128)S(1)}, u32[]{:S(2)}, u32[]{:S(2)}) collective-permute-start(f32[216,128]{1,0:T(8,128)} %get-tuple-element.31), channel_id=1, source_target_pairs={{0,224},{16,240},{32,0},{48,16},{64,32},{80,48},{96,64},{112,80},{... | collective-permute-start | bytes 331784 | tf_op jit(solution)/shard_map/ppermute | solution.py:353
  27.9 2.1 %collective-permute-start.4 = (f32[1048,128]{1,0:T(8,128)}, f32[1048,128]{1,0:T(8,128)S(1)}, u32[]{:S(2)}, u32[]{:S(2)}) collective-permute-start(f32[1048,128]{1,0:T(8,128)} %get-tuple-element.29.own), channel_id=1, source_target_pairs={{0,1},{1,0},{2,3},{3,2},{4,5},{5,4},{6,7},{7,6},{8,9},{9,8},{10,11... | collective-permute-start | bytes 1609736 | tf_op jit(solution)/shard_map/ppermute | solution.py:348
  30.7 3.2 %collective-permute-done.3.p2 = f32[216,128]{1,0:T(8,128)S(1)} collective-permute-done((f32[216,128]{1,0:T(8,128)}, f32[216,128]{1,0:T(8,128)S(1)}, u32[]{:S(2)}, u32[]{:S(2)}) %collective-permute-start.3) | collective-permute-done | bytes 110624 | tf_op jit(solution)/shard_map/ppermute | solution.py:353
  33.9 2.1 %collective-permute-start.5 = (f32[1048,128]{1,0:T(8,128)S(1)}, f32[1048,128]{1,0:T(8,128)S(1)}, u32[]{:S(2)}, u32[]{:S(2)}) collective-permute-start(f32[1048,128]{1,0:T(8,128)S(1)} %collective-permute-done.m1), channel_id=1, source_target_pairs={{0,1},{1,0},{2,3},{3,2},{4,5},{5,4},{6,7},{7,6},{8,9},{9,8},{10,11... | collective-permute-start | bytes 1609736 | tf_op jit(solution)/shard_map/ppermute | solution.py:348
  36.7 1.8 %collective-permute-done.7.m2_o = f32[216,128]{1,0:T(8,128)S(1)} collective-permute-done((f32[216,128]{1,0:T(8,128)S(1)}, f32[216,128]{1,0:T(8,128)S(1)}, u32[]{:S(2)}, u32[]{:S(2)}) %collective-permute-start.7) | collective-permute-done | bytes 110624 | tf_op jit(solution)/shard_map/ppermute | solution.py:348
  38.7 1.0 copy-done.1
  39.7 1.6 %shard_map.65 = (f32[28,112,128]{2,1,0:T(8,128)S(1)}, f32[28,112,128]{2,1,0:T(8,128)S(1)}, f32[120,128]{1,0:T(8,128)S(1)}, f32[336,128]{1,0:T(8,128)S(1)}, f32[336,128]{1,0:T(8,128)S(1)}) custom-call(s32[2]{0:T(128)S(1)} %pad_add_fusion.pos, f32[1048,128]{1,0:T(8,128)S(1)} %copy-done.1, f32[1048,128]{1,0:T(8,128)S(1)} %collective-permute-done.m1, ...), custom_call_target="tpu_custom_call" | custom-call | tf_op jit(solution)/shard_map/pallas_call | solution.py:385
  41.8 1.5 %shard_map.66 = (f32[2,512,128]{2,1,0:T(8,128)S(1)}, f32[2,512,128]{2,1,0:T(8,128)S(1)}) custom-call(s32[2]{0:T(128)S(1)} %pad_add_fusion.pos, s32[16,128]{1,0:T(8,128)S(1)} %bitcast.41, f32[128,128]{1,0:T(8,128)S(1)} %bitcast.32), custom_call_target="tpu_custom_call" | custom-call | tf_op jit(solution)/shard_map/pallas_call | solution.py:385
  43.3 0.9 collective-permute-done.9.lz
  44.2 2.8 %collective-permute-done.10.rz = f32[336,128]{1,0:T(8,128)S(1)} collective-permute-done((f32[336,128]{1,0:T(8,128)S(1)}, f32[336,128]{1,0:T(8,128)S(1)}, u32[]{:S(2)}, u32[]{:S(2)}) %collective-permute-start.10) | collective-permute-done | bytes 172064 | tf_op jit(solution)/shard_map/ppermute | solution.py:353
  46.9 5.2 %shard_map.67 = (f32[28,112,128]{2,1,0:T(8,128)S(1)}, f32[28,112,128]{2,1,0:T(8,128)S(1)}, f32[128,128]{1,0:T(8,128)S(1)}, f32[40,128]{1,0:T(8,128)S(1)}, f32[40,128]{1,0:T(8,128)S(1)}) custom-call(s32[2]{0:T(128)S(1)} %pad_add_fusion.pos, f32[28,112,128]{2,1,0:T(8,128)S(1)} %get-tuple-element.37.fr, ...), custom_call_target="tpu_custom_call", output_to_operand_aliasing={{0}: (1, {}), {1}: (2, {})} | custom-call | tf_op jit(solution)/shard_map/pallas_call | solution.py:385
  52.1 1.1 collective-permute-start.11
  54.1 12.5 %all_to_all.32.refs_0_ = f32[16,40,128]{2,1,0:T(8,128)S(1)} all-to-all(f32[16,40,128]{2,1,0:T(8,128)S(1)} %shard_map.68), channel_id=1, replica_groups=mesh['lat_0'=4,'lat_1'=4,'lon'=8,'ens'=2] {'lat_0','lat_1'}, dimensions={0} | all-to-all | bytes 655360 | tf_op jit(solution)/shard_map/all_to_all | solution.py:379
  66.6 14.9 %all_to_all.33.refs_0_ = f32[8,40,128]{2,1,0:T(8,128)S(1)} all-to-all(f32[8,40,128]{2,1,0:T(8,128)S(1)} %shard_map.69), channel_id=1, replica_groups=mesh['lat_0'=4,'lat_1'=4,'lon'=8,'ens'=2] {'lon'}, dimensions={0} | all-to-all | bytes 327680 | tf_op jit(solution)/shard_map/all_to_all | solution.py:379
  81.5 3.4 %collective-permute-start.12 = (f32[40,128]{1,0:T(8,128)S(1)}, f32[40,128]{1,0:T(8,128)S(1)}, u32[]{:S(2)}, u32[]{:S(2)}) collective-permute-start(f32[40,128]{1,0:T(8,128)S(1)} %bitcast.33), channel_id=1, source_target_pairs={{0,1},{1,0},{2,3},{3,2},{4,5},{5,4},{6,7},{7,6},{8,9},{9,8},{10,11... | collective-permute-start | bytes 61448 | tf_op jit(solution)/shard_map/ppermute | solution.py:348
  85.7 10.4 %shard_map.71 = (f32[128,128]{1,0:T(8,128)S(1)}, f32[40,128]{1,0:T(8,128)S(1)}, f32[40,128]{1,0:T(8,128)S(1)}) custom-call(s32[2]{0:T(128)S(1)} %pad_add_fusion.pos, f32[40,128]{1,0:T(8,128)S(1)} %bitcast.34, f32[40,128]{1,0:T(8,128)S(1)} %collective-permute-done.12.other, f32[28,112,128]{2,1,0:T(8,128)S(1)} %get-tuple-element.47.fr, ...), custom_call_target="tpu_custom_call" | custom-call | tf_op jit(solution)/shard_map/pallas_call | solution.py:385
  97.5 11.2 %all_to_all.34.refs_0_ = f32[16,40,128]{2,1,0:T(8,128)S(1)} all-to-all(f32[16,40,128]{2,1,0:T(8,128)S(1)} %shard_map.72), channel_id=1, replica_groups=mesh['lat_0'=4,'lat_1'=4,'lon'=8,'ens'=2] {'lat_0','lat_1'}, dimensions={0} | all-to-all | bytes 655360 | tf_op jit(solution)/shard_map/all_to_all | solution.py:379
  108.6 10.8 %all_to_all.35.refs_0_ = f32[8,40,128]{2,1,0:T(8,128)S(1)} all-to-all(f32[8,40,128]{2,1,0:T(8,128)S(1)} %shard_map.73), channel_id=1, replica_groups=mesh['lat_0'=4,'lat_1'=4,'lon'=8,'ens'=2] {'lon'}, dimensions={0} | all-to-all | bytes 327680 | tf_op jit(solution)/shard_map/all_to_all | solution.py:379
  119.4 3.5 %collective-permute-start.14 = (f32[40,128]{1,0:T(8,128)S(1)}, f32[40,128]{1,0:T(8,128)S(1)}, u32[]{:S(2)}, u32[]{:S(2)}) collective-permute-start(f32[40,128]{1,0:T(8,128)S(1)} %bitcast.35), channel_id=1, source_target_pairs={{0,1},{1,0},{2,3},{3,2},{4,5},{5,4},{6,7},{7,6},{8,9},{9,8},{10,11... | collective-permute-start | bytes 61448 | tf_op jit(solution)/shard_map/ppermute | solution.py:348
  123.8 6.2 %shard_map.75 = f32[1024,128]{1,0:T(8,128)} custom-call(s32[2]{0:T(128)S(1)} %pad_add_fusion.pos, f32[40,128]{1,0:T(8,128)S(1)} %bitcast.36, f32[40,128]{1,0:T(8,128)S(1)} %collective-permute-done.14.other, f32[128,128]{1,0:T(8,128)S(1)} %get-tuple-element.52.k1, f32[1024,128]{1,0:T(8,128)S(1)} %bitcast.31, f32[1048,128]{1,0:T(8,128)S(1)} %collective-permute-done.4.own_o.other_p), custom_call_target="tpu_custom_call" | custom-call | tf_op jit(solution)/shard_map/pallas_call | solution.py:385
  (31 shorter events, 6.0 us)
Async XLA Ops:
  2.0 31.9 %collective-permute-start.1 = (f32[1048,128]{1,0:T(8,128)}, f32[1048,128]{1,0:T(8,128)S(1)}, u32[]{:S(2)}, u32[]{:S(2)}) collective-permute-start(f32[1048,128]{1,0:T(8,128)} %get-tuple-element.29.own), channel_id=1, source_target_pairs={{0,240},{16,0},{32,16},{48,32},{64,48},{80,64},{96,80},{112,96},{1... | collective-permute-start | bytes 1609736 | tf_op jit(solution)/shard_map/ppermute | solution.py:353
  7.9 26.1 %collective-permute-start = (f32[1048,128]{1,0:T(8,128)}, f32[1048,128]{1,0:T(8,128)S(1)}, u32[]{:S(2)}, u32[]{:S(2)}) collective-permute-start(f32[1048,128]{1,0:T(8,128)} %get-tuple-element.29.own), channel_id=1, source_target_pairs={{0,16},{16,32},{32,48},{48,64},{64,80},{80,96},{96,112},{112,128},... | collective-permute-start | bytes 1609736 | tf_op jit(solution)/shard_map/ppermute | solution.py:353
  7.9 26.1 %all-to-all-start = ((f32[128,1,128]{2,1,0:T(1,128)}), f32[128,1,128]{2,1,0:T(1,128)S(1)}, u32[]{:S(2)}, u32[]{:S(2)}) async-start(f32[128,1,128]{2,1,0:T(1,128)} %bitcast.42), calls=%async_computation | async-start | bytes 131072 | tf_op jit(solution)/shard_map/all_to_all | solution.py:413
  22.8 7.9 %collective-permute-start.2 = (f32[216,128]{1,0:T(8,128)}, f32[216,128]{1,0:T(8,128)S(1)}, u32[]{:S(2)}, u32[]{:S(2)}) collective-permute-start(f32[216,128]{1,0:T(8,128)} %get-tuple-element.30), channel_id=1, source_target_pairs={{0,32},{16,48},{32,64},{48,80},{64,96},{80,112},{96,128},{112,144}... | collective-permute-start | bytes 331784 | tf_op jit(solution)/shard_map/ppermute | solution.py:353
  24.9 9.0 %collective-permute-start.3 = (f32[216,128]{1,0:T(8,128)}, f32[216,128]{1,0:T(8,128)S(1)}, u32[]{:S(2)}, u32[]{:S(2)}) collective-permute-start(f32[216,128]{1,0:T(8,128)} %get-tuple-element.31), channel_id=1, source_target_pairs={{0,224},{16,240},{32,0},{48,16},{64,32},{80,48},{96,64},{112,80},{... | collective-permute-start | bytes 331784 | tf_op jit(solution)/shard_map/ppermute | solution.py:353
  27.9 8.8 %collective-permute-start.4 = (f32[1048,128]{1,0:T(8,128)}, f32[1048,128]{1,0:T(8,128)S(1)}, u32[]{:S(2)}, u32[]{:S(2)}) collective-permute-start(f32[1048,128]{1,0:T(8,128)} %get-tuple-element.29.own), channel_id=1, source_target_pairs={{0,1},{1,0},{2,3},{3,2},{4,5},{5,4},{6,7},{7,6},{8,9},{9,8},{10,11... | collective-permute-start | bytes 1609736 | tf_op jit(solution)/shard_map/ppermute | solution.py:348
  33.9 4.7 %collective-permute-start.5 = (f32[1048,128]{1,0:T(8,128)S(1)}, f32[1048,128]{1,0:T(8,128)S(1)}, u32[]{:S(2)}, u32[]{:S(2)}) collective-permute-start(f32[1048,128]{1,0:T(8,128)S(1)} %collective-permute-done.m1), channel_id=1, source_target_pairs={{0,1},{1,0},{2,3},{3,2},{4,5},{5,4},{6,7},{7,6},{8,9},{9,8},{10,11... | collective-permute-start | bytes 1609736 | tf_op jit(solution)/shard_map/ppermute | solution.py:348
  36.0 2.6 %collective-permute-start.6 = (f32[1048,128]{1,0:T(8,128)S(1)}, f32[1048,128]{1,0:T(8,128)S(1)}, u32[]{:S(2)}, u32[]{:S(2)}) collective-permute-start(f32[1048,128]{1,0:T(8,128)S(1)} %collective-permute-done.1.p1), channel_id=1, source_target_pairs={{0,1},{1,0},{2,3},{3,2},{4,5},{5,4},{6,7},{7,6},{8,9},{9,8},{10,11... | collective-permute-start | bytes 1609736 | tf_op jit(solution)/shard_map/ppermute | solution.py:348
  36.1 2.4 %collective-permute-start.7 = (f32[216,128]{1,0:T(8,128)S(1)}, f32[216,128]{1,0:T(8,128)S(1)}, u32[]{:S(2)}, u32[]{:S(2)}) collective-permute-start(f32[216,128]{1,0:T(8,128)S(1)} %collective-permute-done.2.m2), channel_id=1, source_target_pairs={{0,1},{1,0},{2,3},{3,2},{4,5},{5,4},{6,7},{7,6},{8,9},{9,8},{10,11... | collective-permute-start | bytes 331784 | tf_op jit(solution)/shard_map/ppermute | solution.py:348
  36.5 2.1 %collective-permute-start.8 = (f32[216,128]{1,0:T(8,128)S(1)}, f32[216,128]{1,0:T(8,128)S(1)}, u32[]{:S(2)}, u32[]{:S(2)}) collective-permute-start(f32[216,128]{1,0:T(8,128)S(1)} %collective-permute-done.3.p2), channel_id=1, source_target_pairs={{0,1},{1,0},{2,3},{3,2},{4,5},{5,4},{6,7},{7,6},{8,9},{9,8},{10,11... | collective-permute-start | bytes 331784 | tf_op jit(solution)/shard_map/ppermute | solution.py:348
  38.7 1.0 copy-start.1
  39.7 2.1 %copy-start.2 = (s32[2,1,128,8]{2,3,1,0:T(8,128)S(1)}, s32[2,1,128,8]{2,3,1,0:T(8,128)}, u32[]{:S(2)}) copy-start(s32[2,1,128,8]{2,3,1,0:T(8,128)} %param.9) | copy-start | bytes 24580
  41.3 2.9 %collective-permute-start.9 = (f32[336,128]{1,0:T(8,128)S(1)}, f32[336,128]{1,0:T(8,128)S(1)}, u32[]{:S(2)}, u32[]{:S(2)}) collective-permute-start(f32[336,128]{1,0:T(8,128)S(1)} %get-tuple-element.40), channel_id=1, source_target_pairs={{0,1},{1,2},{2,3},{3,4},{4,5},{5,6},{6,7},{7,8},{8,9},{9,10},{10,1... | collective-permute-start | bytes 516104 | tf_op jit(solution)/shard_map/ppermute | solution.py:353
  41.8 5.1 %collective-permute-start.10 = (f32[336,128]{1,0:T(8,128)S(1)}, f32[336,128]{1,0:T(8,128)S(1)}, u32[]{:S(2)}, u32[]{:S(2)}) collective-permute-start(f32[336,128]{1,0:T(8,128)S(1)} %get-tuple-element.41), channel_id=1, source_target_pairs={{0,15},{1,0},{2,1},{3,2},{4,3},{5,4},{6,5},{7,6},{8,7},{9,8},{10,9... | collective-permute-start | bytes 516104 | tf_op jit(solution)/shard_map/ppermute | solution.py:353
  52.1 1.9 %collective-permute-start.11 = (f32[40,128]{1,0:T(8,128)S(1)}, f32[40,128]{1,0:T(8,128)S(1)}, u32[]{:S(2)}, u32[]{:S(2)}) collective-permute-start(f32[40,128]{1,0:T(8,128)S(1)} %get-tuple-element.46), channel_id=1, source_target_pairs={{0,1},{1,0},{2,3},{3,2},{4,5},{5,4},{6,7},{7,6},{8,9},{9,8},{10,11... | collective-permute-start | bytes 61448 | tf_op jit(solution)/shard_map/ppermute | solution.py:348
  81.5 4.2 %collective-permute-start.12 = (f32[40,128]{1,0:T(8,128)S(1)}, f32[40,128]{1,0:T(8,128)S(1)}, u32[]{:S(2)}, u32[]{:S(2)}) collective-permute-start(f32[40,128]{1,0:T(8,128)S(1)} %bitcast.33), channel_id=1, source_target_pairs={{0,1},{1,0},{2,3},{3,2},{4,5},{5,4},{6,7},{7,6},{8,9},{9,8},{10,11... | collective-permute-start | bytes 61448 | tf_op jit(solution)/shard_map/ppermute | solution.py:348
  96.1 27.6 %copy-start = (f32[2,64,8,128]{3,2,1,0:T(8,128)S(1)}, f32[2,64,8,128]{3,2,1,0:T(8,128)}, u32[]{:S(2)}) copy-start(f32[2,64,8,128]{3,2,1,0:T(8,128)} %param.6) | copy-start | bytes 1572868
  96.2 1.3 collective-permute-start.13
  119.4 4.4 %collective-permute-start.14 = (f32[40,128]{1,0:T(8,128)S(1)}, f32[40,128]{1,0:T(8,128)S(1)}, u32[]{:S(2)}, u32[]{:S(2)}) collective-permute-start(f32[40,128]{1,0:T(8,128)S(1)} %bitcast.35), channel_id=1, source_target_pairs={{0,1},{1,0},{2,3},{3,2},{4,5},{5,4},{6,7},{7,6},{8,9},{9,8},{10,11... | collective-permute-start | bytes 61448 | tf_op jit(solution)/shard_map/ppermute | solution.py:348

commit v5 on v4

--- a/solution.py
+++ b/solution.py
@@ -90,11 +90,20 @@
     return jnp.concatenate([jnp.where(first, mine, others), jnp.where(first, others, mine)], axis=0)
 
 
-def turn_rows(pos, own, m1, p1, m2, p2, own_o, m1_o, p1_o, m2_o, p2_o, FR, FO, tiles, right, left):
+def turn_own(pos, own, own_o, out):
+    first = pos[1] == 0
+    for k in range(2 * ROWS):
+        turned = both_cores(first, own, own_o, k // ROWS * HALF * ROWS + k % ROWS, ROWS).T
+        out[k * HALF : (k + 1) * HALF] = jnp.where(first, turned[:HALF], turned[HALF:])
+    out[OWN:] = own[OWN:]
+
+
+def turn_rows(pos, own, m1, p1, m2, p2, m1_o, p1_o, m2_o, p2_o, FR, FO, tiles, right, left):
     def row_source(field, r):
-        if 2 <= r < 26:
-            which = (r - 2) // ROWS
-            return (m1, own, p1)[which], (m1_o, own_o, p1_o)[which], field * HALF * ROWS + (r - 2) % ROWS, ROWS
+        if 2 <= r < 10:
+            return m1, m1_o, field * HALF * ROWS + r - 2, ROWS
+        if 18 <= r < 26:
+            return p1, p1_o, field * HALF * ROWS + r - 18, ROWS
         k = 2 if field == 0 else (r if r < 2 else r - 26)
         refs = (m2, m2_o) if r < 2 else (p2, p2_o)
         return *refs, k * HALF, 1
@@ -102,11 +111,14 @@
     first = pos[1] == 0
     at = 0
     for field, r, n in EDGE_ROWS:
-        mine, others, start, stride = row_source(field, r)
-        turned = both_cores(first, mine, others, start, stride).T
-        turned = jnp.where(first, turned[:HALF], turned[HALF:])
-        if field == 1 and not 10 <= r < 18:
-            turned = jnp.where(inside(pos[0], r), turned, 0.0)
+        if 10 <= r < 18:
+            k = field * ROWS + r - 10
+            turned = own[k * HALF : (k + 1) * HALF]
+        else:
+            turned = both_cores(first, *row_source(field, r)).T
+            turned = jnp.where(first, turned[:HALF], turned[HALF:])
+            if field == 1:
+                turned = jnp.where(inside(pos[0], r), turned, 0.0)
         (FO if field else FR)[r, LEFT:RIGHT] = turned
         if n:
             right[at : at + n] = turned[HALF - n :]
@@ -411,9 +423,9 @@
     far = [moved(up2, LAT, 2), moved(dn2, LAT, -2)]
     own_other = swap(own)
     obs = lax.all_to_all(obs, LAT_LON, 0, 0, tiled=True)
-    *halo, obs = lax.optimization_barrier((*near, *far, obs))
-    blocks = [own, *halo]
-    others = [own_other] + [swap(x) for x in halo]
+    turned = call(turn_own, shape(OWN + INIT, MEMBERS), pos, own, own_other)
+    *halo, obs, turned = lax.optimization_barrier((*near, *far, obs, turned))
+    others = [swap(x) for x in halo]
     weights, observed = call(scatter_obs, [shape(2, 512, 128), shape(2, 512, 128)], pos, slots, obs)
 
     field = shape(EXT, WIDE, MEMBERS)
@@ -421,7 +433,7 @@
     square = shape(MEMBERS, MEMBERS)
     edge = shape(EDGE + 2 * ROWS, MEMBERS)
     ext_fr, ext_fo, tiles, right, left = call(
-        turn_rows, [field, field, shape(5 * INIT, COLS), edge, edge], pos, *blocks, *others
+        turn_rows, [field, field, shape(5 * INIT, COLS), edge, edge], pos, turned, *halo, *others
     )
     lz, rz = moved(right, LON_ENS, 1), moved(left, LON_ENS, -1)
     state = [pltpu.VMEM((EXT, WIDE, MEMBERS), F32)]
@@ -437,7 +449,7 @@
         scratch=state * 5,
     )
     mine, other = reduced(keep, send)
-    out = call(last_update, shape(2 * HALF * ROWS, COLS), pos, mine, other, k1, own_p, others[0])
+    out = call(last_update, shape(2 * HALF * ROWS, COLS), pos, mine, other, k1, own_p, own_other)
     return out.reshape(parameters.shape)
 
 

time: 130 us -> 129 us (level)
  starting transfers between devices: 39.6 us -> 37 us
    ppermute x6, starting transfers between devices: 11.5 us -> 9.28 us  [moved(): return lax.ppermute(value, axes, [(i, (i + by) % n) for i in range(n)])]
    pallas_call x5 -> x6, Pallas kernels: 24.9 us -> 25.5 us  [call(): pl.pallas_call(kernel, out_shape=out_shape, in_specs=[SMEM] + [VMEM] * le...]
  transfers between devices with their start and end apart: 16 -> 16, of which waited for: 10 -> 10; matrix products, arithmetic and copies ran while one was open for 0% -> 0% of each run, Pallas kernels for 1% -> 2%
where the time goes in v5:
time: 129 us
  blocking collectives  49.3 us (38%)
  starting transfers between devices  37 us (29%)
  Pallas kernels  27.6 us (21%)
  waiting for transfers between devices  13.6 us (11%)
    all_to_all x4, blocking collectives, reduced(): lax.all_to_all(summed(lax.axis_size(axes), *parts), axes, 0, 0, tiled=True)  49.3 us
    pallas_call x6, Pallas kernels, call(): pl.pallas_call(kernel, out_shape=out_shape, in_specs=[SMEM] + [VMEM] * le...  25.5 us
    all_to_all x1, starting transfers between devices, per_device(): obs = lax.all_to_all(obs, LAT_LON, 0, 0, tiled=True)  14.9 us
    ppermute x9, starting transfers between devices, swap(): return lax.ppermute(value, 'ens', [(0, 1), (1, 0)])  12.8 us
    ppermute x6, starting transfers between devices, moved(): return lax.ppermute(value, axes, [(i, (i + by) % n) for i in range(n)])  9.28 us
    ppermute x6, waiting for transfers between devices, moved(): return lax.ppermute(value, axes, [(i, (i + by) % n) for i in range(n)])  8.19 us
    ppermute x9, waiting for transfers between devices, swap(): return lax.ppermute(value, 'ens', [(0, 1), (1, 0)])  5.42 us
  transfers between devices with their start and end apart: 16, of which 10 were waited for; matrix products, arithmetic and copies ran while one was open for 0% of the time, Pallas kernels for 2%

profile of v5, /device:TPU:1, one launch (start us, length us, event | category | flops | bytes accessed | tf_op | source)
XLA Modules:
  0.0 128.8 jit_solution(10638059450047716615)
XLA Ops:
  0.0 2.0 %shard_map.64 = (f32[1048,128]{1,0:T(8,128)}, f32[216,128]{1,0:T(8,128)}, f32[216,128]{1,0:T(8,128)}, f32[128,128]{1,0:T(8,128)}) custom-call(f32[1024,128]{1,0:T(8,128)} %bitcast.30, f32[8,128]{1,0:T(8,128)} %height_hbm.1, f32[16,128]{1,0:T(8,128)} %bitcast.43, f32[16,128]{1,0:T(8,128)} %bitcast.44, f32[16,128]{1,0:T(8,128)} %bitcast.45), custom_call_target="tpu_custom_call" | custom-call | tf_op jit(solution)/shard_map/pallas_call | solution.py:415
  2.0 3.3 %collective-permute-start.4 = (f32[1048,128]{1,0:T(8,128)}, f32[1048,128]{1,0:T(8,128)S(1)}, u32[]{:S(2)}, u32[]{:S(2)}) collective-permute-start(f32[1048,128]{1,0:T(8,128)} %get-tuple-element.30.own), channel_id=1, source_target_pairs={{0,1},{1,0},{2,3},{3,2},{4,5},{5,4},{6,7},{7,6},{8,9},{9,8},{10,11... | collective-permute-start | bytes 1609736 | tf_op jit(solution)/shard_map/ppermute | solution.py:360
  5.3 3.2 %collective-permute-start.1 = (f32[1048,128]{1,0:T(8,128)}, f32[1048,128]{1,0:T(8,128)S(1)}, u32[]{:S(2)}, u32[]{:S(2)}) collective-permute-start(f32[1048,128]{1,0:T(8,128)} %get-tuple-element.30.own), channel_id=1, source_target_pairs={{0,240},{16,0},{32,16},{48,32},{64,48},{80,64},{96,80},{112,96},{1... | collective-permute-start | bytes 1609736 | tf_op jit(solution)/shard_map/ppermute | solution.py:365
  8.6 14.9 %all-to-all-start = ((f32[128,1,128]{2,1,0:T(1,128)}), f32[128,1,128]{2,1,0:T(1,128)S(1)}, u32[]{:S(2)}, u32[]{:S(2)}) async-start(f32[128,1,128]{2,1,0:T(1,128)} %bitcast.42), calls=%async_computation | async-start | bytes 131072 | tf_op jit(solution)/shard_map/all_to_all | solution.py:425
  23.5 2.2 %collective-permute-start.2 = (f32[216,128]{1,0:T(8,128)}, f32[216,128]{1,0:T(8,128)S(1)}, u32[]{:S(2)}, u32[]{:S(2)}) collective-permute-start(f32[216,128]{1,0:T(8,128)} %get-tuple-element.31), channel_id=1, source_target_pairs={{0,32},{16,48},{32,64},{48,80},{64,96},{80,112},{96,128},{112,144}... | collective-permute-start | bytes 331784 | tf_op jit(solution)/shard_map/ppermute | solution.py:365
  25.6 3.0 %collective-permute-start.3 = (f32[216,128]{1,0:T(8,128)}, f32[216,128]{1,0:T(8,128)S(1)}, u32[]{:S(2)}, u32[]{:S(2)}) collective-permute-start(f32[216,128]{1,0:T(8,128)} %get-tuple-element.32), channel_id=1, source_target_pairs={{0,224},{16,240},{32,0},{48,16},{64,32},{80,48},{96,64},{112,80},{... | collective-permute-start | bytes 331784 | tf_op jit(solution)/shard_map/ppermute | solution.py:365
  28.7 1.0 copy-done.1
  31.4 3.8 %collective-permute-done.3.p2 = f32[216,128]{1,0:T(8,128)S(1)} collective-permute-done((f32[216,128]{1,0:T(8,128)}, f32[216,128]{1,0:T(8,128)S(1)}, u32[]{:S(2)}, u32[]{:S(2)}) %collective-permute-start.3) | collective-permute-done | bytes 110624 | tf_op jit(solution)/shard_map/ppermute | solution.py:365
  35.2 0.9 collective-permute-start.5
  36.7 1.9 %collective-permute-done.7.m2_o = f32[216,128]{1,0:T(8,128)S(1)} collective-permute-done((f32[216,128]{1,0:T(8,128)S(1)}, f32[216,128]{1,0:T(8,128)S(1)}, u32[]{:S(2)}, u32[]{:S(2)}) %collective-permute-start.7) | collective-permute-done | bytes 110624 | tf_op jit(solution)/shard_map/ppermute | solution.py:360
  38.8 1.3 %shard_map.66 = (f32[28,112,128]{2,1,0:T(8,128)S(1)}, f32[28,112,128]{2,1,0:T(8,128)S(1)}, f32[120,128]{1,0:T(8,128)S(1)}, f32[336,128]{1,0:T(8,128)S(1)}, f32[336,128]{1,0:T(8,128)S(1)}) custom-call(s32[2]{0:T(128)S(1)} %pad_add_fusion.pos, f32[1048,128]{1,0:T(8,128)S(1)} %shard_map.65.own, f32[1048,128]{1,0:T(8,128)S(1)} %collective-permute-done.m1, ...), custom_call_target="tpu_custom_call" | custom-call | tf_op jit(solution)/shard_map/pallas_call | solution.py:397
  40.1 0.9 collective-permute-start.9
  41.0 1.5 %shard_map.67 = (f32[2,512,128]{2,1,0:T(8,128)S(1)}, f32[2,512,128]{2,1,0:T(8,128)S(1)}) custom-call(s32[2]{0:T(128)S(1)} %pad_add_fusion.pos, s32[16,128]{1,0:T(8,128)S(1)} %bitcast.41, f32[128,128]{1,0:T(8,128)S(1)} %bitcast.32), custom_call_target="tpu_custom_call" | custom-call | tf_op jit(solution)/shard_map/pallas_call | solution.py:397
  42.4 0.9 collective-permute-done.9.lz
  43.3 2.8 %collective-permute-done.10.rz = f32[336,128]{1,0:T(8,128)S(1)} collective-permute-done((f32[336,128]{1,0:T(8,128)S(1)}, f32[336,128]{1,0:T(8,128)S(1)}, u32[]{:S(2)}, u32[]{:S(2)}) %collective-permute-start.10) | collective-permute-done | bytes 172064 | tf_op jit(solution)/shard_map/ppermute | solution.py:365
  46.1 5.2 %shard_map.68 = (f32[28,112,128]{2,1,0:T(8,128)S(1)}, f32[28,112,128]{2,1,0:T(8,128)S(1)}, f32[128,128]{1,0:T(8,128)S(1)}, f32[40,128]{1,0:T(8,128)S(1)}, f32[40,128]{1,0:T(8,128)S(1)}) custom-call(s32[2]{0:T(128)S(1)} %pad_add_fusion.pos, f32[28,112,128]{2,1,0:T(8,128)S(1)} %get-tuple-element.39.fr, ...), custom_call_target="tpu_custom_call", output_to_operand_aliasing={{0}: (1, {}), {1}: (2, {})} | custom-call | tf_op jit(solution)/shard_map/pallas_call | solution.py:397
  52.8 12.5 %all_to_all.32.refs_0_ = f32[16,40,128]{2,1,0:T(8,128)S(1)} all-to-all(f32[16,40,128]{2,1,0:T(8,128)S(1)} %shard_map.69), channel_id=1, replica_groups=mesh['lat_0'=4,'lat_1'=4,'lon'=8,'ens'=2] {'lat_0','lat_1'}, dimensions={0} | all-to-all | bytes 655360 | tf_op jit(solution)/shard_map/all_to_all | solution.py:391
  65.4 14.9 %all_to_all.33.refs_0_ = f32[8,40,128]{2,1,0:T(8,128)S(1)} all-to-all(f32[8,40,128]{2,1,0:T(8,128)S(1)} %shard_map.70), channel_id=1, replica_groups=mesh['lat_0'=4,'lat_1'=4,'lon'=8,'ens'=2] {'lon'}, dimensions={0} | all-to-all | bytes 327680 | tf_op jit(solution)/shard_map/all_to_all | solution.py:391
  80.3 3.4 %collective-permute-start.12 = (f32[40,128]{1,0:T(8,128)S(1)}, f32[40,128]{1,0:T(8,128)S(1)}, u32[]{:S(2)}, u32[]{:S(2)}) collective-permute-start(f32[40,128]{1,0:T(8,128)S(1)} %bitcast.33), channel_id=1, source_target_pairs={{0,1},{1,0},{2,3},{3,2},{4,5},{5,4},{6,7},{7,6},{8,9},{9,8},{10,11... | collective-permute-start | bytes 61448 | tf_op jit(solution)/shard_map/ppermute | solution.py:360
  84.5 10.4 %shard_map.72 = (f32[128,128]{1,0:T(8,128)S(1)}, f32[40,128]{1,0:T(8,128)S(1)}, f32[40,128]{1,0:T(8,128)S(1)}) custom-call(s32[2]{0:T(128)S(1)} %pad_add_fusion.pos, f32[40,128]{1,0:T(8,128)S(1)} %bitcast.34, f32[40,128]{1,0:T(8,128)S(1)} %collective-permute-done.12.other, f32[28,112,128]{2,1,0:T(8,128)S(1)} %get-tuple-element.49.fr, ...), custom_call_target="tpu_custom_call" | custom-call | tf_op jit(solution)/shard_map/pallas_call | solution.py:397
  96.2 11.2 %all_to_all.34.refs_0_ = f32[16,40,128]{2,1,0:T(8,128)S(1)} all-to-all(f32[16,40,128]{2,1,0:T(8,128)S(1)} %shard_map.73), channel_id=1, replica_groups=mesh['lat_0'=4,'lat_1'=4,'lon'=8,'ens'=2] {'lat_0','lat_1'}, dimensions={0} | all-to-all | bytes 655360 | tf_op jit(solution)/shard_map/all_to_all | solution.py:391
  107.4 10.8 %all_to_all.35.refs_0_ = f32[8,40,128]{2,1,0:T(8,128)S(1)} all-to-all(f32[8,40,128]{2,1,0:T(8,128)S(1)} %shard_map.74), channel_id=1, replica_groups=mesh['lat_0'=4,'lat_1'=4,'lon'=8,'ens'=2] {'lon'}, dimensions={0} | all-to-all | bytes 327680 | tf_op jit(solution)/shard_map/all_to_all | solution.py:391
  118.2 3.5 %collective-permute-start.14 = (f32[40,128]{1,0:T(8,128)S(1)}, f32[40,128]{1,0:T(8,128)S(1)}, u32[]{:S(2)}, u32[]{:S(2)}) collective-permute-start(f32[40,128]{1,0:T(8,128)S(1)} %bitcast.35), channel_id=1, source_target_pairs={{0,1},{1,0},{2,3},{3,2},{4,5},{5,4},{6,7},{7,6},{8,9},{9,8},{10,11... | collective-permute-start | bytes 61448 | tf_op jit(solution)/shard_map/ppermute | solution.py:360
  122.6 6.2 %shard_map.76 = f32[1024,128]{1,0:T(8,128)} custom-call(s32[2]{0:T(128)S(1)} %pad_add_fusion.pos, f32[40,128]{1,0:T(8,128)S(1)} %bitcast.36, f32[40,128]{1,0:T(8,128)S(1)} %collective-permute-done.14.other, f32[128,128]{1,0:T(8,128)S(1)} %get-tuple-element.54.k1, f32[1024,128]{1,0:T(8,128)S(1)} %bitcast.31, f32[1048,128]{1,0:T(8,128)S(1)} %collective-permute-done.4.own_o.other_p), custom_call_target="tpu_custom_call" | custom-call | tf_op jit(solution)/shard_map/pallas_call | solution.py:397
  (32 shorter events, 7.1 us)
Async XLA Ops:
  2.0 26.7 %collective-permute-start.4 = (f32[1048,128]{1,0:T(8,128)}, f32[1048,128]{1,0:T(8,128)S(1)}, u32[]{:S(2)}, u32[]{:S(2)}) collective-permute-start(f32[1048,128]{1,0:T(8,128)} %get-tuple-element.30.own), channel_id=1, source_target_pairs={{0,1},{1,0},{2,3},{3,2},{4,5},{5,4},{6,7},{7,6},{8,9},{9,8},{10,11... | collective-permute-start | bytes 1609736 | tf_op jit(solution)/shard_map/ppermute | solution.py:360
  5.3 29.8 %collective-permute-start.1 = (f32[1048,128]{1,0:T(8,128)}, f32[1048,128]{1,0:T(8,128)S(1)}, u32[]{:S(2)}, u32[]{:S(2)}) collective-permute-start(f32[1048,128]{1,0:T(8,128)} %get-tuple-element.30.own), channel_id=1, source_target_pairs={{0,240},{16,0},{32,16},{48,32},{64,48},{80,64},{96,80},{112,96},{1... | collective-permute-start | bytes 1609736 | tf_op jit(solution)/shard_map/ppermute | solution.py:365
  8.6 26.6 %collective-permute-start = (f32[1048,128]{1,0:T(8,128)}, f32[1048,128]{1,0:T(8,128)S(1)}, u32[]{:S(2)}, u32[]{:S(2)}) collective-permute-start(f32[1048,128]{1,0:T(8,128)} %get-tuple-element.30.own), channel_id=1, source_target_pairs={{0,16},{16,32},{32,48},{48,64},{64,80},{80,96},{96,112},{112,128},... | collective-permute-start | bytes 1609736 | tf_op jit(solution)/shard_map/ppermute | solution.py:365
  8.6 26.6 %all-to-all-start = ((f32[128,1,128]{2,1,0:T(1,128)}), f32[128,1,128]{2,1,0:T(1,128)S(1)}, u32[]{:S(2)}, u32[]{:S(2)}) async-start(f32[128,1,128]{2,1,0:T(1,128)} %bitcast.42), calls=%async_computation | async-start | bytes 131072 | tf_op jit(solution)/shard_map/all_to_all | solution.py:425
  23.5 7.9 %collective-permute-start.2 = (f32[216,128]{1,0:T(8,128)}, f32[216,128]{1,0:T(8,128)S(1)}, u32[]{:S(2)}, u32[]{:S(2)}) collective-permute-start(f32[216,128]{1,0:T(8,128)} %get-tuple-element.31), channel_id=1, source_target_pairs={{0,32},{16,48},{32,64},{48,80},{64,96},{80,112},{96,128},{112,144}... | collective-permute-start | bytes 331784 | tf_op jit(solution)/shard_map/ppermute | solution.py:365
  25.6 9.5 %collective-permute-start.3 = (f32[216,128]{1,0:T(8,128)}, f32[216,128]{1,0:T(8,128)S(1)}, u32[]{:S(2)}, u32[]{:S(2)}) collective-permute-start(f32[216,128]{1,0:T(8,128)} %get-tuple-element.32), channel_id=1, source_target_pairs={{0,224},{16,240},{32,0},{48,16},{64,32},{80,48},{96,64},{112,80},{... | collective-permute-start | bytes 331784 | tf_op jit(solution)/shard_map/ppermute | solution.py:365
  28.7 1.0 copy-start.1
  30.6 10.3 %copy-start.2 = (s32[2,1,128,8]{2,3,1,0:T(8,128)S(1)}, s32[2,1,128,8]{2,3,1,0:T(8,128)}, u32[]{:S(2)}) copy-start(s32[2,1,128,8]{2,3,1,0:T(8,128)} %param.9) | copy-start | bytes 24580
  35.2 3.6 %collective-permute-start.5 = (f32[1048,128]{1,0:T(8,128)S(1)}, f32[1048,128]{1,0:T(8,128)S(1)}, u32[]{:S(2)}, u32[]{:S(2)}) collective-permute-start(f32[1048,128]{1,0:T(8,128)S(1)} %collective-permute-done.m1), channel_id=1, source_target_pairs={{0,1},{1,0},{2,3},{3,2},{4,5},{5,4},{6,7},{7,6},{8,9},{9,8},{10,11... | collective-permute-start | bytes 1609736 | tf_op jit(solution)/shard_map/ppermute | solution.py:360
  36.1 2.6 %collective-permute-start.6 = (f32[1048,128]{1,0:T(8,128)S(1)}, f32[1048,128]{1,0:T(8,128)S(1)}, u32[]{:S(2)}, u32[]{:S(2)}) collective-permute-start(f32[1048,128]{1,0:T(8,128)S(1)} %collective-permute-done.1.p1), channel_id=1, source_target_pairs={{0,1},{1,0},{2,3},{3,2},{4,5},{5,4},{6,7},{7,6},{8,9},{9,8},{10,11... | collective-permute-start | bytes 1609736 | tf_op jit(solution)/shard_map/ppermute | solution.py:360
  36.2 2.4 %collective-permute-start.7 = (f32[216,128]{1,0:T(8,128)S(1)}, f32[216,128]{1,0:T(8,128)S(1)}, u32[]{:S(2)}, u32[]{:S(2)}) collective-permute-start(f32[216,128]{1,0:T(8,128)S(1)} %collective-permute-done.2.m2), channel_id=1, source_target_pairs={{0,1},{1,0},{2,3},{3,2},{4,5},{5,4},{6,7},{7,6},{8,9},{9,8},{10,11... | collective-permute-start | bytes 331784 | tf_op jit(solution)/shard_map/ppermute | solution.py:360
  36.6 2.1 %collective-permute-start.8 = (f32[216,128]{1,0:T(8,128)S(1)}, f32[216,128]{1,0:T(8,128)S(1)}, u32[]{:S(2)}, u32[]{:S(2)}) collective-permute-start(f32[216,128]{1,0:T(8,128)S(1)} %collective-permute-done.3.p2), channel_id=1, source_target_pairs={{0,1},{1,0},{2,3},{3,2},{4,5},{5,4},{6,7},{7,6},{8,9},{9,8},{10,11... | collective-permute-start | bytes 331784 | tf_op jit(solution)/shard_map/ppermute | solution.py:360
  40.1 3.3 %collective-permute-start.9 = (f32[336,128]{1,0:T(8,128)S(1)}, f32[336,128]{1,0:T(8,128)S(1)}, u32[]{:S(2)}, u32[]{:S(2)}) collective-permute-start(f32[336,128]{1,0:T(8,128)S(1)} %get-tuple-element.42), channel_id=1, source_target_pairs={{0,1},{1,2},{2,3},{3,4},{4,5},{5,6},{6,7},{7,8},{8,9},{9,10},{10,1... | collective-permute-start | bytes 516104 | tf_op jit(solution)/shard_map/ppermute | solution.py:365
  41.0 5.1 %collective-permute-start.10 = (f32[336,128]{1,0:T(8,128)S(1)}, f32[336,128]{1,0:T(8,128)S(1)}, u32[]{:S(2)}, u32[]{:S(2)}) collective-permute-start(f32[336,128]{1,0:T(8,128)S(1)} %get-tuple-element.43), channel_id=1, source_target_pairs={{0,15},{1,0},{2,1},{3,2},{4,3},{5,4},{6,5},{7,6},{8,7},{9,8},{10,9... | collective-permute-start | bytes 516104 | tf_op jit(solution)/shard_map/ppermute | solution.py:365
  51.3 1.5 %collective-permute-start.11 = (f32[40,128]{1,0:T(8,128)S(1)}, f32[40,128]{1,0:T(8,128)S(1)}, u32[]{:S(2)}, u32[]{:S(2)}) collective-permute-start(f32[40,128]{1,0:T(8,128)S(1)} %get-tuple-element.48), channel_id=1, source_target_pairs={{0,1},{1,0},{2,3},{3,2},{4,5},{5,4},{6,7},{7,6},{8,9},{9,8},{10,11... | collective-permute-start | bytes 61448 | tf_op jit(solution)/shard_map/ppermute | solution.py:360
  80.3 4.2 %collective-permute-start.12 = (f32[40,128]{1,0:T(8,128)S(1)}, f32[40,128]{1,0:T(8,128)S(1)}, u32[]{:S(2)}, u32[]{:S(2)}) collective-permute-start(f32[40,128]{1,0:T(8,128)S(1)} %bitcast.33), channel_id=1, source_target_pairs={{0,1},{1,0},{2,3},{3,2},{4,5},{5,4},{6,7},{7,6},{8,9},{9,8},{10,11... | collective-permute-start | bytes 61448 | tf_op jit(solution)/shard_map/ppermute | solution.py:360
  94.9 27.7 %copy-start = (f32[2,64,8,128]{3,2,1,0:T(8,128)S(1)}, f32[2,64,8,128]{3,2,1,0:T(8,128)}, u32[]{:S(2)}) copy-start(f32[2,64,8,128]{3,2,1,0:T(8,128)} %param.6) | copy-start | bytes 1572868
  94.9 1.3 collective-permute-start.13
  118.2 4.4 %collective-permute-start.14 = (f32[40,128]{1,0:T(8,128)S(1)}, f32[40,128]{1,0:T(8,128)S(1)}, u32[]{:S(2)}, u32[]{:S(2)}) collective-permute-start(f32[40,128]{1,0:T(8,128)S(1)} %bitcast.35), channel_id=1, source_target_pairs={{0,1},{1,0},{2,3},{3,2},{4,5},{5,4},{6,7},{7,6},{8,9},{9,8},{10,11... | collective-permute-start | bytes 61448 | tf_op jit(solution)/shard_map/ppermute | solution.py:360

commit v6 on v5

--- a/solution.py
+++ b/solution.py
@@ -60,7 +60,7 @@
     for copy in copies[:2]:
         copy.wait()
     lines = [values[...], precision[...], jnp.zeros((96, MEMBERS), F32)]
-    obs[...] = jnp.concatenate(lines, axis=0).T
+    obs[...] = jnp.concatenate(lines, axis=0).T[:, :32]
     for copy in copies[2:]:
         copy.wait()
     for k, (f, up_row, down_row) in enumerate(((1, 6, 0), (1, 7, 1), (0, 7, 0))):
@@ -142,7 +142,7 @@
 
 
 def scatter_obs(pos, slots, received, weights, observed):
-    received = received[...].T
+    received = jnp.concatenate([received[...], jnp.zeros((MEMBERS, 96), F32)], axis=1).T
     values, precision = received[:16], received[16:32]
     lines = ROWS * HALF
     k = iota((lines, MEMBERS), 0)
@@ -414,7 +414,7 @@
     two_far = shape(3 * HALF + INIT, COLS)
     own, up2, dn2, obs = pl.pallas_call(
         collect,
-        out_shape=[shape(OWN + INIT, COLS), two_far, two_far, shape(128, 128)],
+        out_shape=[shape(OWN + INIT, COLS), two_far, two_far, shape(128, 32)],
         in_specs=[pl.BlockSpec(memory_space=pl.ANY)] * 5,
         out_specs=[VMEM] * 4,
         scratch_shapes=[pltpu.VMEM((16, COLS), F32)] * 2 + [pltpu.SemaphoreType.DMA((5,))],

time: 129 us -> 129 us (level)
    all_to_all x1, waiting for transfers between devices: 0.01 us -> 3.36 us  [per_device(): obs = lax.all_to_all(obs, LAT_LON, 0, 0, tiled=True)]
    ppermute x6, waiting for transfers between devices: 8.19 us -> 4.83 us  [moved(): return lax.ppermute(value, axes, [(i, (i + by) % n) for i in range(n)])]
where the time goes in v6:
time: 129 us
  blocking collectives  49.1 us (38%)
  starting transfers between devices  37.1 us (29%)
  Pallas kernels  27.6 us (21%)
  waiting for transfers between devices  13.6 us (11%)
    all_to_all x4, blocking collectives, reduced(): lax.all_to_all(summed(lax.axis_size(axes), *parts), axes, 0, 0, tiled=True)  49.1 us
    pallas_call x6, Pallas kernels, call(): pl.pallas_call(kernel, out_shape=out_shape, in_specs=[SMEM] + [VMEM] * le...  25.5 us
    all_to_all x1, starting transfers between devices, per_device(): obs = lax.all_to_all(obs, LAT_LON, 0, 0, tiled=True)  14.9 us
    ppermute x9, starting transfers between devices, swap(): return lax.ppermute(value, 'ens', [(0, 1), (1, 0)])  13.1 us
    ppermute x6, starting transfers between devices, moved(): return lax.ppermute(value, axes, [(i, (i + by) % n) for i in range(n)])  9.09 us
    ppermute x9, waiting for transfers between devices, swap(): return lax.ppermute(value, 'ens', [(0, 1), (1, 0)])  5.41 us
    ppermute x6, waiting for transfers between devices, moved(): return lax.ppermute(value, axes, [(i, (i + by) % n) for i in range(n)])  4.83 us
    all_to_all x1, waiting for transfers between devices, per_device(): obs = lax.all_to_all(obs, LAT_LON, 0, 0, tiled=True)  3.36 us
  transfers between devices with their start and end apart: 16, of which 10 were waited for; matrix products, arithmetic and copies ran while one was open for 0% of the time, Pallas kernels for 2%

profile of v6, /device:TPU:1, one launch (start us, length us, event | category | flops | bytes accessed | tf_op | source)
XLA Modules:
  0.0 128.7 jit_solution(8193142239258625576)
XLA Ops:
  0.0 2.0 %shard_map.64 = (f32[1048,128]{1,0:T(8,128)}, f32[216,128]{1,0:T(8,128)}, f32[216,128]{1,0:T(8,128)}, f32[128,32]{1,0:T(8,128)}) custom-call(f32[1024,128]{1,0:T(8,128)} %bitcast.30, f32[8,128]{1,0:T(8,128)} %height_hbm.1, f32[16,128]{1,0:T(8,128)} %bitcast.43, f32[16,128]{1,0:T(8,128)} %bitcast.44, f32[16,128]{1,0:T(8,128)} %bitcast.45), custom_call_target="tpu_custom_call" | custom-call | tf_op jit(solution)/shard_map/pallas_call | solution.py:415
  2.0 3.3 %collective-permute-start.4 = (f32[1048,128]{1,0:T(8,128)}, f32[1048,128]{1,0:T(8,128)S(1)}, u32[]{:S(2)}, u32[]{:S(2)}) collective-permute-start(f32[1048,128]{1,0:T(8,128)} %get-tuple-element.30.own), channel_id=1, source_target_pairs={{0,1},{1,0},{2,3},{3,2},{4,5},{5,4},{6,7},{7,6},{8,9},{9,8},{10,11... | collective-permute-start | bytes 1609736 | tf_op jit(solution)/shard_map/ppermute | solution.py:360
  5.3 3.2 %collective-permute-start.1 = (f32[1048,128]{1,0:T(8,128)}, f32[1048,128]{1,0:T(8,128)S(1)}, u32[]{:S(2)}, u32[]{:S(2)}) collective-permute-start(f32[1048,128]{1,0:T(8,128)} %get-tuple-element.30.own), channel_id=1, source_target_pairs={{0,240},{16,0},{32,16},{48,32},{64,48},{80,64},{96,80},{112,96},{1... | collective-permute-start | bytes 1609736 | tf_op jit(solution)/shard_map/ppermute | solution.py:365
  8.6 14.9 %all-to-all-start = ((f32[128,1,32]{2,1,0:T(1,128)}), f32[128,1,32]{2,1,0:T(1,128)S(1)}, u32[]{:S(2)}, u32[]{:S(2)}) async-start(f32[128,1,32]{2,1,0:T(1,128)} %bitcast.42), calls=%async_computation | async-start | bytes 131072 | tf_op jit(solution)/shard_map/all_to_all | solution.py:425
  23.5 2.2 %collective-permute-start.2 = (f32[216,128]{1,0:T(8,128)}, f32[216,128]{1,0:T(8,128)S(1)}, u32[]{:S(2)}, u32[]{:S(2)}) collective-permute-start(f32[216,128]{1,0:T(8,128)} %get-tuple-element.31), channel_id=1, source_target_pairs={{0,32},{16,48},{32,64},{48,80},{64,96},{80,112},{96,128},{112,144}... | collective-permute-start | bytes 331784 | tf_op jit(solution)/shard_map/ppermute | solution.py:365
  25.6 3.0 %collective-permute-start.3 = (f32[216,128]{1,0:T(8,128)}, f32[216,128]{1,0:T(8,128)S(1)}, u32[]{:S(2)}, u32[]{:S(2)}) collective-permute-start(f32[216,128]{1,0:T(8,128)} %get-tuple-element.32), channel_id=1, source_target_pairs={{0,224},{16,240},{32,0},{48,16},{64,32},{80,48},{96,64},{112,80},{... | collective-permute-start | bytes 331784 | tf_op jit(solution)/shard_map/ppermute | solution.py:365
  28.7 1.0 copy-done.1
  30.7 3.4 %all-to-all-done = f32[128,1,32]{2,1,0:T(1,128)S(1)} async-done(((f32[128,1,32]{2,1,0:T(1,128)}), f32[128,1,32]{2,1,0:T(1,128)S(1)}, u32[]{:S(2)}, u32[]{:S(2)}) %all-to-all-start) | async-done | bytes 16416 | tf_op jit(solution)/shard_map/all_to_all | solution.py:425
  34.0 1.2 collective-permute-done.3.p2
  35.2 1.0 collective-permute-start.5
  36.8 1.9 %collective-permute-done.7.m2_o = f32[216,128]{1,0:T(8,128)S(1)} collective-permute-done((f32[216,128]{1,0:T(8,128)S(1)}, f32[216,128]{1,0:T(8,128)S(1)}, u32[]{:S(2)}, u32[]{:S(2)}) %collective-permute-start.7) | collective-permute-done | bytes 110624 | tf_op jit(solution)/shard_map/ppermute | solution.py:360
  38.9 1.3 %shard_map.66 = (f32[28,112,128]{2,1,0:T(8,128)S(1)}, f32[28,112,128]{2,1,0:T(8,128)S(1)}, f32[120,128]{1,0:T(8,128)S(1)}, f32[336,128]{1,0:T(8,128)S(1)}, f32[336,128]{1,0:T(8,128)S(1)}) custom-call(s32[2]{0:T(128)S(1)} %pad_add_fusion.pos, f32[1048,128]{1,0:T(8,128)S(1)} %shard_map.65.own, f32[1048,128]{1,0:T(8,128)S(1)} %collective-permute-done.m1, ...), custom_call_target="tpu_custom_call" | custom-call | tf_op jit(solution)/shard_map/pallas_call | solution.py:397
  40.9 1.5 %shard_map.67 = (f32[2,512,128]{2,1,0:T(8,128)S(1)}, f32[2,512,128]{2,1,0:T(8,128)S(1)}) custom-call(s32[2]{0:T(128)S(1)} %pad_add_fusion.pos, s32[16,128]{1,0:T(8,128)S(1)} %bitcast.41, f32[128,32]{1,0:T(8,128)S(1)} %bitcast.32), custom_call_target="tpu_custom_call" | custom-call | tf_op jit(solution)/shard_map/pallas_call | solution.py:397
  42.3 0.9 collective-permute-done.9.lz
  43.2 2.8 %collective-permute-done.10.rz = f32[336,128]{1,0:T(8,128)S(1)} collective-permute-done((f32[336,128]{1,0:T(8,128)S(1)}, f32[336,128]{1,0:T(8,128)S(1)}, u32[]{:S(2)}, u32[]{:S(2)}) %collective-permute-start.10) | collective-permute-done | bytes 172064 | tf_op jit(solution)/shard_map/ppermute | solution.py:365
  46.0 5.2 %shard_map.68 = (f32[28,112,128]{2,1,0:T(8,128)S(1)}, f32[28,112,128]{2,1,0:T(8,128)S(1)}, f32[128,128]{1,0:T(8,128)S(1)}, f32[40,128]{1,0:T(8,128)S(1)}, f32[40,128]{1,0:T(8,128)S(1)}) custom-call(s32[2]{0:T(128)S(1)} %pad_add_fusion.pos, f32[28,112,128]{2,1,0:T(8,128)S(1)} %get-tuple-element.39.fr, ...), custom_call_target="tpu_custom_call", output_to_operand_aliasing={{0}: (1, {}), {1}: (2, {})} | custom-call | tf_op jit(solution)/shard_map/pallas_call | solution.py:397
  52.9 12.3 %all_to_all.32.refs_0_ = f32[16,40,128]{2,1,0:T(8,128)S(1)} all-to-all(f32[16,40,128]{2,1,0:T(8,128)S(1)} %shard_map.69), channel_id=1, replica_groups=mesh['lat_0'=4,'lat_1'=4,'lon'=8,'ens'=2] {'lat_0','lat_1'}, dimensions={0} | all-to-all | bytes 655360 | tf_op jit(solution)/shard_map/all_to_all | solution.py:391
  65.3 14.9 %all_to_all.33.refs_0_ = f32[8,40,128]{2,1,0:T(8,128)S(1)} all-to-all(f32[8,40,128]{2,1,0:T(8,128)S(1)} %shard_map.70), channel_id=1, replica_groups=mesh['lat_0'=4,'lat_1'=4,'lon'=8,'ens'=2] {'lon'}, dimensions={0} | all-to-all | bytes 327680 | tf_op jit(solution)/shard_map/all_to_all | solution.py:391
  80.2 3.4 %collective-permute-start.12 = (f32[40,128]{1,0:T(8,128)S(1)}, f32[40,128]{1,0:T(8,128)S(1)}, u32[]{:S(2)}, u32[]{:S(2)}) collective-permute-start(f32[40,128]{1,0:T(8,128)S(1)} %bitcast.33), channel_id=1, source_target_pairs={{0,1},{1,0},{2,3},{3,2},{4,5},{5,4},{6,7},{7,6},{8,9},{9,8},{10,11... | collective-permute-start | bytes 61448 | tf_op jit(solution)/shard_map/ppermute | solution.py:360
  84.4 10.4 %shard_map.72 = (f32[128,128]{1,0:T(8,128)S(1)}, f32[40,128]{1,0:T(8,128)S(1)}, f32[40,128]{1,0:T(8,128)S(1)}) custom-call(s32[2]{0:T(128)S(1)} %pad_add_fusion.pos, f32[40,128]{1,0:T(8,128)S(1)} %bitcast.34, f32[40,128]{1,0:T(8,128)S(1)} %collective-permute-done.12.other, f32[28,112,128]{2,1,0:T(8,128)S(1)} %get-tuple-element.49.fr, ...), custom_call_target="tpu_custom_call" | custom-call | tf_op jit(solution)/shard_map/pallas_call | solution.py:397
  96.1 11.2 %all_to_all.34.refs_0_ = f32[16,40,128]{2,1,0:T(8,128)S(1)} all-to-all(f32[16,40,128]{2,1,0:T(8,128)S(1)} %shard_map.73), channel_id=1, replica_groups=mesh['lat_0'=4,'lat_1'=4,'lon'=8,'ens'=2] {'lat_0','lat_1'}, dimensions={0} | all-to-all | bytes 655360 | tf_op jit(solution)/shard_map/all_to_all | solution.py:391
  107.3 10.8 %all_to_all.35.refs_0_ = f32[8,40,128]{2,1,0:T(8,128)S(1)} all-to-all(f32[8,40,128]{2,1,0:T(8,128)S(1)} %shard_map.74), channel_id=1, replica_groups=mesh['lat_0'=4,'lat_1'=4,'lon'=8,'ens'=2] {'lon'}, dimensions={0} | all-to-all | bytes 327680 | tf_op jit(solution)/shard_map/all_to_all | solution.py:391
  118.1 3.5 %collective-permute-start.14 = (f32[40,128]{1,0:T(8,128)S(1)}, f32[40,128]{1,0:T(8,128)S(1)}, u32[]{:S(2)}, u32[]{:S(2)}) collective-permute-start(f32[40,128]{1,0:T(8,128)S(1)} %bitcast.35), channel_id=1, source_target_pairs={{0,1},{1,0},{2,3},{3,2},{4,5},{5,4},{6,7},{7,6},{8,9},{9,8},{10,11... | collective-permute-start | bytes 61448 | tf_op jit(solution)/shard_map/ppermute | solution.py:360
  122.5 6.2 %shard_map.76 = f32[1024,128]{1,0:T(8,128)} custom-call(s32[2]{0:T(128)S(1)} %pad_add_fusion.pos, f32[40,128]{1,0:T(8,128)S(1)} %bitcast.36, f32[40,128]{1,0:T(8,128)S(1)} %collective-permute-done.14.other, f32[128,128]{1,0:T(8,128)S(1)} %get-tuple-element.54.k1, f32[1024,128]{1,0:T(8,128)S(1)} %bitcast.31, f32[1048,128]{1,0:T(8,128)S(1)} %collective-permute-done.4.own_o.other_p), custom_call_target="tpu_custom_call" | custom-call | tf_op jit(solution)/shard_map/pallas_call | solution.py:397
  (32 shorter events, 7.3 us)
Async XLA Ops:
  2.0 26.7 %collective-permute-start.4 = (f32[1048,128]{1,0:T(8,128)}, f32[1048,128]{1,0:T(8,128)S(1)}, u32[]{:S(2)}, u32[]{:S(2)}) collective-permute-start(f32[1048,128]{1,0:T(8,128)} %get-tuple-element.30.own), channel_id=1, source_target_pairs={{0,1},{1,0},{2,3},{3,2},{4,5},{5,4},{6,7},{7,6},{8,9},{9,8},{10,11... | collective-permute-start | bytes 1609736 | tf_op jit(solution)/shard_map/ppermute | solution.py:360
  5.3 29.8 %collective-permute-start.1 = (f32[1048,128]{1,0:T(8,128)}, f32[1048,128]{1,0:T(8,128)S(1)}, u32[]{:S(2)}, u32[]{:S(2)}) collective-permute-start(f32[1048,128]{1,0:T(8,128)} %get-tuple-element.30.own), channel_id=1, source_target_pairs={{0,240},{16,0},{32,16},{48,32},{64,48},{80,64},{96,80},{112,96},{1... | collective-permute-start | bytes 1609736 | tf_op jit(solution)/shard_map/ppermute | solution.py:365
  8.6 26.6 %collective-permute-start = (f32[1048,128]{1,0:T(8,128)}, f32[1048,128]{1,0:T(8,128)S(1)}, u32[]{:S(2)}, u32[]{:S(2)}) collective-permute-start(f32[1048,128]{1,0:T(8,128)} %get-tuple-element.30.own), channel_id=1, source_target_pairs={{0,16},{16,32},{32,48},{48,64},{64,80},{80,96},{96,112},{112,128},... | collective-permute-start | bytes 1609736 | tf_op jit(solution)/shard_map/ppermute | solution.py:365
  8.6 25.5 %all-to-all-start = ((f32[128,1,32]{2,1,0:T(1,128)}), f32[128,1,32]{2,1,0:T(1,128)S(1)}, u32[]{:S(2)}, u32[]{:S(2)}) async-start(f32[128,1,32]{2,1,0:T(1,128)} %bitcast.42), calls=%async_computation | async-start | bytes 131072 | tf_op jit(solution)/shard_map/all_to_all | solution.py:425
  23.5 10.5 %collective-permute-start.2 = (f32[216,128]{1,0:T(8,128)}, f32[216,128]{1,0:T(8,128)S(1)}, u32[]{:S(2)}, u32[]{:S(2)}) collective-permute-start(f32[216,128]{1,0:T(8,128)} %get-tuple-element.31), channel_id=1, source_target_pairs={{0,32},{16,48},{32,64},{48,80},{64,96},{80,112},{96,128},{112,144}... | collective-permute-start | bytes 331784 | tf_op jit(solution)/shard_map/ppermute | solution.py:365
  25.6 9.5 %collective-permute-start.3 = (f32[216,128]{1,0:T(8,128)}, f32[216,128]{1,0:T(8,128)S(1)}, u32[]{:S(2)}, u32[]{:S(2)}) collective-permute-start(f32[216,128]{1,0:T(8,128)} %get-tuple-element.32), channel_id=1, source_target_pairs={{0,224},{16,240},{32,0},{48,16},{64,32},{80,48},{96,64},{112,80},{... | collective-permute-start | bytes 331784 | tf_op jit(solution)/shard_map/ppermute | solution.py:365
  28.7 1.0 copy-start.1
  30.6 10.2 %copy-start.2 = (s32[2,1,128,8]{2,3,1,0:T(8,128)S(1)}, s32[2,1,128,8]{2,3,1,0:T(8,128)}, u32[]{:S(2)}) copy-start(s32[2,1,128,8]{2,3,1,0:T(8,128)} %param.9) | copy-start | bytes 24580
  35.2 3.7 %collective-permute-start.5 = (f32[1048,128]{1,0:T(8,128)S(1)}, f32[1048,128]{1,0:T(8,128)S(1)}, u32[]{:S(2)}, u32[]{:S(2)}) collective-permute-start(f32[1048,128]{1,0:T(8,128)S(1)} %collective-permute-done.m1), channel_id=1, source_target_pairs={{0,1},{1,0},{2,3},{3,2},{4,5},{5,4},{6,7},{7,6},{8,9},{9,8},{10,11... | collective-permute-start | bytes 1609736 | tf_op jit(solution)/shard_map/ppermute | solution.py:360
  36.2 2.6 %collective-permute-start.6 = (f32[1048,128]{1,0:T(8,128)S(1)}, f32[1048,128]{1,0:T(8,128)S(1)}, u32[]{:S(2)}, u32[]{:S(2)}) collective-permute-start(f32[1048,128]{1,0:T(8,128)S(1)} %collective-permute-done.1.p1), channel_id=1, source_target_pairs={{0,1},{1,0},{2,3},{3,2},{4,5},{5,4},{6,7},{7,6},{8,9},{9,8},{10,11... | collective-permute-start | bytes 1609736 | tf_op jit(solution)/shard_map/ppermute | solution.py:360
  36.3 2.4 %collective-permute-start.7 = (f32[216,128]{1,0:T(8,128)S(1)}, f32[216,128]{1,0:T(8,128)S(1)}, u32[]{:S(2)}, u32[]{:S(2)}) collective-permute-start(f32[216,128]{1,0:T(8,128)S(1)} %collective-permute-done.2.m2), channel_id=1, source_target_pairs={{0,1},{1,0},{2,3},{3,2},{4,5},{5,4},{6,7},{7,6},{8,9},{9,8},{10,11... | collective-permute-start | bytes 331784 | tf_op jit(solution)/shard_map/ppermute | solution.py:360
  36.7 2.1 %collective-permute-start.8 = (f32[216,128]{1,0:T(8,128)S(1)}, f32[216,128]{1,0:T(8,128)S(1)}, u32[]{:S(2)}, u32[]{:S(2)}) collective-permute-start(f32[216,128]{1,0:T(8,128)S(1)} %collective-permute-done.3.p2), channel_id=1, source_target_pairs={{0,1},{1,0},{2,3},{3,2},{4,5},{5,4},{6,7},{7,6},{8,9},{9,8},{10,11... | collective-permute-start | bytes 331784 | tf_op jit(solution)/shard_map/ppermute | solution.py:360
  40.2 3.1 %collective-permute-start.9 = (f32[336,128]{1,0:T(8,128)S(1)}, f32[336,128]{1,0:T(8,128)S(1)}, u32[]{:S(2)}, u32[]{:S(2)}) collective-permute-start(f32[336,128]{1,0:T(8,128)S(1)} %get-tuple-element.42), channel_id=1, source_target_pairs={{0,1},{1,2},{2,3},{3,4},{4,5},{5,6},{6,7},{7,8},{8,9},{9,10},{10,1... | collective-permute-start | bytes 516104 | tf_op jit(solution)/shard_map/ppermute | solution.py:365
  40.9 5.1 %collective-permute-start.10 = (f32[336,128]{1,0:T(8,128)S(1)}, f32[336,128]{1,0:T(8,128)S(1)}, u32[]{:S(2)}, u32[]{:S(2)}) collective-permute-start(f32[336,128]{1,0:T(8,128)S(1)} %get-tuple-element.43), channel_id=1, source_target_pairs={{0,15},{1,0},{2,1},{3,2},{4,3},{5,4},{6,5},{7,6},{8,7},{9,8},{10,9... | collective-permute-start | bytes 516104 | tf_op jit(solution)/shard_map/ppermute | solution.py:365
  51.2 1.7 %collective-permute-start.11 = (f32[40,128]{1,0:T(8,128)S(1)}, f32[40,128]{1,0:T(8,128)S(1)}, u32[]{:S(2)}, u32[]{:S(2)}) collective-permute-start(f32[40,128]{1,0:T(8,128)S(1)} %get-tuple-element.48), channel_id=1, source_target_pairs={{0,1},{1,0},{2,3},{3,2},{4,5},{5,4},{6,7},{7,6},{8,9},{9,8},{10,11... | collective-permute-start | bytes 61448 | tf_op jit(solution)/shard_map/ppermute | solution.py:360
  80.2 4.2 %collective-permute-start.12 = (f32[40,128]{1,0:T(8,128)S(1)}, f32[40,128]{1,0:T(8,128)S(1)}, u32[]{:S(2)}, u32[]{:S(2)}) collective-permute-start(f32[40,128]{1,0:T(8,128)S(1)} %bitcast.33), channel_id=1, source_target_pairs={{0,1},{1,0},{2,3},{3,2},{4,5},{5,4},{6,7},{7,6},{8,9},{9,8},{10,11... | collective-permute-start | bytes 61448 | tf_op jit(solution)/shard_map/ppermute | solution.py:360
  94.8 27.6 %copy-start = (f32[2,64,8,128]{3,2,1,0:T(8,128)S(1)}, f32[2,64,8,128]{3,2,1,0:T(8,128)}, u32[]{:S(2)}) copy-start(f32[2,64,8,128]{3,2,1,0:T(8,128)} %param.6) | copy-start | bytes 1572868
  94.8 1.3 collective-permute-start.13
  118.1 4.4 %collective-permute-start.14 = (f32[40,128]{1,0:T(8,128)S(1)}, f32[40,128]{1,0:T(8,128)S(1)}, u32[]{:S(2)}, u32[]{:S(2)}) collective-permute-start(f32[40,128]{1,0:T(8,128)S(1)} %bitcast.35), channel_id=1, source_target_pairs={{0,1},{1,0},{2,3},{3,2},{4,5},{5,4},{6,7},{7,6},{8,9},{9,8},{10,11... | collective-permute-start | bytes 61448 | tf_op jit(solution)/shard_map/ppermute | solution.py:360

commit v7 on v5

--- a/solution.py
+++ b/solution.py
@@ -235,7 +235,7 @@
             row(a, b, 11 - reach + 2 * i)
             return carry
 
-        lax.fori_loop(0, (ROWS + 2 * reach) // 2, body, 0)
+        lax.fori_loop(0, (ROWS + 2 * reach) // 2, body, 0, unroll=True)
 
     for step in range(1, STEPS):
         reach = 2 * (STEPS - 1 - step)

time: 129 us -> 129 us (level)
  no operation moved by 1% of the time
where the time goes in v7:
time: 129 us; the launch traced here: 128 us
  blocking collectives  49.3 us (38%)
  starting transfers between devices  37.1 us (29%)
  Pallas kernels  26.9 us (21%)
  waiting for transfers between devices  13.6 us (11%)
    all_to_all x4, blocking collectives, reduced(): lax.all_to_all(summed(lax.axis_size(axes), *parts), axes, 0, 0, tiled=True)  49.3 us
    pallas_call x6, Pallas kernels, call(): pl.pallas_call(kernel, out_shape=out_shape, in_specs=[SMEM] + [VMEM] * le...  24.8 us
    all_to_all x1, starting transfers between devices, per_device(): obs = lax.all_to_all(obs, LAT_LON, 0, 0, tiled=True)  14.9 us
    ppermute x9, starting transfers between devices, swap(): return lax.ppermute(value, 'ens', [(0, 1), (1, 0)])  12.9 us
    ppermute x6, starting transfers between devices, moved(): return lax.ppermute(value, axes, [(i, (i + by) % n) for i in range(n)])  9.28 us
    ppermute x6, waiting for transfers between devices, moved(): return lax.ppermute(value, axes, [(i, (i + by) % n) for i in range(n)])  8.19 us
    ppermute x9, waiting for transfers between devices, swap(): return lax.ppermute(value, 'ens', [(0, 1), (1, 0)])  5.42 us
  transfers between devices with their start and end apart: 16, of which 10 were waited for; matrix products, arithmetic and copies ran while one was open for 0% of the time, Pallas kernels for 2%

profile of v7, /device:TPU:1, one launch (start us, length us, event | category | flops | bytes accessed | tf_op | source)
XLA Modules:
  0.0 128.2 jit_solution(15477555440596512095)
XLA Ops:
  0.0 2.0 %shard_map.64 = (f32[1048,128]{1,0:T(8,128)}, f32[216,128]{1,0:T(8,128)}, f32[216,128]{1,0:T(8,128)}, f32[128,128]{1,0:T(8,128)}) custom-call(f32[1024,128]{1,0:T(8,128)} %bitcast.30, f32[8,128]{1,0:T(8,128)} %height_hbm.1, f32[16,128]{1,0:T(8,128)} %bitcast.43, f32[16,128]{1,0:T(8,128)} %bitcast.44, f32[16,128]{1,0:T(8,128)} %bitcast.45), custom_call_target="tpu_custom_call" | custom-call | tf_op jit(solution)/shard_map/pallas_call | solution.py:415
  2.0 3.3 %collective-permute-start.4 = (f32[1048,128]{1,0:T(8,128)}, f32[1048,128]{1,0:T(8,128)S(1)}, u32[]{:S(2)}, u32[]{:S(2)}) collective-permute-start(f32[1048,128]{1,0:T(8,128)} %get-tuple-element.30.own), channel_id=1, source_target_pairs={{0,1},{1,0},{2,3},{3,2},{4,5},{5,4},{6,7},{7,6},{8,9},{9,8},{10,11... | collective-permute-start | bytes 1609736 | tf_op jit(solution)/shard_map/ppermute | solution.py:360
  5.3 3.2 %collective-permute-start.1 = (f32[1048,128]{1,0:T(8,128)}, f32[1048,128]{1,0:T(8,128)S(1)}, u32[]{:S(2)}, u32[]{:S(2)}) collective-permute-start(f32[1048,128]{1,0:T(8,128)} %get-tuple-element.30.own), channel_id=1, source_target_pairs={{0,240},{16,0},{32,16},{48,32},{64,48},{80,64},{96,80},{112,96},{1... | collective-permute-start | bytes 1609736 | tf_op jit(solution)/shard_map/ppermute | solution.py:365
  8.6 14.9 %all-to-all-start = ((f32[128,1,128]{2,1,0:T(1,128)}), f32[128,1,128]{2,1,0:T(1,128)S(1)}, u32[]{:S(2)}, u32[]{:S(2)}) async-start(f32[128,1,128]{2,1,0:T(1,128)} %bitcast.42), calls=%async_computation | async-start | bytes 131072 | tf_op jit(solution)/shard_map/all_to_all | solution.py:425
  23.5 2.2 %collective-permute-start.2 = (f32[216,128]{1,0:T(8,128)}, f32[216,128]{1,0:T(8,128)S(1)}, u32[]{:S(2)}, u32[]{:S(2)}) collective-permute-start(f32[216,128]{1,0:T(8,128)} %get-tuple-element.31), channel_id=1, source_target_pairs={{0,32},{16,48},{32,64},{48,80},{64,96},{80,112},{96,128},{112,144}... | collective-permute-start | bytes 331784 | tf_op jit(solution)/shard_map/ppermute | solution.py:365
  25.6 3.0 %collective-permute-start.3 = (f32[216,128]{1,0:T(8,128)}, f32[216,128]{1,0:T(8,128)S(1)}, u32[]{:S(2)}, u32[]{:S(2)}) collective-permute-start(f32[216,128]{1,0:T(8,128)} %get-tuple-element.32), channel_id=1, source_target_pairs={{0,224},{16,240},{32,0},{48,16},{64,32},{80,48},{96,64},{112,80},{... | collective-permute-start | bytes 331784 | tf_op jit(solution)/shard_map/ppermute | solution.py:365
  28.7 1.0 copy-done.1
  31.4 3.8 %collective-permute-done.3.p2 = f32[216,128]{1,0:T(8,128)S(1)} collective-permute-done((f32[216,128]{1,0:T(8,128)}, f32[216,128]{1,0:T(8,128)S(1)}, u32[]{:S(2)}, u32[]{:S(2)}) %collective-permute-start.3) | collective-permute-done | bytes 110624 | tf_op jit(solution)/shard_map/ppermute | solution.py:365
  35.2 0.9 collective-permute-start.5
  36.7 1.9 %collective-permute-done.7.m2_o = f32[216,128]{1,0:T(8,128)S(1)} collective-permute-done((f32[216,128]{1,0:T(8,128)S(1)}, f32[216,128]{1,0:T(8,128)S(1)}, u32[]{:S(2)}, u32[]{:S(2)}) %collective-permute-start.7) | collective-permute-done | bytes 110624 | tf_op jit(solution)/shard_map/ppermute | solution.py:360
  38.8 1.3 %shard_map.66 = (f32[28,112,128]{2,1,0:T(8,128)S(1)}, f32[28,112,128]{2,1,0:T(8,128)S(1)}, f32[120,128]{1,0:T(8,128)S(1)}, f32[336,128]{1,0:T(8,128)S(1)}, f32[336,128]{1,0:T(8,128)S(1)}) custom-call(s32[2]{0:T(128)S(1)} %pad_add_fusion.pos, f32[1048,128]{1,0:T(8,128)S(1)} %shard_map.65.own, f32[1048,128]{1,0:T(8,128)S(1)} %collective-permute-done.m1, ...), custom_call_target="tpu_custom_call" | custom-call | tf_op jit(solution)/shard_map/pallas_call | solution.py:397
  40.1 0.9 collective-permute-start.9
  41.0 1.5 %shard_map.67 = (f32[2,512,128]{2,1,0:T(8,128)S(1)}, f32[2,512,128]{2,1,0:T(8,128)S(1)}) custom-call(s32[2]{0:T(128)S(1)} %pad_add_fusion.pos, s32[16,128]{1,0:T(8,128)S(1)} %bitcast.41, f32[128,128]{1,0:T(8,128)S(1)} %bitcast.32), custom_call_target="tpu_custom_call" | custom-call | tf_op jit(solution)/shard_map/pallas_call | solution.py:397
  42.4 0.9 collective-permute-done.9.lz
  43.3 2.8 %collective-permute-done.10.rz = f32[336,128]{1,0:T(8,128)S(1)} collective-permute-done((f32[336,128]{1,0:T(8,128)S(1)}, f32[336,128]{1,0:T(8,128)S(1)}, u32[]{:S(2)}, u32[]{:S(2)}) %collective-permute-start.10) | collective-permute-done | bytes 172064 | tf_op jit(solution)/shard_map/ppermute | solution.py:365
  46.1 4.9 %shard_map.68 = (f32[28,112,128]{2,1,0:T(8,128)S(1)}, f32[28,112,128]{2,1,0:T(8,128)S(1)}, f32[128,128]{1,0:T(8,128)S(1)}, f32[40,128]{1,0:T(8,128)S(1)}, f32[40,128]{1,0:T(8,128)S(1)}) custom-call(s32[2]{0:T(128)S(1)} %pad_add_fusion.pos, f32[28,112,128]{2,1,0:T(8,128)S(1)} %get-tuple-element.39.fr, ...), custom_call_target="tpu_custom_call", output_to_operand_aliasing={{0}: (1, {}), {1}: (2, {})} | custom-call | tf_op jit(solution)/shard_map/pallas_call | solution.py:397
  52.4 12.5 %all_to_all.32.refs_0_ = f32[16,40,128]{2,1,0:T(8,128)S(1)} all-to-all(f32[16,40,128]{2,1,0:T(8,128)S(1)} %shard_map.69), channel_id=1, replica_groups=mesh['lat_0'=4,'lat_1'=4,'lon'=8,'ens'=2] {'lat_0','lat_1'}, dimensions={0} | all-to-all | bytes 655360 | tf_op jit(solution)/shard_map/all_to_all | solution.py:391
  65.0 14.9 %all_to_all.33.refs_0_ = f32[8,40,128]{2,1,0:T(8,128)S(1)} all-to-all(f32[8,40,128]{2,1,0:T(8,128)S(1)} %shard_map.70), channel_id=1, replica_groups=mesh['lat_0'=4,'lat_1'=4,'lon'=8,'ens'=2] {'lon'}, dimensions={0} | all-to-all | bytes 327680 | tf_op jit(solution)/shard_map/all_to_all | solution.py:391
  79.8 3.6 %collective-permute-start.12 = (f32[40,128]{1,0:T(8,128)S(1)}, f32[40,128]{1,0:T(8,128)S(1)}, u32[]{:S(2)}, u32[]{:S(2)}) collective-permute-start(f32[40,128]{1,0:T(8,128)S(1)} %bitcast.33), channel_id=1, source_target_pairs={{0,1},{1,0},{2,3},{3,2},{4,5},{5,4},{6,7},{7,6},{8,9},{9,8},{10,11... | collective-permute-start | bytes 61448 | tf_op jit(solution)/shard_map/ppermute | solution.py:360
  84.3 10.0 %shard_map.72 = (f32[128,128]{1,0:T(8,128)S(1)}, f32[40,128]{1,0:T(8,128)S(1)}, f32[40,128]{1,0:T(8,128)S(1)}) custom-call(s32[2]{0:T(128)S(1)} %pad_add_fusion.pos, f32[40,128]{1,0:T(8,128)S(1)} %bitcast.34, f32[40,128]{1,0:T(8,128)S(1)} %collective-permute-done.12.other, f32[28,112,128]{2,1,0:T(8,128)S(1)} %get-tuple-element.49.fr, ...), custom_call_target="tpu_custom_call" | custom-call | tf_op jit(solution)/shard_map/pallas_call | solution.py:397
  95.6 11.2 %all_to_all.34.refs_0_ = f32[16,40,128]{2,1,0:T(8,128)S(1)} all-to-all(f32[16,40,128]{2,1,0:T(8,128)S(1)} %shard_map.73), channel_id=1, replica_groups=mesh['lat_0'=4,'lat_1'=4,'lon'=8,'ens'=2] {'lat_0','lat_1'}, dimensions={0} | all-to-all | bytes 655360 | tf_op jit(solution)/shard_map/all_to_all | solution.py:391
  106.8 10.8 %all_to_all.35.refs_0_ = f32[8,40,128]{2,1,0:T(8,128)S(1)} all-to-all(f32[8,40,128]{2,1,0:T(8,128)S(1)} %shard_map.74), channel_id=1, replica_groups=mesh['lat_0'=4,'lat_1'=4,'lon'=8,'ens'=2] {'lon'}, dimensions={0} | all-to-all | bytes 327680 | tf_op jit(solution)/shard_map/all_to_all | solution.py:391
  117.6 3.6 %collective-permute-start.14 = (f32[40,128]{1,0:T(8,128)S(1)}, f32[40,128]{1,0:T(8,128)S(1)}, u32[]{:S(2)}, u32[]{:S(2)}) collective-permute-start(f32[40,128]{1,0:T(8,128)S(1)} %bitcast.35), channel_id=1, source_target_pairs={{0,1},{1,0},{2,3},{3,2},{4,5},{5,4},{6,7},{7,6},{8,9},{9,8},{10,11... | collective-permute-start | bytes 61448 | tf_op jit(solution)/shard_map/ppermute | solution.py:360
  122.0 6.2 %shard_map.76 = f32[1024,128]{1,0:T(8,128)} custom-call(s32[2]{0:T(128)S(1)} %pad_add_fusion.pos, f32[40,128]{1,0:T(8,128)S(1)} %bitcast.36, f32[40,128]{1,0:T(8,128)S(1)} %collective-permute-done.14.other, f32[128,128]{1,0:T(8,128)S(1)} %get-tuple-element.54.k1, f32[1024,128]{1,0:T(8,128)S(1)} %bitcast.31, f32[1048,128]{1,0:T(8,128)S(1)} %collective-permute-done.4.own_o.other_p), custom_call_target="tpu_custom_call" | custom-call | tf_op jit(solution)/shard_map/pallas_call | solution.py:397
  (32 shorter events, 6.9 us)
Async XLA Ops:
  2.0 26.7 %collective-permute-start.4 = (f32[1048,128]{1,0:T(8,128)}, f32[1048,128]{1,0:T(8,128)S(1)}, u32[]{:S(2)}, u32[]{:S(2)}) collective-permute-start(f32[1048,128]{1,0:T(8,128)} %get-tuple-element.30.own), channel_id=1, source_target_pairs={{0,1},{1,0},{2,3},{3,2},{4,5},{5,4},{6,7},{7,6},{8,9},{9,8},{10,11... | collective-permute-start | bytes 1609736 | tf_op jit(solution)/shard_map/ppermute | solution.py:360
  5.3 29.8 %collective-permute-start.1 = (f32[1048,128]{1,0:T(8,128)}, f32[1048,128]{1,0:T(8,128)S(1)}, u32[]{:S(2)}, u32[]{:S(2)}) collective-permute-start(f32[1048,128]{1,0:T(8,128)} %get-tuple-element.30.own), channel_id=1, source_target_pairs={{0,240},{16,0},{32,16},{48,32},{64,48},{80,64},{96,80},{112,96},{1... | collective-permute-start | bytes 1609736 | tf_op jit(solution)/shard_map/ppermute | solution.py:365
  8.6 26.6 %collective-permute-start = (f32[1048,128]{1,0:T(8,128)}, f32[1048,128]{1,0:T(8,128)S(1)}, u32[]{:S(2)}, u32[]{:S(2)}) collective-permute-start(f32[1048,128]{1,0:T(8,128)} %get-tuple-element.30.own), channel_id=1, source_target_pairs={{0,16},{16,32},{32,48},{48,64},{64,80},{80,96},{96,112},{112,128},... | collective-permute-start | bytes 1609736 | tf_op jit(solution)/shard_map/ppermute | solution.py:365
  8.6 26.6 %all-to-all-start = ((f32[128,1,128]{2,1,0:T(1,128)}), f32[128,1,128]{2,1,0:T(1,128)S(1)}, u32[]{:S(2)}, u32[]{:S(2)}) async-start(f32[128,1,128]{2,1,0:T(1,128)} %bitcast.42), calls=%async_computation | async-start | bytes 131072 | tf_op jit(solution)/shard_map/all_to_all | solution.py:425
  23.5 7.9 %collective-permute-start.2 = (f32[216,128]{1,0:T(8,128)}, f32[216,128]{1,0:T(8,128)S(1)}, u32[]{:S(2)}, u32[]{:S(2)}) collective-permute-start(f32[216,128]{1,0:T(8,128)} %get-tuple-element.31), channel_id=1, source_target_pairs={{0,32},{16,48},{32,64},{48,80},{64,96},{80,112},{96,128},{112,144}... | collective-permute-start | bytes 331784 | tf_op jit(solution)/shard_map/ppermute | solution.py:365
  25.6 9.5 %collective-permute-start.3 = (f32[216,128]{1,0:T(8,128)}, f32[216,128]{1,0:T(8,128)S(1)}, u32[]{:S(2)}, u32[]{:S(2)}) collective-permute-start(f32[216,128]{1,0:T(8,128)} %get-tuple-element.32), channel_id=1, source_target_pairs={{0,224},{16,240},{32,0},{48,16},{64,32},{80,48},{96,64},{112,80},{... | collective-permute-start | bytes 331784 | tf_op jit(solution)/shard_map/ppermute | solution.py:365
  28.7 1.0 copy-start.1
  30.6 10.3 %copy-start.2 = (s32[2,1,128,8]{2,3,1,0:T(8,128)S(1)}, s32[2,1,128,8]{2,3,1,0:T(8,128)}, u32[]{:S(2)}) copy-start(s32[2,1,128,8]{2,3,1,0:T(8,128)} %param.9) | copy-start | bytes 24580
  35.2 3.6 %collective-permute-start.5 = (f32[1048,128]{1,0:T(8,128)S(1)}, f32[1048,128]{1,0:T(8,128)S(1)}, u32[]{:S(2)}, u32[]{:S(2)}) collective-permute-start(f32[1048,128]{1,0:T(8,128)S(1)} %collective-permute-done.m1), channel_id=1, source_target_pairs={{0,1},{1,0},{2,3},{3,2},{4,5},{5,4},{6,7},{7,6},{8,9},{9,8},{10,11... | collective-permute-start | bytes 1609736 | tf_op jit(solution)/shard_map/ppermute | solution.py:360
  36.1 2.6 %collective-permute-start.6 = (f32[1048,128]{1,0:T(8,128)S(1)}, f32[1048,128]{1,0:T(8,128)S(1)}, u32[]{:S(2)}, u32[]{:S(2)}) collective-permute-start(f32[1048,128]{1,0:T(8,128)S(1)} %collective-permute-done.1.p1), channel_id=1, source_target_pairs={{0,1},{1,0},{2,3},{3,2},{4,5},{5,4},{6,7},{7,6},{8,9},{9,8},{10,11... | collective-permute-start | bytes 1609736 | tf_op jit(solution)/shard_map/ppermute | solution.py:360
  36.2 2.4 %collective-permute-start.7 = (f32[216,128]{1,0:T(8,128)S(1)}, f32[216,128]{1,0:T(8,128)S(1)}, u32[]{:S(2)}, u32[]{:S(2)}) collective-permute-start(f32[216,128]{1,0:T(8,128)S(1)} %collective-permute-done.2.m2), channel_id=1, source_target_pairs={{0,1},{1,0},{2,3},{3,2},{4,5},{5,4},{6,7},{7,6},{8,9},{9,8},{10,11... | collective-permute-start | bytes 331784 | tf_op jit(solution)/shard_map/ppermute | solution.py:360
  36.6 2.1 %collective-permute-start.8 = (f32[216,128]{1,0:T(8,128)S(1)}, f32[216,128]{1,0:T(8,128)S(1)}, u32[]{:S(2)}, u32[]{:S(2)}) collective-permute-start(f32[216,128]{1,0:T(8,128)S(1)} %collective-permute-done.3.p2), channel_id=1, source_target_pairs={{0,1},{1,0},{2,3},{3,2},{4,5},{5,4},{6,7},{7,6},{8,9},{9,8},{10,11... | collective-permute-start | bytes 331784 | tf_op jit(solution)/shard_map/ppermute | solution.py:360
  40.1 3.3 %collective-permute-start.9 = (f32[336,128]{1,0:T(8,128)S(1)}, f32[336,128]{1,0:T(8,128)S(1)}, u32[]{:S(2)}, u32[]{:S(2)}) collective-permute-start(f32[336,128]{1,0:T(8,128)S(1)} %get-tuple-element.42), channel_id=1, source_target_pairs={{0,1},{1,2},{2,3},{3,4},{4,5},{5,6},{6,7},{7,8},{8,9},{9,10},{10,1... | collective-permute-start | bytes 516104 | tf_op jit(solution)/shard_map/ppermute | solution.py:365
  41.0 5.1 %collective-permute-start.10 = (f32[336,128]{1,0:T(8,128)S(1)}, f32[336,128]{1,0:T(8,128)S(1)}, u32[]{:S(2)}, u32[]{:S(2)}) collective-permute-start(f32[336,128]{1,0:T(8,128)S(1)} %get-tuple-element.43), channel_id=1, source_target_pairs={{0,15},{1,0},{2,1},{3,2},{4,3},{5,4},{6,5},{7,6},{8,7},{9,8},{10,9... | collective-permute-start | bytes 516104 | tf_op jit(solution)/shard_map/ppermute | solution.py:365
  51.0 1.3 %collective-permute-start.11 = (f32[40,128]{1,0:T(8,128)S(1)}, f32[40,128]{1,0:T(8,128)S(1)}, u32[]{:S(2)}, u32[]{:S(2)}) collective-permute-start(f32[40,128]{1,0:T(8,128)S(1)} %get-tuple-element.48), channel_id=1, source_target_pairs={{0,1},{1,0},{2,3},{3,2},{4,5},{5,4},{6,7},{7,6},{8,9},{9,8},{10,11... | collective-permute-start | bytes 61448 | tf_op jit(solution)/shard_map/ppermute | solution.py:360
  79.8 4.4 %collective-permute-start.12 = (f32[40,128]{1,0:T(8,128)S(1)}, f32[40,128]{1,0:T(8,128)S(1)}, u32[]{:S(2)}, u32[]{:S(2)}) collective-permute-start(f32[40,128]{1,0:T(8,128)S(1)} %bitcast.33), channel_id=1, source_target_pairs={{0,1},{1,0},{2,3},{3,2},{4,5},{5,4},{6,7},{7,6},{8,9},{9,8},{10,11... | collective-permute-start | bytes 61448 | tf_op jit(solution)/shard_map/ppermute | solution.py:360
  94.3 27.7 %copy-start = (f32[2,64,8,128]{3,2,1,0:T(8,128)S(1)}, f32[2,64,8,128]{3,2,1,0:T(8,128)}, u32[]{:S(2)}) copy-start(f32[2,64,8,128]{3,2,1,0:T(8,128)} %param.6) | copy-start | bytes 1572868
  94.3 1.3 collective-permute-start.13
  117.6 4.4 %collective-permute-start.14 = (f32[40,128]{1,0:T(8,128)S(1)}, f32[40,128]{1,0:T(8,128)S(1)}, u32[]{:S(2)}, u32[]{:S(2)}) collective-permute-start(f32[40,128]{1,0:T(8,128)S(1)} %bitcast.35), channel_id=1, source_target_pairs={{0,1},{1,0},{2,3},{3,2},{4,5},{5,4},{6,7},{7,6},{8,9},{9,8},{10,11... | collective-permute-start | bytes 61448 | tf_op jit(solution)/shard_map/ppermute | solution.py:360
